TPU v7x, 32 devices: a whole 2x2x4 slice. The times are simulated.
32 devices in a mesh: seq: 16 (over z, x, core), shard: 2 (over y).
Axes of the slice: x: 2, y: 2, z: 4, core: 2. Of those that a mesh axis runs over, the one named last changes fastest.
Arguments:
- x_embed: bfloat16 [2, 8192, 768], P('shard', 'seq'), may hold values from -9 to 9
- doc_ids: int32 [2, 8192], P('shard', 'seq'), may hold values from 0 to 3, never falling along the last dimension, each value on 1 to 4096 neighbouring positions
- owners: int32 [2, 8192, 2], P('shard', 'seq'), may hold values from 0 to 31, all different within a row; in each aligned block of 512 rows (0 to 511, 512 to 1023, ..., all dimensions but the last counted through in order) at most 64 rows name the same one
- row_ids: int32 [2, 8192, 2], P('shard', 'seq'), may hold values from 0 to 24999
- table: bfloat16 [800000, 192], P(('seq', 'shard')), may hold values from -6 to 6
- ngram_weight: bfloat16 [384, 768], P('shard'), may hold values from -0.3125 to 0.3125
- stream_gain: bfloat16 [768], P('shard'), may hold values from 0.5 to 1.5
- query_weight: bfloat16 [768, 768], P('shard'), may hold values from -0.21875 to 0.21875
- key_weight: bfloat16 [768, 768], P('shard'), may hold values from -0.21875 to 0.21875
- value_weight: bfloat16 [768, 768], P('shard'), may hold values from -0.21875 to 0.21875
- out_weight: bfloat16 [768, 768], P('shard'), may hold values from -1.75 to 1.75
- mixer_gain: bfloat16 [768], P('shard'), may hold values from 0.5 to 1.5
- gate_weight: bfloat16 [768, 2048], P('shard'), may hold values from -0.21875 to 0.21875
- up_weight: bfloat16 [768, 2048], P('shard'), may hold values from -0.21875 to 0.21875
- down_weight: bfloat16 [2048, 768], P('shard'), may hold values from -0.25 to 0.25
- feed_gain: bfloat16 [768], P('shard'), may hold values from 0.5 to 1.5
- cotangent: bfloat16 [2, 8192, 768], P('shard', 'seq'), may hold values from -6 to 6
Outputs:
- mixed: bfloat16 [2, 8192, 768], P('shard', 'seq')
- grad_input: float32 [2, 8192, 768], P('shard', 'seq')
- stream_rms: float32 [], replicated
- mixer_rms: float32 [], replicated
- feed_rms: float32 [], replicated
- grad_table: float32 [800000, 192], P(('seq', 'shard'))
- grad_ngram: float32 [384, 768], P('shard')
- grad_stream_gain: float32 [768], P('shard')
- grad_query: float32 [768, 768], P('shard')
- grad_key: float32 [768, 768], P('shard')
- grad_value: float32 [768, 768], P('shard')
- grad_out: float32 [768, 768], P('shard')
- grad_mixer_gain: float32 [768], P('shard')
- grad_gate: float32 [768, 2048], P('shard')
- grad_up: float32 [768, 2048], P('shard')
- grad_down: float32 [2048, 768], P('shard')
- grad_feed_gain: float32 [768], P('shard')
Inputs may be any that keep to these rules, and one draw needn't show every extreme that they name: `owners`: the two shards named by one token differ; among the ids of one device's tokens no shard is named more than 64 times. `doc_ids`: along a sequence the document numbers never fall; each document covers 1 to 4096 tokens, and one covers exactly 4096.
All inputs are finite; a program needn't handle non-finite values.
Results may differ from a plain program's by a relative error of at most 0.019.
Values may be sent and summed in bfloat16 or wider, within the bound.
A program may use at most 192 MiB of HBM per device.

v0:
```python
import jax
import jax.numpy as jnp
from jax import lax
from jax.sharding import PartitionSpec as P

HEADS = 12
HEAD_DIM = 64
DOC_MAX = 4096


EPSILON = 1e-06
ROPE_BASE = 500000.0
MASKED_SCORE = -1e30


def as_sent(array):
    return jax.tree.map(lambda a: a.astype(jnp.bfloat16) if a.dtype == jnp.float32 else a, array)


def passed_along(block, axis, distance):
    devices = range(lax.axis_size(axis))
    route = [(i - distance, i) for i in devices if i - distance in devices]
    return lax.ppermute(block, axis, route)


def passed_along_2(block, axis, distance):
    devices = range(lax.axis_size(axis))
    route = [((i - distance) % len(devices), i) for i in devices]
    return lax.ppermute(block, axis, route)


def norm_parts(field, gain_row):
    inverse = lax.rsqrt(jnp.mean(field * field, axis=-1, keepdims=True) + EPSILON)
    unit_rows = field * inverse
    return (unit_rows * gain_row, unit_rows, inverse)


def norm_back(gradient, unit_rows, inverse, gain_row):
    scaled = gradient * gain_row
    back_rows = inverse * (
        scaled - unit_rows * jnp.mean(scaled * unit_rows, axis=-1, keepdims=True)
    )
    return (back_rows, jnp.sum(gradient * unit_rows, axis=0))


def rotary(field, places, direction):
    half_dim = HEAD_DIM // 2
    frequency = ROPE_BASE ** (-2.0 * jnp.arange(half_dim, dtype=jnp.float32) / HEAD_DIM)
    angles = places.astype(jnp.float32)[:, None] * frequency[None, :]
    cosine = jnp.cos(angles)[:, None, :]
    sine_part = direction * jnp.sin(angles)[:, None, :]
    first_half = field[..., :half_dim]
    second_half = field[..., half_dim:]
    return jnp.concatenate(
        [
            first_half * cosine - second_half * sine_part,
            second_half * cosine + first_half * sine_part,
        ],
        axis=-1,
    )


def split_heads(matrix):
    return matrix.reshape(matrix.shape[0], HEADS, HEAD_DIM)


def shards(
    x_embed,
    doc_ids,
    owners,
    row_ids,
    table,
    ngram_weight,
    stream_gain,
    query_weight,
    key_weight,
    value_weight,
    out_weight,
    mixer_gain,
    gate_weight,
    up_weight,
    down_weight,
    feed_gain,
    cotangent,
):
    tokens = x_embed.shape[1]
    seq_count = lax.axis_size("seq")
    shard_count = lax.axis_size("shard")
    owner_count = seq_count * shard_count
    capacity = max(2, 4 * tokens // owner_count)
    score_scale = HEAD_DIM ** (-0.5)
    gathered = (
        lax.all_gather(ngram_weight, "shard", axis=0, tiled=True),
        lax.all_gather(stream_gain, "shard", axis=0, tiled=True),
        lax.all_gather(query_weight, "shard", axis=0, tiled=True),
        lax.all_gather(key_weight, "shard", axis=0, tiled=True),
        lax.all_gather(value_weight, "shard", axis=0, tiled=True),
        lax.all_gather(out_weight, "shard", axis=0, tiled=True),
        lax.all_gather(mixer_gain, "shard", axis=0, tiled=True),
        lax.all_gather(gate_weight, "shard", axis=0, tiled=True),
        lax.all_gather(up_weight, "shard", axis=0, tiled=True),
        lax.all_gather(down_weight, "shard", axis=0, tiled=True),
        lax.all_gather(feed_gain, "shard", axis=0, tiled=True),
    )
    (
        full_ngram,
        full_stream_gain,
        full_query,
        full_key,
        full_value,
        full_out,
        full_mixer_gain,
        full_gate,
        full_up,
        full_down,
        full_feed_gain,
    ) = gathered
    gain_stream = full_stream_gain.astype(jnp.float32)
    gain_mixer = full_mixer_gain.astype(jnp.float32)
    gain_feed = full_feed_gain.astype(jnp.float32)
    flat_owner = owners.reshape(-1)
    flat_row = row_ids.reshape(-1)
    request_count = flat_owner.shape[0]
    one_hot = (flat_owner[:, None] == jnp.arange(owner_count, dtype=jnp.int32)[None, :]).astype(
        jnp.bfloat16
    )
    earlier = (jnp.arange(request_count)[:, None] > jnp.arange(request_count)[None, :]).astype(
        jnp.bfloat16
    )
    before = jnp.dot(earlier, one_hot, preferred_element_type=jnp.float32)
    rank_index = jnp.sum(before * one_hot, axis=1).astype(jnp.int32)
    slot_index = flat_owner * capacity + rank_index
    request = jnp.full((owner_count * capacity,), -1, jnp.int32).at[slot_index].set(flat_row)
    asked_rows = lax.all_to_all(
        lax.all_to_all(
            request.reshape(seq_count, shard_count, capacity),
            "seq",
            split_axis=0,
            concat_axis=0,
            tiled=True,
        ),
        "shard",
        split_axis=1,
        concat_axis=1,
        tiled=True,
    )
    present = asked_rows >= 0
    found_rows = jnp.take(table, jnp.maximum(asked_rows, 0).reshape(-1), axis=0)
    found_rows = jnp.where(present.reshape(-1)[:, None], found_rows, jnp.zeros_like(found_rows))
    answer = lax.all_to_all(
        lax.all_to_all(
            found_rows.reshape(seq_count, shard_count, capacity, -1),
            "seq",
            split_axis=0,
            concat_axis=0,
            tiled=True,
        ),
        "shard",
        split_axis=1,
        concat_axis=1,
        tiled=True,
    )
    picked = jnp.take(answer.reshape(owner_count * capacity, -1), slot_index, axis=0).reshape(
        tokens, -1
    )
    inputs = x_embed[0].astype(jnp.float32)
    embedded = jnp.dot(picked, full_ngram, preferred_element_type=jnp.float32)
    stream = inputs + embedded
    residual, unit_zero, inverse_zero = norm_parts(stream, gain_stream)
    normed_one, unit_one, inverse_one = norm_parts(residual, gain_mixer)
    mixer_in = normed_one.astype(jnp.bfloat16)
    query_rows = jnp.dot(mixer_in, full_query, preferred_element_type=jnp.float32)
    key_rows = jnp.dot(mixer_in, full_key, preferred_element_type=jnp.float32)
    value_rows = jnp.dot(mixer_in, full_value, preferred_element_type=jnp.float32)
    my_index = lax.axis_index("seq")
    places = my_index * tokens + jnp.arange(tokens, dtype=jnp.int32)
    query_rot = rotary(split_heads(query_rows), places, 1.0).astype(jnp.bfloat16)
    key_rot = rotary(split_heads(key_rows), places, 1.0).astype(jnp.bfloat16).reshape(tokens, -1)
    value_low = value_rows.astype(jnp.bfloat16)
    own_docs = doc_ids[0]
    own_block = (key_rot, value_low, own_docs.astype(jnp.bfloat16))
    query_docs = own_docs.astype(jnp.float32)

    def block_scores(key_block, source):
        key_heads = split_heads(key_block[0])
        raw_scores = jnp.einsum(
            "qhd,khd->hqk", query_rot, key_heads, preferred_element_type=jnp.float32
        )
        key_places = source * tokens + jnp.arange(tokens, dtype=jnp.int32)
        allowed = (
            (places[:, None] >= key_places[None, :])
            & (query_docs[:, None] == key_block[2].astype(jnp.float32)[None, :])
            & (source >= 0)
        )
        return jnp.where(allowed[None], raw_scores * score_scale, MASKED_SCORE)

    def absorb(running, key_block, source):
        row_max, row_sum = running
        scores = block_scores(key_block, source)
        new_max = jnp.maximum(row_max, jnp.max(scores, axis=-1, keepdims=True))
        row_sum = row_sum * jnp.exp(row_max - new_max) + jnp.sum(
            jnp.exp(scores - new_max), axis=-1, keepdims=True
        )
        return (new_max, row_sum)

    start_running = (
        jnp.full((HEADS, tokens, 1), MASKED_SCORE, jnp.float32),
        jnp.zeros((HEADS, tokens, 1), jnp.float32),
    )
    running = absorb(start_running, own_block, my_index)
    doc_span = min(DOC_MAX, tokens * seq_count)
    reach_count = min((doc_span + tokens - 2) // tokens, seq_count - 1)
    steps_back = jnp.arange(1, reach_count + 1, dtype=jnp.int32)

    def fetch_step(carried_in, step_back):
        key_block, running_now = carried_in
        key_block = jax.tree.map(
            lambda part, own: part.astype(own.dtype),
            passed_along(as_sent(key_block), "seq", 1),
            key_block,
        )
        return ((key_block, absorb(running_now, key_block, my_index - step_back)), key_block)

    (unused_block, running), kept_blocks = lax.scan(fetch_step, (own_block, running), steps_back)
    log_sum = running[0] + jnp.log(running[1])

    def emit_block(partial_value, key_block, source):
        low_sum, full_sum = partial_value
        probability = jnp.exp(block_scores(key_block, source) - log_sum)
        value_heads = split_heads(key_block[1])
        prob_low = probability.astype(jnp.bfloat16)
        prob_rest = (probability - prob_low.astype(jnp.float32)).astype(jnp.bfloat16)
        main_part = jnp.einsum(
            "hqk,khd->qhd", prob_low, value_heads, preferred_element_type=jnp.float32
        )
        rest_part = jnp.einsum(
            "hqk,khd->qhd", prob_rest, value_heads, preferred_element_type=jnp.float32
        )
        return (low_sum + main_part, full_sum + (main_part + rest_part))

    zero_heads = jnp.zeros((tokens, HEADS, HEAD_DIM), jnp.float32)
    partial_value = emit_block((zero_heads, zero_heads), own_block, my_index)

    def emit_step(partial_now, scan_item):
        step_back, key_block = scan_item
        return (emit_block(partial_now, key_block, my_index - step_back), None)

    (mixed_low, mixed_full), unused = lax.scan(emit_step, partial_value, (steps_back, kept_blocks))
    heads_low = mixed_low.reshape(tokens, -1).astype(jnp.bfloat16)
    mixer_out = jnp.dot(heads_low, full_out, preferred_element_type=jnp.float32)
    middle = residual + mixer_out
    normed_two, unit_two, inverse_two = norm_parts(middle, gain_feed)
    feed_in = normed_two.astype(jnp.bfloat16)
    gate_rows = jnp.dot(feed_in, full_gate, preferred_element_type=jnp.float32)
    up_rows = jnp.dot(feed_in, full_up, preferred_element_type=jnp.float32)
    sigmoid = jax.nn.sigmoid(gate_rows)
    hidden = (gate_rows * sigmoid * up_rows).astype(jnp.bfloat16)
    feed_out = jnp.dot(hidden, full_down, preferred_element_type=jnp.float32)
    result = middle + feed_out
    mixed = result.astype(jnp.bfloat16)[None]
    energies = lax.psum(
        (jnp.sum(stream * stream), jnp.sum(mixer_out * mixer_out), jnp.sum(feed_out * feed_out)),
        ("seq", "shard"),
    )
    entry_count = owner_count * tokens * stream.shape[1]
    stream_rms = jnp.sqrt(energies[0] / entry_count)
    mixer_rms = jnp.sqrt(energies[1] / entry_count)
    feed_rms = jnp.sqrt(energies[2] / entry_count)
    grad_result = cotangent[0].astype(jnp.float32)
    grad_feed = cotangent[0]
    grad_down = jnp.einsum("tf,td->fd", hidden, grad_feed, preferred_element_type=jnp.float32)
    grad_hidden = jnp.einsum("td,fd->tf", grad_feed, full_down, preferred_element_type=jnp.float32)
    grad_gate_rows = (grad_hidden * up_rows * sigmoid * (1.0 + gate_rows * (1.0 - sigmoid))).astype(
        jnp.bfloat16
    )
    grad_up_rows = (grad_hidden * gate_rows * sigmoid).astype(jnp.bfloat16)
    grad_gate = jnp.einsum("td,tf->df", feed_in, grad_gate_rows, preferred_element_type=jnp.float32)
    grad_up = jnp.einsum("td,tf->df", feed_in, grad_up_rows, preferred_element_type=jnp.float32)
    grad_feed_in = jnp.einsum(
        "tf,df->td", grad_gate_rows, full_gate, preferred_element_type=jnp.float32
    ) + jnp.einsum("tf,df->td", grad_up_rows, full_up, preferred_element_type=jnp.float32)
    back_two, grad_feed_gain = norm_back(grad_feed_in, unit_two, inverse_two, gain_feed)
    grad_middle = grad_result + back_two
    grad_mixer = grad_middle.astype(jnp.bfloat16)
    grad_out = jnp.einsum("te,td->ed", heads_low, grad_mixer, preferred_element_type=jnp.float32)
    grad_heads = split_heads(
        jnp.einsum("td,ed->te", grad_mixer, full_out, preferred_element_type=jnp.float32).astype(
            jnp.bfloat16
        )
    )
    delta_rows = jnp.sum(grad_heads.astype(jnp.float32) * mixed_full, axis=-1)
    row_delta = jnp.transpose(delta_rows)[:, :, None]

    def block_grads(key_block, source):
        probability = jnp.exp(block_scores(key_block, source) - log_sum)
        key_heads = split_heads(key_block[0])
        value_heads = split_heads(key_block[1])
        grad_prob = jnp.einsum(
            "qhd,khd->hqk", grad_heads, value_heads, preferred_element_type=jnp.float32
        )
        grad_score = (probability * (grad_prob - row_delta)).astype(jnp.bfloat16)
        part_query = (
            jnp.einsum("hqk,khd->qhd", grad_score, key_heads, preferred_element_type=jnp.float32)
            * score_scale
        )
        part_key = (
            jnp.einsum("hqk,qhd->khd", grad_score, query_rot, preferred_element_type=jnp.float32)
            * score_scale
        )
        part_value = jnp.einsum(
            "hqk,qhd->khd",
            probability.astype(jnp.bfloat16),
            grad_heads,
            preferred_element_type=jnp.float32,
        )
        return (part_query, part_key.reshape(tokens, -1), part_value.reshape(tokens, -1))

    own_query, own_key, own_value = block_grads(own_block, my_index)

    def take_block(previous):
        return jax.tree.map(
            lambda part, own: part.astype(own.dtype),
            passed_along(as_sent(previous), "seq", 1),
            previous,
        )

    def back_step(carried_in, scan_item):
        step_back, kept_item = scan_item
        passing, grad_now, previous = carried_in
        key_block = take_block(previous)
        part_query, part_key, part_value = block_grads(key_block, my_index - step_back)
        grad_now = grad_now + part_query
        passing = jax.tree.map(
            lambda part, own: part.astype(own.dtype),
            passed_along_2(as_sent(passing), "seq", 1),
            passing,
        )
        return (((passing[0] + part_key, passing[1] + part_value), grad_now, key_block), None)

    (passing, grad_query_rot, unused_block), sent_parts = lax.scan(
        back_step, ((own_key, own_value), own_query, own_block), (steps_back, kept_blocks)
    )
    carried = (
        passed_along_2(passing[0].astype(jnp.bfloat16), "seq", -reach_count).astype(jnp.float32),
        passed_along_2(passing[1].astype(jnp.bfloat16), "seq", -reach_count).astype(jnp.float32),
    )
    grad_query_low = rotary(grad_query_rot, places, -1.0).reshape(tokens, -1).astype(jnp.bfloat16)
    grad_key_low = (
        rotary(split_heads(carried[0]), places, -1.0).reshape(tokens, -1).astype(jnp.bfloat16)
    )
    grad_value_low = carried[1].astype(jnp.bfloat16)
    grad_query = jnp.einsum(
        "td,te->de", mixer_in, grad_query_low, preferred_element_type=jnp.float32
    )
    grad_key = jnp.einsum("td,te->de", mixer_in, grad_key_low, preferred_element_type=jnp.float32)
    grad_value = jnp.einsum(
        "td,te->de", mixer_in, grad_value_low, preferred_element_type=jnp.float32
    )
    grad_mixer_in = jnp.einsum(
        "te,de->td", grad_query_low, full_query, preferred_element_type=jnp.float32
    )
    grad_mixer_in = grad_mixer_in + jnp.einsum(
        "te,de->td", grad_key_low, full_key, preferred_element_type=jnp.float32
    )
    grad_mixer_in = grad_mixer_in + jnp.einsum(
        "te,de->td", grad_value_low, full_value, preferred_element_type=jnp.float32
    )
    back_one, grad_mixer_gain = norm_back(grad_mixer_in, unit_one, inverse_one, gain_mixer)
    grad_residual = grad_middle + back_one
    back_zero, grad_stream_gain = norm_back(grad_residual, unit_zero, inverse_zero, gain_stream)
    grad_input = back_zero[None]
    grad_embed = back_zero.astype(jnp.bfloat16)
    grad_ngram = jnp.einsum("ti,to->io", picked, grad_embed, preferred_element_type=jnp.float32)
    grad_picked = (
        jnp.einsum("to,io->ti", grad_embed, full_ngram, preferred_element_type=jnp.float32)
        .astype(jnp.bfloat16)
        .reshape(request_count, -1)
    )
    outgoing = (
        jnp.zeros((owner_count * capacity, grad_picked.shape[1]), jnp.bfloat16)
        .at[slot_index]
        .set(grad_picked)
    )
    incoming = lax.all_to_all(
        lax.all_to_all(
            outgoing.reshape(seq_count, shard_count, capacity, -1),
            "seq",
            split_axis=0,
            concat_axis=0,
            tiled=True,
        ),
        "shard",
        split_axis=1,
        concat_axis=1,
        tiled=True,
    )
    incoming = (
        jnp.where(present[..., None], incoming, jnp.zeros_like(incoming))
        .reshape(owner_count * capacity, -1)
        .astype(jnp.float32)
    )
    grad_table = (
        jnp.zeros(table.shape, jnp.float32).at[jnp.maximum(asked_rows, 0).reshape(-1)].add(incoming)
    )
    shares = (
        lax.psum_scatter(
            grad_ngram.astype(jnp.bfloat16), "shard", scatter_dimension=0, tiled=True
        ).astype(jnp.float32),
        lax.psum_scatter(
            grad_stream_gain.astype(jnp.bfloat16), "shard", scatter_dimension=0, tiled=True
        ).astype(jnp.float32),
        lax.psum_scatter(
            grad_query.astype(jnp.bfloat16), "shard", scatter_dimension=0, tiled=True
        ).astype(jnp.float32),
        lax.psum_scatter(
            grad_key.astype(jnp.bfloat16), "shard", scatter_dimension=0, tiled=True
        ).astype(jnp.float32),
        lax.psum_scatter(
            grad_value.astype(jnp.bfloat16), "shard", scatter_dimension=0, tiled=True
        ).astype(jnp.float32),
        lax.psum_scatter(
            grad_out.astype(jnp.bfloat16), "shard", scatter_dimension=0, tiled=True
        ).astype(jnp.float32),
        lax.psum_scatter(
            grad_mixer_gain.astype(jnp.bfloat16), "shard", scatter_dimension=0, tiled=True
        ).astype(jnp.float32),
        lax.psum_scatter(
            grad_gate.astype(jnp.bfloat16), "shard", scatter_dimension=0, tiled=True
        ).astype(jnp.float32),
        lax.psum_scatter(
            grad_up.astype(jnp.bfloat16), "shard", scatter_dimension=0, tiled=True
        ).astype(jnp.float32),
        lax.psum_scatter(
            grad_down.astype(jnp.bfloat16), "shard", scatter_dimension=0, tiled=True
        ).astype(jnp.float32),
        lax.psum_scatter(
            grad_feed_gain.astype(jnp.bfloat16), "shard", scatter_dimension=0, tiled=True
        ).astype(jnp.float32),
    )
    totals = lax.psum(
        (
            shares[0],
            shares[1],
            shares[2],
            shares[3],
            shares[4],
            shares[5],
            shares[6],
            shares[7],
            shares[8],
            shares[9],
            shares[10],
        ),
        "seq",
    )
    return (
        mixed,
        grad_input,
        stream_rms,
        mixer_rms,
        feed_rms,
        grad_table,
        totals[0],
        totals[1],
        totals[2],
        totals[3],
        totals[4],
        totals[5],
        totals[6],
        totals[7],
        totals[8],
        totals[9],
        totals[10],
    )


def solution(mesh):
    return jax.shard_map(
        shards,
        mesh=mesh,
        in_specs=(
            P("shard", "seq", None),
            P("shard", "seq"),
            P("shard", "seq", None),
            P("shard", "seq", None),
            P(("seq", "shard"), None),
            P("shard", None),
            P("shard"),
            P("shard", None),
            P("shard", None),
            P("shard", None),
            P("shard", None),
            P("shard"),
            P("shard", None),
            P("shard", None),
            P("shard", None),
            P("shard"),
            P("shard", "seq", None),
        ),
        out_specs=(
            P("shard", "seq", None),
            P("shard", "seq", None),
            P(),
            P(),
            P(),
            P(("seq", "shard"), None),
            P("shard", None),
            P("shard"),
            P("shard", None),
            P("shard", None),
            P("shard", None),
            P("shard", None),
            P("shard"),
            P("shard", None),
            P("shard", None),
            P("shard", None),
            P("shard"),
        ),
        check_vma=False,
    )
```

profile of v0, /device:TPU:0, one launch (start us, length us, event | category | flops | bytes accessed | tf_op | source)
XLA Modules:
  0.0 1669.0 jit_solution(12060297811500638718)
XLA Ops:
  17.3 13.6 all_to_all.30
  36.1 14.8 copy.174
  51.9 12.9 gather_fusion
  98.4 27.0 %all_gather.33 = bf16[384,768]{1,0:T(8,128)(2,1)S(1)} all-gather(bf16[192,768]{1,0:T(8,128)(2,1)S(1)} %copy-done.48), channel_id=1, replica_groups=mesh['seq'=16,'shard'=2] {'shard'}, dimensions={0}, use_global_device_ids=true | all-gather | bytes 884736 | tf_op jit(solution)/shard_map/all_gather | solution.py:93
  149.7 237.3 %while.59 = (s32[]{:T(128)}, bf16[512,768]{0,1:T(8,128)(2,1)}, bf16[512,768]{1,0:T(8,128)(2,1)}, bf16[512]{0:T(512)(128)(2,1)S(1)}, f32[12,512,1]{1,0,2:T(8,128)...) while((s32[]{:T(128)}, bf16[512,768]{0,1:T(8,128)(2,1)}, ...), condition=%wide.region_9.10_spmd.clone, body=%wide.region_6.9_spmd.clone.sunk | while | flops 425735680 | bytes 40453468 | solution.py:224
  167.3 14.3 collective-permute-start
  198.0 14.4 collective-permute-start
  228.7 14.4 collective-permute-start
  260.4 13.5 collective-permute-start
  292.0 12.6 collective-permute-start
  323.7 11.7 collective-permute-start
  355.3 10.8 collective-permute-start
  400.1 198.2 %while.60 = (s32[]{:T(128)}, f32[512,12,64]{0,2,1:T(8,128)}, f32[512,12,64]{0,2,1:T(8,128)}, bf16[8,512,768]{2,1,0:T(8,128)(2,1)}, s32[8]{0:T(128)S(1)}, /*index...) while((s32[]{:T(128)}, f32[512,12,64]{0,2,1:T(8,128)}, ...), condition=%wide.region_11.12_spmd.clone, body=%wide.region_10.11_spmd.clone.sunk | while | flops 1244792320 | bytes 131399016 | solution.py:248
  655.8 346.3 %while.61 = (s32[]{:T(128)}, bf16[512,768]{0,1:T(8,128)(2,1)}, bf16[512,768]{0,1:T(8,128)(2,1)}, f32[512,12,64]{0,2,1:T(8,128)S(1)}, bf16[512,768]{0,1:T(8,128)(...) while((s32[]{:T(128)}, bf16[512,768]{0,1:T(8,128)(2,1)}, ...), condition=%wide.region_16.17_spmd.clone, body=%wide.region_15.16_spmd.clone.sunk | while | flops 2049312256 | bytes 94467520 | solution.py:340
  1002.1 12.9 collective-permute-start.8
  1015.1 48.0 %collective-permute-done.8 = bf16[512,768]{0,1:T(8,128)(2,1)S(1)} collective-permute-done((bf16[512,768]{0,1:T(8,128)(2,1)}, bf16[512,768]{0,1:T(8,128)(2,1)S(1)}, u32[]{:S(2)}, u32[]{:S(2)}) %collective-permute-start.8) | collective-permute-done | bytes 786464 | tf_op jit(solution)/shard_map/ppermute | solution.py:29
  1067.4 11.5 collective-permute-done.9
  1121.3 29.1 %all_to_all.31 = bf16[16,2,64,192]{3,2,1,0:T(8,128)(2,1)S(1)} all-to-all(bf16[16,2,64,192]{3,2,1,0:T(8,128)(2,1)S(1)} %bitcast.277), channel_id=1, replica_groups=mesh['seq'=16,'shard'=2] {'seq'}, dimensions={0} | all-to-all | bytes 1572864 | tf_op jit(solution)/shard_map/all_to_all | solution.py:385
  1156.3 57.2 %all-reduce.3 = (f32[]{:T(128)}, f32[]{:T(128)}, f32[]{:T(128)}) all-reduce(f32[]{:T(128)} %get-tuple-element.673, f32[]{:T(128)} %get-tuple-element.796, f32[]{:T(128)} %get-tuple-element.793), channel_id=1, replica_groups=mesh['seq'=16,'shard'=2] {'seq','shard'}, use_global_device_ids=true, to_apply=%region_20.21 | all-reduce | flops 3 | bytes 24 | tf_op jit(solution)/shard_map/psum | solution.py:261
  1222.2 23.5 %scatter_custom_fusion.2 = f32[25000,192]{1,0:T(8,128)} fusion(s32[2048]{0:T(1024)} %bitcast.315, f32[]{:T(128)} %constant.76.clone.1, bf16[2048,192]{1,0:T(8,128)(2,1)S(1)} %bitcast.276), kind=kCustom, calls=%fused_computation.57 | custom fusion | flops 786432 | bytes 19986944 | tf_op jit(solution)/shard_map/scatter-add | solution.py:403
  1245.6 23.6 %copy.193 = f32[25000,192]{0,1:T(8,128)} copy(f32[25000,192]{1,0:T(8,128)} %scatter_custom_fusion.2) | data formatting | bytes 38400000
  1269.3 31.2 %reduce-scatter.21.cloned.1.call-done = bf16[384,2048]{1,0:T(8,128)(2,1)} async-done(((bf16[768,2048]{1,0:T(8,128)(2,1)}), bf16[384,2048]{1,0:T(8,128)(2,1)}) %reduce-scatter.21.cloned.1.call-update) | async-done | bytes 1572880 | tf_op jit(solution)/shard_map/reduce_scatter | solution.py:430
  1300.5 46.1 %reduce-scatter.23.cloned.1.call-done = bf16[1024,768]{1,0:T(8,128)(2,1)} async-done(((bf16[2048,768]{1,0:T(8,128)(2,1)}), bf16[1024,768]{1,0:T(8,128)(2,1)}) %reduce-scatter.23.cloned.1.call-update) | async-done | bytes 1572880 | tf_op jit(solution)/shard_map/reduce_scatter | solution.py:433
  1346.7 312.2 %all-reduce.7 = (f32[192,768]{1,0:T(8,128)}, f32[384]{0:T(512)}, f32[384,768]{1,0:T(8,128)}, f32[384,768]{1,0:T(8,128)}, f32[384,768]{1,0:T(8,128)}, /*index=5*/...) all-reduce(bf16[192,768]{1,0:T(8,128)(2,1)S(1)} %copy-done.49, ...), channel_id=1, replica_groups=mesh['seq'=16,'shard'=2] {'seq'}, use_global_device_ids=true, to_apply=%region_28.29 | all-reduce | flops 3687552 | bytes 22127616 | tf_op jit(solution)/shard_map/psum | solution.py:440
  (899 shorter events, 872.2 us)
Async XLA Ops:
  7.2 126.6 %all-gather.11.cloned.1.call-start = ((), (), s32[]{:S(2)}) async-start(), calls=%async_computation.14 | async-start | bytes 1769472 | tf_op jit(solution)/shard_map/all_gather | solution.py:97
  7.9 129.4 %all-gather.13.cloned.1.call-start = ((), (), s32[]{:S(2)}) async-start(), calls=%async_computation.15 | async-start | bytes 1769472 | tf_op jit(solution)/shard_map/all_gather | solution.py:95
  8.7 131.0 %all-gather.15.cloned.1.call-start = ((), (), s32[]{:S(2)}) async-start(), calls=%async_computation.16 | async-start | bytes 1769472 | tf_op jit(solution)/shard_map/all_gather | solution.py:96
  9.4 590.5 %all-gather.17.cloned.1.call-start = ((), (), s32[]{:S(2)}) async-start(), calls=%async_computation.17 | async-start | bytes 1769472 | tf_op jit(solution)/shard_map/all_gather | solution.py:98
  10.0 594.6 %all-gather.19.cloned.1.call-start = ((), (), s32[]{:S(2)}) async-start(), calls=%async_computation.18 | async-start | bytes 4718592 | tf_op jit(solution)/shard_map/all_gather | solution.py:100
  10.6 599.9 %all-gather.21.cloned.1.call-start = ((), (), s32[]{:S(2)}) async-start(), calls=%async_computation.19 | async-start | bytes 4718592 | tf_op jit(solution)/shard_map/all_gather | solution.py:101
  66.3 26.7 %all-to-all-start.2 = ((bf16[16,2,64,192]{3,2,1,0:T(8,128)(2,1)}), bf16[16,2,64,192]{3,2,1,0:T(8,128)(2,1)S(1)}, u32[]{:S(2)}, u32[]{:S(2)}) async-start(bf16[16,2,64,192]{3,2,1,0:T(8,128)(2,1)} %select_select_fusion), calls=%async_computation.2 | async-start | bytes 2097152 | tf_op jit(solution)/shard_map/all_to_all | solution.py:151
  70.1 546.2 %all-gather.23.cloned.1.call-start = ((), (), s32[]{:S(2)}) async-start(), calls=%async_computation.20 | async-start | bytes 4718592 | tf_op jit(solution)/shard_map/all_gather | solution.py:102
  94.0 31.6 %all-to-all-start.3 = ((bf16[16,2,64,192]{3,2,0,1:T(8,128)(2,1)}), bf16[16,2,64,192]{3,2,0,1:T(8,128)(2,1)S(1)}, u32[]{:S(2)}, u32[]{:S(2)}) async-start(bf16[16,2,64,192]{3,2,0,1:T(8,128)(2,1)} %copy.175), calls=%async_computation.3 | async-start | bytes 2097152 | tf_op jit(solution)/shard_map/all_to_all | solution.py:150
  97.6 1124.1 %reduce-scatter.9.cloned.1.call-start = ((), (), s32[]{:S(2)}) async-start(), calls=%async_computation.21 | async-start | bytes 884736 | tf_op jit(solution)/shard_map/reduce_scatter | solution.py:406
  292.0 23.3 %collective-permute-start = (bf16[512,768]{0,1:T(8,128)(2,1)}, bf16[512,768]{0,1:T(8,128)(2,1)S(1)}, u32[]{:S(2)}, u32[]{:S(2)}) collective-permute-start(bf16[512,768]{0,1:T(8,128)(2,1)} %get-tuple-element.1093), channel_id=1, source_target_pairs={{0,2},{2,4},{4,6},{6,8},{8,10},{10,12},{12,14},{14,16},{16,18},{18... | collective-permute-start | bytes 2359304 | tf_op jit(solution)/shard_map/while/body/eval_jaxpr/ppermute | solution.py:23
  323.7 23.3 %collective-permute-start = (bf16[512,768]{0,1:T(8,128)(2,1)}, bf16[512,768]{0,1:T(8,128)(2,1)S(1)}, u32[]{:S(2)}, u32[]{:S(2)}) collective-permute-start(bf16[512,768]{0,1:T(8,128)(2,1)} %get-tuple-element.1093), channel_id=1, source_target_pairs={{0,2},{2,4},{4,6},{6,8},{8,10},{10,12},{12,14},{14,16},{16,18},{18... | collective-permute-start | bytes 2359304 | tf_op jit(solution)/shard_map/while/body/eval_jaxpr/ppermute | solution.py:23
  355.3 23.3 %collective-permute-start = (bf16[512,768]{0,1:T(8,128)(2,1)}, bf16[512,768]{0,1:T(8,128)(2,1)S(1)}, u32[]{:S(2)}, u32[]{:S(2)}) collective-permute-start(bf16[512,768]{0,1:T(8,128)(2,1)} %get-tuple-element.1093), channel_id=1, source_target_pairs={{0,2},{2,4},{4,6},{6,8},{8,10},{10,12},{12,14},{14,16},{16,18},{18... | collective-permute-start | bytes 2359304 | tf_op jit(solution)/shard_map/while/body/eval_jaxpr/ppermute | solution.py:23
  656.0 26.7 %collective-permute-start.3 = (bf16[512,768]{0,1:T(8,128)(2,1)}, bf16[512,768]{0,1:T(8,128)(2,1)S(1)}, u32[]{:S(2)}, u32[]{:S(2)}) collective-permute-start(bf16[512,768]{0,1:T(8,128)(2,1)} %get-tuple-element.1193), channel_id=1, source_target_pairs={{0,2},{2,4},{4,6},{6,8},{8,10},{10,12},{12,14},{14,16},{16,18},{18... | collective-permute-start | bytes 2359304 | tf_op jit(solution)/shard_map/while/body/eval_jaxpr/ppermute | solution.py:23
  1002.1 61.0 %collective-permute-start.8 = (bf16[512,768]{0,1:T(8,128)(2,1)}, bf16[512,768]{0,1:T(8,128)(2,1)S(1)}, u32[]{:S(2)}, u32[]{:S(2)}) collective-permute-start(bf16[512,768]{0,1:T(8,128)(2,1)} %get-tuple-element.243), channel_id=1, source_target_pairs={{16,0},{18,2},{20,4},{22,6},{24,8},{26,10},{28,12},{30,14},{0,16},... | collective-permute-start | bytes 2359304 | tf_op jit(solution)/shard_map/ppermute | solution.py:29
  1015.1 63.8 %collective-permute-start.9 = (bf16[512,768]{0,1:T(8,128)(2,1)}, bf16[512,768]{0,1:T(8,128)(2,1)S(1)}, u32[]{:S(2)}, u32[]{:S(2)}) collective-permute-start(bf16[512,768]{0,1:T(8,128)(2,1)} %get-tuple-element.244), channel_id=1, source_target_pairs={{16,0},{18,2},{20,4},{22,6},{24,8},{26,10},{28,12},{30,14},{0,16},... | collective-permute-start | bytes 2359304 | tf_op jit(solution)/shard_map/ppermute | solution.py:29
  1084.6 137.1 %reduce-scatter.17.cloned.1.call-start = ((), (), s32[]{:S(2)}) async-start(), calls=%async_computation.25 | async-start | bytes 1769472 | tf_op jit(solution)/shard_map/reduce_scatter | solution.py:421
  1087.6 181.6 %reduce-scatter.11.cloned.1.call-start = ((), (), s32[]{:S(2)}) async-start(), calls=%async_computation.22 | async-start | bytes 1769472 | tf_op jit(solution)/shard_map/reduce_scatter | solution.py:412
  1091.0 178.3 %reduce-scatter.13.cloned.1.call-start = ((), (), s32[]{:S(2)}) async-start(), calls=%async_computation.23 | async-start | bytes 1769472 | tf_op jit(solution)/shard_map/reduce_scatter | solution.py:415
  1094.1 175.2 %reduce-scatter.15.cloned.1.call-start = ((), (), s32[]{:S(2)}) async-start(), calls=%async_computation.24 | async-start | bytes 1769472 | tf_op jit(solution)/shard_map/reduce_scatter | solution.py:418
  1096.0 173.2 %reduce-scatter.19.cloned.1.call-start = ((), (), s32[]{:S(2)}) async-start(), calls=%async_computation.26 | async-start | bytes 4718592 | tf_op jit(solution)/shard_map/reduce_scatter | solution.py:427
  1101.4 199.1 %reduce-scatter.21.cloned.1.call-start = ((), (), s32[]{:S(2)}) async-start(), calls=%async_computation.27 | async-start | bytes 4718592 | tf_op jit(solution)/shard_map/reduce_scatter | solution.py:430
  1107.7 239.0 %reduce-scatter.23.cloned.1.call-start = ((), (), s32[]{:S(2)}) async-start(), calls=%async_computation.28 | async-start | bytes 4718592 | tf_op jit(solution)/shard_map/reduce_scatter | solution.py:433
  1151.5 70.2 %all-to-all-start.5 = ((bf16[16,2,64,192]{3,2,0,1:T(8,128)(2,1)}), bf16[16,2,64,192]{3,2,0,1:T(8,128)(2,1)S(1)}, u32[]{:S(2)}, u32[]{:S(2)}) async-start(bf16[16,2,64,192]{3,2,0,1:T(8,128)(2,1)} %copy.191), calls=%async_computation.5 | async-start | bytes 2097152 | tf_op jit(solution)/shard_map/all_to_all | solution.py:384
  (191 other events, 2275.7 us)
Sparse Core Ops, SparseCore 0:
  9.5 25.5 all-gather.10
  36.6 22.7 all-gather.12
  61.0 22.8 all-gather.14
  85.2 29.4 all-gather.16
  116.1 44.7 all-gather.18
  162.2 44.8 all-gather.20
  208.7 44.8 all-gather.22
  1084.7 14.3 reduce-scatter.8
  1101.9 21.8 reduce-scatter.16
  1126.4 21.8 reduce-scatter.10
  1151.1 33.2 reduce-scatter.12
  1187.1 20.7 reduce-scatter.14
  1210.7 43.6 reduce-scatter.18
  1257.1 43.3 reduce-scatter.20
  1303.2 43.4 reduce-scatter.22
where the time goes:
time: 1680 us; the launch traced here: 1670 us
  blocking collectives  458 us (27%)
  matrix products  362 us (22%)
  starting transfers between devices  346 us (21%)
  local copies, waits for them, and re-layouts  210 us (12%)
  waiting for transfers between devices  149 us (9%)
  other arithmetic  103 us (6%)
  between operations  21.7 us (1%)
  loops' own time  19.6 us (1%)
    psum x1, blocking collectives, shards(): lax.psum((shares[0], shares[1], shares[2], shares[3], shares[4], shares[5...  312 us
    ppermute x48, starting transfers between devices, passed_along(): return lax.ppermute(block, axis, route)  296 us
    dot_general x25, matrix products, block_scores(): jnp.einsum('qhd,khd->hqk', query_rot, key_heads, preferred_element_type=j...  84.7 us
    while x152, local copies, waits for them, and re-layouts  68.8 us
    ppermute x18, waiting for transfers between devices, passed_along_2(): return lax.ppermute(block, axis, route)  59.5 us
    dot_general x9, matrix products, emit_block(): jnp.einsum('hqk,khd->qhd', prob_low, value_heads, preferred_element_type=...  57.6 us
    psum x1, blocking collectives, shards(): lax.psum((jnp.sum(stream * stream), jnp.sum(mixer_out * mixer_out), jnp.s...  57.2 us
    unnamed x177, local copies, waits for them, and re-layouts  56.8 us
  transfers between devices with their start and end apart: 85, of which 5 were waited for; matrix products, arithmetic and copies ran while one was open for 34% of the time, Pallas kernels for 0%

commit v1 on v0

--- a/solution.py
+++ b/solution.py
@@ -1,32 +1,48 @@
+import functools
+
 import jax
 import jax.numpy as jnp
+import numpy as np
 from jax import lax
+from jax.experimental import pallas as pl
+from jax.experimental.pallas import tpu as pltpu
 from jax.sharding import PartitionSpec as P
 
 HEADS = 12
 HEAD_DIM = 64
 DOC_MAX = 4096
-
+DOC_FEATURES = 16
 
 EPSILON = 1e-06
 ROPE_BASE = 500000.0
-MASKED_SCORE = -1e30
-
-
-def as_sent(array):
-    return jax.tree.map(lambda a: a.astype(jnp.bfloat16) if a.dtype == jnp.float32 else a, array)
-
-
-def passed_along(block, axis, distance):
-    devices = range(lax.axis_size(axis))
-    route = [(i - distance, i) for i in devices if i - distance in devices]
-    return lax.ppermute(block, axis, route)
-
-
-def passed_along_2(block, axis, distance):
-    devices = range(lax.axis_size(axis))
-    route = [((i - distance) % len(devices), i) for i in devices]
-    return lax.ppermute(block, axis, route)
+LOG2E = 1.4426950408889634
+LN2 = 0.6931471805599453
+FAR = 1073741824.0
+
+GROUP = 3
+GROUPS = HEADS // GROUP
+HALF = HEAD_DIM // 2
+VROWS = 80
+SLOTS = 12
+DOC_LANE = 96
+LSE_LANE = 112
+DELTA_LANE = 192
+
+F32 = jnp.float32
+BF16 = jnp.bfloat16
+VMEM_BIG = 64000000
+
+
+def nt(a, b):
+    return lax.dot_general(a, b, (((1,), (1,)), ((), ())), preferred_element_type=F32)
+
+
+def nn(a, b):
+    return jnp.dot(a, b, preferred_element_type=F32)
+
+
+def tn(a, b):
+    return lax.dot_general(a, b, (((0,), (0,)), ((), ())), preferred_element_type=F32)
 
 
 def norm_parts(field, gain_row):
@@ -43,25 +59,741 @@
     return (back_rows, jnp.sum(gradient * unit_rows, axis=0))
 
 
-def rotary(field, places, direction):
-    half_dim = HEAD_DIM // 2
-    frequency = ROPE_BASE ** (-2.0 * jnp.arange(half_dim, dtype=jnp.float32) / HEAD_DIM)
-    angles = places.astype(jnp.float32)[:, None] * frequency[None, :]
-    cosine = jnp.cos(angles)[:, None, :]
-    sine_part = direction * jnp.sin(angles)[:, None, :]
-    first_half = field[..., :half_dim]
-    second_half = field[..., half_dim:]
-    return jnp.concatenate(
-        [
-            first_half * cosine - second_half * sine_part,
-            second_half * cosine + first_half * sine_part,
+CHUNKS = 2
+
+
+def remote(src, dst, sems, kind, chunk, target):
+    return pltpu.make_async_remote_copy(
+        src_ref=src,
+        dst_ref=dst,
+        send_sem=sems[0].at[kind, chunk],
+        recv_sem=sems[1].at[kind, chunk],
+        device_id={"seq": target},
+        device_id_type=pl.DeviceIdType.MESH,
+    )
+
+
+def greet(me, group_count):
+    barrier = pltpu.get_barrier_semaphore()
+    group = me // 4
+    mine = me % 4
+    peers = (group * 4 + (mine + 2) % 4, group * 4 + mine + 1 - 2 * (mine % 2))
+    for peer in peers:
+        pl.semaphore_signal(
+            barrier, inc=1, device_id={"seq": peer}, device_id_type=pl.DeviceIdType.MESH
+        )
+    up = group + 1 < group_count
+    down = group > 0
+
+    @pl.when(up)
+    def _():
+        pl.semaphore_signal(
+            barrier, inc=1, device_id={"seq": me + 4}, device_id_type=pl.DeviceIdType.MESH
+        )
+
+    @pl.when(down)
+    def _():
+        pl.semaphore_signal(
+            barrier, inc=1, device_id={"seq": me - 4}, device_id_type=pl.DeviceIdType.MESH
+        )
+
+    pl.semaphore_wait(barrier, 2 + up.astype(jnp.int32) + down.astype(jnp.int32))
+
+
+def gather_kernel(group_count, own_ref, out_ref, send_sem, recv_sem, local_sem):
+    me = lax.axis_index("seq")
+    group = me // 4
+    mine = me % 4
+    core = mine % 2
+    far = mine // 2
+    over = (mine + 2) % 4
+    partner = mine + 1 - 2 * core
+    over_id = group * 4 + over
+    partner_id = group * 4 + partner
+    rows = own_ref.shape[0] // CHUNKS
+    sems = (send_sem, recv_sem)
+    has_one = group >= 1
+    has_two = group >= 2
+    up = group + 1 < group_count
+    greet(me, group_count)
+
+    def part(ref, chunk):
+        return ref.at[pl.ds(chunk * rows, rows)]
+
+    def slot(level, pos, chunk):
+        return out_ref.at[level * 4 + pos, pl.ds(chunk * rows, rows)]
+
+    def own_send(kind, level, target, chunk):
+        return remote(part(own_ref, chunk), slot(level, mine, chunk), sems, kind, chunk, target)
+
+    def relay(kind, level, pos, to_level, target, chunk):
+        return remote(slot(level, pos, chunk), slot(to_level, pos, chunk), sems, kind, chunk, target)
+
+    moves = {
+        "z1": lambda c: own_send(0, 1, me + 4, c),
+        "x0": lambda c: own_send(1, 0, over_id, c),
+        "c0": lambda c: own_send(2, 0, partner_id, c),
+        "c0b": lambda c: relay(3, 0, over, 0, partner_id, c),
+        "z2": lambda c: relay(4, 1, mine, 2, me + 4, c),
+        "x1": lambda c: relay(5, 1, mine, 1, over_id, c),
+        "c1a": lambda c: relay(6, 1, mine, 1, partner_id, c),
+        "c1b": lambda c: relay(7, 1, over, 1, partner_id, c),
+        "x2": lambda c: relay(8, 2, mine, 2, over_id, c),
+        "c2a": lambda c: relay(9, 2, mine, 2, partner_id, c),
+        "c2b": lambda c: relay(10, 2, over, 2, partner_id, c),
+    }
+    sends = {
+        "z1": up,
+        "x0": far == 0,
+        "c0": core == 0,
+        "c0b": far == 1,
+        "z2": has_one & up,
+        "x1": has_one,
+        "c1a": has_one,
+        "c1b": has_one,
+        "x2": has_two & (far == 1),
+        "c2a": has_two & (core == 1),
+        "c2b": has_two & (far == 0),
+    }
+    receives = {
+        "z1": has_one,
+        "x0": far == 1,
+        "c0": core == 1,
+        "c0b": far == 1,
+        "z2": has_two,
+        "x1": has_one,
+        "c1a": has_one,
+        "c1b": has_one,
+        "x2": has_two & (far == 0),
+        "c2a": has_two & (core == 0),
+        "c2b": has_two & (far == 0),
+    }
+
+    def start(name, chunk):
+        @pl.when(sends[name])
+        def _():
+            moves[name](chunk).start()
+
+    def take(name, chunk):
+        @pl.when(receives[name])
+        def _():
+            moves[name](chunk).wait_recv()
+
+    def finish(name, chunk):
+        @pl.when(sends[name])
+        def _():
+            moves[name](chunk).wait_send()
+
+    every = range(CHUNKS)
+    for chunk in every:
+        for name in ("z1", "x0", "c0"):
+            start(name, chunk)
+    local = pltpu.make_async_copy(own_ref, out_ref.at[mine], local_sem)
+    local.start()
+    for chunk in every:
+        take("z1", chunk)
+        for name in ("z2", "x1", "c1a"):
+            start(name, chunk)
+        take("x0", chunk)
+        start("c0b", chunk)
+    for chunk in every:
+        take("x1", chunk)
+        start("c1b", chunk)
+        take("z2", chunk)
+        start("x2", chunk)
+        start("c2a", chunk)
+    for chunk in every:
+        take("x2", chunk)
+        start("c2b", chunk)
+    for chunk in every:
+        for name in ("c0", "c0b", "c1a", "c1b", "c2a", "c2b"):
+            take(name, chunk)
+    local.wait()
+    for chunk in every:
+        for name in moves:
+            finish(name, chunk)
+
+
+def halo_gather(own, group_count):
+    tokens, width = own.shape
+    return pl.pallas_call(
+        functools.partial(gather_kernel, group_count),
+        out_shape=jax.ShapeDtypeStruct((SLOTS + 1, tokens, width), own.dtype),
+        in_specs=[pl.BlockSpec(memory_space=pltpu.VMEM)],
+        out_specs=pl.BlockSpec(memory_space=pl.ANY),
+        scratch_shapes=[
+            pltpu.SemaphoreType.DMA((11, CHUNKS)),
+            pltpu.SemaphoreType.DMA((11, CHUNKS)),
+            pltpu.SemaphoreType.DMA,
         ],
-        axis=-1,
-    )
-
-
-def split_heads(matrix):
-    return matrix.reshape(matrix.shape[0], HEADS, HEAD_DIM)
+        compiler_params=pltpu.CompilerParams(collective_id=1, has_side_effects=True),
+        name="halo_gather",
+    )(own)
+
+
+def reduce_kernel(
+    group_count, part_ref, out_ref, work_ref, got_ref, send_sem, recv_sem, local_sem
+):
+    me = lax.axis_index("seq")
+    group = me // 4
+    mine = me % 4
+    core = mine % 2
+    far = mine // 2
+    over = (mine + 2) % 4
+    partner = mine + 1 - 2 * core
+    partner_over = (partner + 2) % 4
+    over_id = group * 4 + over
+    partner_id = group * 4 + partner
+    rows = out_ref.shape[0] // CHUNKS
+    sems = (send_sem, recv_sem)
+    has_one = group >= 1
+    has_two = group >= 2
+    up = group + 1 < group_count
+
+    def load(level):
+        four = pl.ds(level * 4, 4)
+        return pltpu.make_async_copy(part_ref.at[four], work_ref.at[four], local_sem.at[level])
+
+    for level in (2, 1, 0):
+        load(level).start()
+    greet(me, group_count)
+
+    def span(chunk):
+        return pl.ds(chunk * rows, rows)
+
+    def send(kind, level, pos, target, chunk):
+        return remote(
+            work_ref.at[level * 4 + pos, span(chunk)],
+            got_ref.at[kind, span(chunk)],
+            sems,
+            kind,
+            chunk,
+            target,
+        )
+
+    moves = {
+        "c2o": lambda c: send(0, 2, partner_over, partner_id, c),
+        "c2": lambda c: send(1, 2, partner, partner_id, c),
+        "c1o": lambda c: send(2, 1, partner_over, partner_id, c),
+        "c1": lambda c: send(3, 1, partner, partner_id, c),
+        "c0o": lambda c: send(4, 0, partner_over, partner_id, c),
+        "c0": lambda c: send(5, 0, partner, partner_id, c),
+        "x2": lambda c: send(6, 2, over, over_id, c),
+        "x1": lambda c: send(7, 1, over, over_id, c),
+        "x0": lambda c: send(8, 0, over, over_id, c),
+        "z2": lambda c: send(9, 2, mine, me - 4, c),
+        "z1": lambda c: send(10, 1, mine, me - 4, c),
+    }
+    kinds = {name: kind for kind, name in enumerate(moves)}
+    sends = {
+        "c2o": has_two & (far == 0),
+        "c2": has_two & (core == 0),
+        "c1o": has_one,
+        "c1": has_one,
+        "c0o": far == 1,
+        "c0": core == 1,
+        "x2": has_two & (far == 0),
+        "x1": has_one,
+        "x0": far == 1,
+        "z2": has_two,
+        "z1": has_one,
+    }
+    receives = {
+        "c2o": has_two & (far == 0),
+        "c2": has_two & (core == 1),
+        "c1o": has_one,
+        "c1": has_one,
+        "c0o": far == 1,
+        "c0": core == 0,
+        "x2": has_two & (far == 1),
+        "x1": has_one,
+        "x0": far == 0,
+        "z2": has_one & up,
+        "z1": up,
+    }
+    lands = {
+        "c2o": (2, over),
+        "c2": (2, mine),
+        "c1o": (1, over),
+        "c1": (1, mine),
+        "c0o": (0, over),
+        "c0": (0, mine),
+        "x2": (2, mine),
+        "x1": (1, mine),
+        "x0": (0, mine),
+        "z2": (1, mine),
+        "z1": (0, mine),
+    }
+
+    def start(name, chunk):
+        @pl.when(sends[name])
+        def _():
+            moves[name](chunk).start()
+
+    def absorb(name, chunk):
+        @pl.when(receives[name])
+        def _():
+            moves[name](chunk).wait_recv()
+            level, pos = lands[name]
+            at = level * 4 + pos
+            total = work_ref[at, span(chunk), :].astype(F32) + got_ref[
+                kinds[name], span(chunk), :
+            ].astype(F32)
+            work_ref[at, span(chunk), :] = total.astype(BF16)
+
+    every = range(CHUNKS)
+    for level in (2, 1, 0):
+        load(level).wait()
+        for name in (f"c{level}o", f"c{level}"):
+            for chunk in every:
+                start(name, chunk)
+    for level in (2, 1, 0):
+        for chunk in every:
+            absorb(f"c{level}o", chunk)
+            start(f"x{level}", chunk)
+    for chunk in every:
+        absorb("c2", chunk)
+        absorb("x2", chunk)
+        start("z2", chunk)
+    for chunk in every:
+        absorb("c1", chunk)
+        absorb("x1", chunk)
+        absorb("z2", chunk)
+        start("z1", chunk)
+    for chunk in every:
+        absorb("c0", chunk)
+        absorb("x0", chunk)
+        absorb("z1", chunk)
+        out_ref[span(chunk), :] = work_ref[mine, span(chunk), :].astype(F32)
+    for name in moves:
+        for chunk in every:
+
+            @pl.when(sends[name])
+            def _():
+                moves[name](chunk).wait_send()
+
+
+def halo_reduce(parts, group_count):
+    slots, tokens, width = parts.shape
+    return pl.pallas_call(
+        functools.partial(reduce_kernel, group_count),
+        out_shape=jax.ShapeDtypeStruct((tokens, width), F32),
+        in_specs=[pl.BlockSpec(memory_space=pl.ANY)],
+        out_specs=pl.BlockSpec(memory_space=pltpu.VMEM),
+        scratch_shapes=[
+            pltpu.VMEM((SLOTS, tokens, width), BF16),
+            pltpu.VMEM((11, tokens, width), BF16),
+            pltpu.SemaphoreType.DMA((11, CHUNKS)),
+            pltpu.SemaphoreType.DMA((11, CHUNKS)),
+            pltpu.SemaphoreType.DMA((3,)),
+        ],
+        compiler_params=pltpu.CompilerParams(
+            collective_id=2, has_side_effects=True, vmem_limit_bytes=VMEM_BIG
+        ),
+        name="halo_reduce",
+    )(parts)
+
+
+def lane_tables(tokens):
+    theta = ROPE_BASE ** (-2.0 * jnp.arange(HALF, dtype=F32) / HEAD_DIM)
+    lanes = jnp.concatenate([theta] * GROUP + [jnp.zeros((128 - GROUP * HALF,), F32)])
+    angle = jnp.arange(tokens, dtype=F32)[:, None] * lanes[None, :]
+    return theta, lanes, jnp.cos(angle), jnp.sin(angle)
+
+
+def rotate(pair, cosine, sine):
+    first, second = pair[:, :128], pair[:, 128:]
+    return first * cosine - second * sine, second * cosine + first * sine
+
+
+def block_angles(step, cos_row, sin_row, cos_block, sin_block):
+    c_row, s_row = cos_row[...], sin_row[...]
+    c_blk, s_blk = cos_block[pl.ds(step, 1), :], sin_block[pl.ds(step, 1), :]
+    return c_row * c_blk - s_row * s_blk, s_row * c_blk + c_row * s_blk
+
+
+def head_lanes(shape, start, width):
+    lane = lax.broadcasted_iota(jnp.int32, shape, 1)
+    return (lane >= start) & (lane < start + width)
+
+
+def forward_kernel(
+    slot_ref, valid_ref, own_ref, x_ref, wq_ref, wk_ref, wv_ref, cr_ref, sr_ref, cb_ref, sb_ref,
+    kf_ref, qf_ref, out_ref, lse_ref, qm_ref, kb_ref, vt_ref, acc_ref, top_ref,
+):
+    step = pl.program_id(0)
+    tokens = own_ref.shape[0]
+
+    @pl.when(step == 0)
+    def _():
+        cosine, sine = block_angles(0, cr_ref, sr_ref, cb_ref, sb_ref)
+        features = qf_ref[...].astype(F32)
+
+        def one_group(g, carry):
+            first, second = rotate(nn(own_ref[...], wq_ref[g]), cosine, sine)
+            for hh in range(GROUP):
+                mask = head_lanes((tokens, 128), hh * HALF, HALF)
+                scale = LOG2E * HEAD_DIM**-0.5
+                qm_ref[g * GROUP + hh, :, :128] = (
+                    jnp.where(mask, first * scale, features).astype(BF16)
+                )
+                qm_ref[g * GROUP + hh, :, 128:] = (
+                    jnp.where(mask, second * scale, 0.0).astype(BF16)
+                )
+            return carry
+
+        lax.fori_loop(0, GROUPS, one_group, 0)
+        top_ref[...] = jnp.full_like(top_ref, -FAR * FAR)
+        acc_ref[...] = jnp.zeros_like(acc_ref)
+
+    @pl.when(valid_ref[step] > 0)
+    def _():
+        x = x_ref[0]
+        cosine, sine = block_angles(step, cr_ref, sr_ref, cb_ref, sb_ref)
+        features = kf_ref[0].astype(F32)
+
+        def keys(g, carry):
+            first, second = rotate(nn(x_ref[0], wk_ref[g]), cosine, sine)
+            kb_ref[g, :, :128] = (first + features).astype(BF16)
+            kb_ref[g, :, 128:] = second.astype(BF16)
+            values = nt(wv_ref[g], x_ref[0])
+            row = lax.broadcasted_iota(jnp.int32, values.shape, 0) % VROWS
+            values = jnp.where(row == HEAD_DIM, 1.0, values).astype(BF16)
+            for hh in range(GROUP):
+                vt_ref[g * GROUP + hh] = values[hh * VROWS : (hh + 1) * VROWS]
+            return carry
+
+        lax.fori_loop(0, GROUPS, keys, 0)
+
+        def attend(causal):
+            def one_group(g, carry):
+                for hh in range(GROUP):
+                    h = g * GROUP + hh
+                    scores = nt(kb_ref[g], qm_ref[h])
+                    if causal:
+                        key = lax.broadcasted_iota(jnp.int32, scores.shape, 0)
+                        query = lax.broadcasted_iota(jnp.int32, scores.shape, 1)
+                        scores = jnp.where(key <= query, scores, -FAR)
+                    old = top_ref[h]
+                    new = jnp.maximum(old, jnp.max(scores, axis=0, keepdims=True))
+                    prob = jnp.exp2(scores - new).astype(BF16)
+                    fade = jnp.exp2(old - new)
+                    acc_ref[h] = acc_ref[h] * fade + nn(vt_ref[h], prob)
+                    top_ref[h] = new
+                return carry
+
+            lax.fori_loop(0, GROUPS, one_group, 0)
+
+        @pl.when(step == 0)
+        def _():
+            attend(True)
+
+        @pl.when(step > 0)
+        def _():
+            attend(False)
+
+    @pl.when(step == pl.num_programs(0) - 1)
+    def _():
+        lses = []
+        for g in range(GROUPS):
+            parts = []
+            for h in range(g * GROUP, (g + 1) * GROUP):
+                total = acc_ref[h, HEAD_DIM : HEAD_DIM + 1, :]
+                parts.append(acc_ref[h, :HEAD_DIM, :] / total)
+                lses.append(top_ref[h] + jnp.log2(total))
+            parts.append(jnp.zeros((256 - GROUP * HEAD_DIM, tokens), F32))
+            out_ref[:, g * 256 : (g + 1) * 256] = jnp.concatenate(parts, axis=0).T
+        lses.append(jnp.zeros((128 - HEADS, tokens), F32))
+        lse_ref[...] = jnp.concatenate(lses, axis=0).T
+
+
+def whole(*shape):
+    return pl.BlockSpec(shape, lambda *_: (0,) * len(shape), pipeline_mode=pl.Buffered(1))
+
+
+def attention_forward(own, blocks, slots, valid, weights, tables, features):
+    tokens, width = own.shape
+    steps = slots.shape[0]
+    key_features, query_features = features
+    wq, wk, wv = weights
+    return pl.pallas_call(
+        forward_kernel,
+        out_shape=(
+            jax.ShapeDtypeStruct((tokens, GROUPS * 256), F32),
+            jax.ShapeDtypeStruct((tokens, 128), F32),
+        ),
+        grid_spec=pltpu.PrefetchScalarGridSpec(
+            num_scalar_prefetch=2,
+            grid=(steps,),
+            in_specs=[
+                whole(tokens, width),
+                pl.BlockSpec((1, tokens, width), lambda t, slot, valid: (slot[t], 0, 0)),
+                whole(*wq.shape),
+                whole(*wk.shape),
+                whole(*wv.shape),
+                whole(tokens, 128),
+                whole(tokens, 128),
+                whole(*tables[2].shape),
+                whole(*tables[3].shape),
+                pl.BlockSpec((1, tokens, 128), lambda t, slot, valid: (t, 0, 0)),
+                whole(tokens, 128),
+            ],
+            out_specs=[whole(tokens, GROUPS * 256), whole(tokens, 128)],
+            scratch_shapes=[
+                pltpu.VMEM((HEADS, tokens, 256), BF16),
+                pltpu.VMEM((GROUPS, tokens, 256), BF16),
+                pltpu.VMEM((HEADS, VROWS, tokens), BF16),
+                pltpu.VMEM((HEADS, VROWS, tokens), F32),
+                pltpu.VMEM((HEADS, 1, tokens), F32),
+            ],
+        ),
+        compiler_params=pltpu.CompilerParams(
+            dimension_semantics=("arbitrary",), vmem_limit_bytes=VMEM_BIG
+        ),
+        name="attention_forward",
+    )(slots, valid, own, blocks, wq, wk, wv, *tables, key_features, query_features)
+
+
+def split_bf16(column):
+    high = column.astype(BF16).astype(F32)
+    return high, column - high
+
+
+def backward_kernel(
+    slot_ref, valid_ref, own_ref, x_ref, wq_ref, wk_ref, wkt_ref, wv_ref, cr_ref, sr_ref, cb_ref,
+    sb_ref, ct_ref, st_ref, kf_ref, qf_ref, go_ref, heads_ref, lse_ref, gx_ref, dq_ref, dwk_ref,
+    dwv_ref, qb_ref, gm_ref, kb_ref, kt_ref, vb_ref, dqt_ref, dk_ref, dv_ref, gxa_ref, wka_ref,
+    wva_ref,
+):
+    step = pl.program_id(0)
+    tokens = own_ref.shape[0]
+
+    @pl.when(step == 0)
+    def _():
+        cosine, sine = block_angles(0, cr_ref, sr_ref, cb_ref, sb_ref)
+        features = qf_ref[...].astype(F32)
+
+        def one_group(g, carry):
+            first, second = rotate(nn(own_ref[...], wq_ref[g]), cosine, sine)
+            lane = lax.broadcasted_iota(jnp.int32, (tokens, 128), 1)
+            wide = lax.broadcasted_iota(jnp.int32, (tokens, 256), 1)
+            lanes = pl.ds(pl.multiple_of(g * 256, 256), 256)
+            grads = go_ref[:, lanes].astype(F32)
+            products = grads * heads_ref[:, lanes]
+            for hh in range(GROUP):
+                h = g * GROUP + hh
+                lse = jnp.sum(jnp.where(lane == h, lse_ref[...], 0.0), axis=1, keepdims=True)
+                own = head_lanes((tokens, 256), hh * HEAD_DIM, HEAD_DIM)
+                delta = jnp.sum(jnp.where(own, products, 0.0), axis=1, keepdims=True)
+                lse_one, rest = split_bf16(lse)
+                lse_two, lse_three = split_bf16(rest)
+                mask = head_lanes((tokens, 128), hh * HALF, HALF)
+                scale = LOG2E * HEAD_DIM**-0.5
+                tile = jnp.where(mask, first * scale, features)
+                tile = jnp.where(lane == LSE_LANE, -lse_one, tile)
+                tile = jnp.where(lane == LSE_LANE + 1, -lse_two, tile)
+                tile = jnp.where(lane == LSE_LANE + 2, -lse_three, tile)
+                qb_ref[h, :, :128] = tile.astype(BF16)
+                qb_ref[h, :, 128:] = jnp.where(mask, second * scale, 0.0).astype(BF16)
+                delta_one, delta_two = split_bf16(delta)
+                tile = jnp.where(own, grads, 0.0)
+                tile = jnp.where(wide == DELTA_LANE, -delta_one, tile)
+                tile = jnp.where(wide == DELTA_LANE + 1, -delta_two, tile)
+                gm_ref[h] = tile.astype(BF16)
+            return carry
+
+        lax.fori_loop(0, GROUPS, one_group, 0)
+        dqt_ref[...] = jnp.zeros_like(dqt_ref)
+        wka_ref[...] = jnp.zeros_like(wka_ref)
+        wva_ref[...] = jnp.zeros_like(wva_ref)
+
+    @pl.when(valid_ref[step] > 0)
+    def _():
+        cosine, sine = block_angles(step, cr_ref, sr_ref, cb_ref, sb_ref)
+        features = kf_ref[0].astype(F32)
+
+        def keys(g, carry):
+            first, second = rotate(nn(x_ref[0], wk_ref[g]), cosine, sine)
+            kb_ref[g, :, :128] = (first + features).astype(BF16)
+            kb_ref[g, :, 128:] = second.astype(BF16)
+            values = nn(x_ref[0], wv_ref[g])
+            wide = lax.broadcasted_iota(jnp.int32, values.shape, 1)
+            ones = (wide == DELTA_LANE) | (wide == DELTA_LANE + 1)
+            vb_ref[g] = jnp.where(ones, 1.0, values).astype(BF16)
+            turned = nt(wkt_ref[g], x_ref[0])
+            for hh in range(GROUP):
+                upper = turned[hh * HEAD_DIM : hh * HEAD_DIM + HALF]
+                lower = turned[hh * HEAD_DIM + HALF : (hh + 1) * HEAD_DIM]
+                c_row, s_row = ct_ref[step], st_ref[step]
+                kt_ref[g * GROUP + hh, :HALF] = (upper * c_row - lower * s_row).astype(BF16)
+                kt_ref[g * GROUP + hh, HALF:] = (lower * c_row + upper * s_row).astype(BF16)
+            return carry
+
+        lax.fori_loop(0, GROUPS, keys, 0)
+
+        def grads(causal):
+            def one_group(g, carry):
+                for hh in range(GROUP):
+                    h = g * GROUP + hh
+                    prob = jnp.exp2(nt(kb_ref[g], qb_ref[h]))
+                    if causal:
+                        key = lax.broadcasted_iota(jnp.int32, prob.shape, 0)
+                        query = lax.broadcasted_iota(jnp.int32, prob.shape, 1)
+                        prob = jnp.where(key <= query, prob, 0.0)
+                    grad = (prob * nt(vb_ref[g], gm_ref[h])).astype(BF16)
+                    prob = prob.astype(BF16)
+                    value_part = nn(prob, gm_ref[h])
+                    key_part = nn(grad, qb_ref[h])
+                    if hh == 0:
+                        dv_ref[...] = value_part
+                        dk_ref[...] = key_part
+                    else:
+                        dv_ref[...] += value_part
+                        dk_ref[...] += key_part
+                    dqt_ref[h] += nn(kt_ref[h], grad)
+                first, second = rotate(dk_ref[...] * LN2, cosine, -sine)
+                pad = head_lanes((tokens, 128), 0, GROUP * HALF)
+                key_rows = jnp.concatenate(
+                    [jnp.where(pad, first, 0.0), jnp.where(pad, second, 0.0)], axis=1
+                ).astype(BF16)
+                keep = head_lanes((tokens, 256), 0, GROUP * HEAD_DIM)
+                value_rows = jnp.where(keep, dv_ref[...], 0.0).astype(BF16)
+                wka_ref[g] += tn(x_ref[0], key_rows)
+                wva_ref[g] += tn(x_ref[0], value_rows)
+                gxa_ref[...] += nt(key_rows, wk_ref[g]) + nt(value_rows, wv_ref[g])
+                return carry
+
+            gxa_ref[...] = jnp.zeros_like(gxa_ref)
+            lax.fori_loop(0, GROUPS, one_group, 0)
+            gx_ref[0] = gxa_ref[...].astype(BF16)
+
+        @pl.when(step == 0)
+        def _():
+            grads(True)
+
+        @pl.when(step > 0)
+        def _():
+            grads(False)
+
+    @pl.when(step == pl.num_programs(0) - 1)
+    def _():
+        for h in range(HEADS):
+            upper = dqt_ref[h, :HALF, :] * HEAD_DIM**-0.5
+            lower = dqt_ref[h, HALF:, :] * HEAD_DIM**-0.5
+            c_row, s_row = ct_ref[0], st_ref[0]
+            dq_ref[h * HEAD_DIM : h * HEAD_DIM + HALF, :] = (
+                upper * c_row + lower * s_row
+            ).astype(BF16)
+            dq_ref[h * HEAD_DIM + HALF : (h + 1) * HEAD_DIM, :] = (
+                lower * c_row - upper * s_row
+            ).astype(BF16)
+        dwk_ref[...] = wka_ref[...].astype(BF16)
+        dwv_ref[...] = wva_ref[...].astype(BF16)
+
+
+def attention_backward(
+    own, blocks, slots, valid, weights, tables, turned, features, grad_heads, heads, lse
+):
+    tokens, width = own.shape
+    steps = slots.shape[0]
+    key_features, query_features = features
+    wq, wk, wkt, wv = weights
+    ct, st = turned
+    return pl.pallas_call(
+        backward_kernel,
+        out_shape=(
+            jax.ShapeDtypeStruct((SLOTS + 1, tokens, width), BF16),
+            jax.ShapeDtypeStruct((width, tokens), BF16),
+            jax.ShapeDtypeStruct(wk.shape, BF16),
+            jax.ShapeDtypeStruct(wv.shape, BF16),
+        ),
+        grid_spec=pltpu.PrefetchScalarGridSpec(
+            num_scalar_prefetch=2,
+            grid=(steps,),
+            in_specs=[
+                whole(tokens, width),
+                pl.BlockSpec((1, tokens, width), lambda t, slot, valid: (slot[t], 0, 0)),
+                whole(*wq.shape),
+                whole(*wk.shape),
+                whole(*wkt.shape),
+                whole(*wv.shape),
+                whole(tokens, 128),
+                whole(tokens, 128),
+                whole(*tables[2].shape),
+                whole(*tables[3].shape),
+                whole(*ct.shape),
+                whole(*st.shape),
+                pl.BlockSpec((1, tokens, 128), lambda t, slot, valid: (t, 0, 0)),
+                whole(tokens, 128),
+                whole(tokens, GROUPS * 256),
+                whole(tokens, GROUPS * 256),
+                whole(tokens, 128),
+            ],
+            out_specs=[
+                pl.BlockSpec((1, tokens, width), lambda t, slot, valid: (slot[t], 0, 0)),
+                whole(width, tokens),
+                whole(*wk.shape),
+                whole(*wv.shape),
+            ],
+            scratch_shapes=[
+                pltpu.VMEM((HEADS, tokens, 256), BF16),
+                pltpu.VMEM((HEADS, tokens, 256), BF16),
+                pltpu.VMEM((GROUPS, tokens, 256), BF16),
+                pltpu.VMEM((HEADS, HEAD_DIM, tokens), BF16),
+                pltpu.VMEM((GROUPS, tokens, 256), BF16),
+                pltpu.VMEM((HEADS, HEAD_DIM, tokens), F32),
+                pltpu.VMEM((tokens, 256), F32),
+                pltpu.VMEM((tokens, 256), F32),
+                pltpu.VMEM((tokens, width), F32),
+                pltpu.VMEM(wk.shape, F32),
+                pltpu.VMEM(wv.shape, F32),
+            ],
+        ),
+        compiler_params=pltpu.CompilerParams(
+            dimension_semantics=("arbitrary",), vmem_limit_bytes=VMEM_BIG
+        ),
+        name="attention_backward",
+    )(
+        slots, valid, own, blocks, wq, wk, wkt, wv, *tables, ct, st, key_features,
+        query_features, grad_heads, heads, lse,
+    )
+
+
+def rotary_groups(weight):
+    rows = weight.shape[0]
+    split = weight.reshape(rows, GROUPS, GROUP, 2, HALF).transpose(1, 0, 3, 2, 4)
+    split = split.reshape(GROUPS, rows, 2, GROUP * HALF)
+    split = jnp.pad(split, ((0, 0), (0, 0), (0, 0), (0, 128 - GROUP * HALF)))
+    return split.reshape(GROUPS, rows, 256)
+
+
+def from_rotary_groups(grouped):
+    rows = grouped.shape[1]
+    split = grouped.reshape(GROUPS, rows, 2, 128)[..., : GROUP * HALF]
+    split = split.reshape(GROUPS, rows, 2, GROUP, HALF).transpose(1, 0, 3, 2, 4)
+    return split.reshape(rows, HEADS * HEAD_DIM)
+
+
+def value_groups(weight):
+    rows = weight.shape[0]
+    split = weight.reshape(rows, GROUPS, GROUP * HEAD_DIM).transpose(1, 0, 2)
+    return jnp.pad(split, ((0, 0), (0, 0), (0, 256 - GROUP * HEAD_DIM)))
+
+
+def from_value_groups(grouped):
+    rows = grouped.shape[1]
+    return grouped[..., : GROUP * HEAD_DIM].transpose(1, 0, 2).reshape(rows, HEADS * HEAD_DIM)
+
+
+def padded_rows(weight):
+    split = weight.reshape(GROUPS, GROUP * HEAD_DIM, weight.shape[1])
+    split = jnp.pad(split, ((0, 0), (0, 256 - GROUP * HEAD_DIM), (0, 0)))
+    return split.reshape(GROUPS * 256, weight.shape[1])
+
+
+def from_padded_rows(grouped):
+    split = grouped.reshape(GROUPS, 256, grouped.shape[1])[:, : GROUP * HEAD_DIM]
+    return split.reshape(HEADS * HEAD_DIM, grouped.shape[1])
 
 
 def shards(
@@ -169,85 +901,49 @@
     residual, unit_zero, inverse_zero = norm_parts(stream, gain_stream)
     normed_one, unit_one, inverse_one = norm_parts(residual, gain_mixer)
     mixer_in = normed_one.astype(jnp.bfloat16)
-    query_rows = jnp.dot(mixer_in, full_query, preferred_element_type=jnp.float32)
-    key_rows = jnp.dot(mixer_in, full_key, preferred_element_type=jnp.float32)
-    value_rows = jnp.dot(mixer_in, full_value, preferred_element_type=jnp.float32)
     my_index = lax.axis_index("seq")
-    places = my_index * tokens + jnp.arange(tokens, dtype=jnp.int32)
-    query_rot = rotary(split_heads(query_rows), places, 1.0).astype(jnp.bfloat16)
-    key_rot = rotary(split_heads(key_rows), places, 1.0).astype(jnp.bfloat16).reshape(tokens, -1)
-    value_low = value_rows.astype(jnp.bfloat16)
-    own_docs = doc_ids[0]
-    own_block = (key_rot, value_low, own_docs.astype(jnp.bfloat16))
-    query_docs = own_docs.astype(jnp.float32)
-
-    def block_scores(key_block, source):
-        key_heads = split_heads(key_block[0])
-        raw_scores = jnp.einsum(
-            "qhd,khd->hqk", query_rot, key_heads, preferred_element_type=jnp.float32
-        )
-        key_places = source * tokens + jnp.arange(tokens, dtype=jnp.int32)
-        allowed = (
-            (places[:, None] >= key_places[None, :])
-            & (query_docs[:, None] == key_block[2].astype(jnp.float32)[None, :])
-            & (source >= 0)
-        )
-        return jnp.where(allowed[None], raw_scores * score_scale, MASKED_SCORE)
-
-    def absorb(running, key_block, source):
-        row_max, row_sum = running
-        scores = block_scores(key_block, source)
-        new_max = jnp.maximum(row_max, jnp.max(scores, axis=-1, keepdims=True))
-        row_sum = row_sum * jnp.exp(row_max - new_max) + jnp.sum(
-            jnp.exp(scores - new_max), axis=-1, keepdims=True
-        )
-        return (new_max, row_sum)
-
-    start_running = (
-        jnp.full((HEADS, tokens, 1), MASKED_SCORE, jnp.float32),
-        jnp.zeros((HEADS, tokens, 1), jnp.float32),
-    )
-    running = absorb(start_running, own_block, my_index)
-    doc_span = min(DOC_MAX, tokens * seq_count)
-    reach_count = min((doc_span + tokens - 2) // tokens, seq_count - 1)
-    steps_back = jnp.arange(1, reach_count + 1, dtype=jnp.int32)
-
-    def fetch_step(carried_in, step_back):
-        key_block, running_now = carried_in
-        key_block = jax.tree.map(
-            lambda part, own: part.astype(own.dtype),
-            passed_along(as_sent(key_block), "seq", 1),
-            key_block,
-        )
-        return ((key_block, absorb(running_now, key_block, my_index - step_back)), key_block)
-
-    (unused_block, running), kept_blocks = lax.scan(fetch_step, (own_block, running), steps_back)
-    log_sum = running[0] + jnp.log(running[1])
-
-    def emit_block(partial_value, key_block, source):
-        low_sum, full_sum = partial_value
-        probability = jnp.exp(block_scores(key_block, source) - log_sum)
-        value_heads = split_heads(key_block[1])
-        prob_low = probability.astype(jnp.bfloat16)
-        prob_rest = (probability - prob_low.astype(jnp.float32)).astype(jnp.bfloat16)
-        main_part = jnp.einsum(
-            "hqk,khd->qhd", prob_low, value_heads, preferred_element_type=jnp.float32
-        )
-        rest_part = jnp.einsum(
-            "hqk,khd->qhd", prob_rest, value_heads, preferred_element_type=jnp.float32
-        )
-        return (low_sum + main_part, full_sum + (main_part + rest_part))
-
-    zero_heads = jnp.zeros((tokens, HEADS, HEAD_DIM), jnp.float32)
-    partial_value = emit_block((zero_heads, zero_heads), own_block, my_index)
-
-    def emit_step(partial_now, scan_item):
-        step_back, key_block = scan_item
-        return (emit_block(partial_now, key_block, my_index - step_back), None)
-
-    (mixed_low, mixed_full), unused = lax.scan(emit_step, partial_value, (steps_back, kept_blocks))
-    heads_low = mixed_low.reshape(tokens, -1).astype(jnp.bfloat16)
-    mixer_out = jnp.dot(heads_low, full_out, preferred_element_type=jnp.float32)
+    reach_count = min((min(DOC_MAX, tokens * seq_count) + tokens - 2) // tokens, seq_count - 1)
+    steps = reach_count + 1
+    sources = my_index - jnp.arange(steps, dtype=jnp.int32)
+    valid = (sources >= 0).astype(jnp.int32)
+    levels = my_index // 4 - sources // 4
+    slots = jnp.where(sources >= 0, levels * 4 + sources % 4, SLOTS)
+    all_docs = lax.all_gather(doc_ids[0], "seq", axis=0)
+    step_docs = jnp.take(all_docs, jnp.maximum(sources, 0), axis=0)
+    lane = jnp.arange(128, dtype=jnp.int32)
+    doc_lane = (lane >= DOC_LANE) & (lane < DOC_LANE + DOC_FEATURES)
+    lse_lane = (lane >= LSE_LANE) & (lane < LSE_LANE + 3)
+    same = step_docs[:, :, None] == (lane - DOC_LANE)[None, None, :]
+    key_features = ((same & doc_lane) | lse_lane).astype(BF16)
+    same_own = doc_ids[0][:, None] == (lane - DOC_LANE)[None, :]
+    query_features = jnp.where(doc_lane & ~same_own, -FAR, 0.0).astype(BF16)
+    theta, lane_theta, cos_row, sin_row = lane_tables(tokens)
+    starts = (sources * tokens).astype(F32)
+    block_rows = jnp.pad(starts, (0, 16 - steps))[:, None] * lane_theta[None, :]
+    tables = (cos_row, sin_row, jnp.cos(block_rows), jnp.sin(block_rows))
+    turned_block = starts[:, None, None] * theta[None, :, None]
+    cos_block, sin_block = jnp.cos(turned_block), jnp.sin(turned_block)
+    turned_row = theta[:, None] * jnp.arange(tokens, dtype=F32)[None, :]
+    cos_turn, sin_turn = jnp.cos(turned_row)[None], jnp.sin(turned_row)[None]
+    turned = (
+        cos_block * cos_turn - sin_block * sin_turn,
+        sin_block * cos_turn + cos_block * sin_turn,
+    )
+    features = (key_features, query_features)
+    query_groups = rotary_groups(full_query)
+    key_groups = rotary_groups(full_key)
+    value_turned = jnp.pad(
+        full_value.T.reshape(HEADS, HEAD_DIM, -1), ((0, 0), (0, VROWS - HEAD_DIM), (0, 0))
+    ).reshape(GROUPS, GROUP * VROWS, -1)
+    key_turned = full_key.T.reshape(GROUPS, GROUP * HEAD_DIM, -1)
+    value_grouped = value_groups(full_value)
+    out_rows = padded_rows(full_out)
+    blocks = halo_gather(mixer_in, seq_count // 4)
+    mixed_full, log_sum = attention_forward(
+        mixer_in, blocks, slots, valid, (query_groups, key_groups, value_turned), tables, features
+    )
+    heads_low = mixed_full.astype(BF16)
+    mixer_out = jnp.dot(heads_low, out_rows, preferred_element_type=jnp.float32)
     middle = residual + mixer_out
     normed_two, unit_two, inverse_two = norm_parts(middle, gain_feed)
     feed_in = normed_two.astype(jnp.bfloat16)
@@ -282,88 +978,32 @@
     back_two, grad_feed_gain = norm_back(grad_feed_in, unit_two, inverse_two, gain_feed)
     grad_middle = grad_result + back_two
     grad_mixer = grad_middle.astype(jnp.bfloat16)
-    grad_out = jnp.einsum("te,td->ed", heads_low, grad_mixer, preferred_element_type=jnp.float32)
-    grad_heads = split_heads(
-        jnp.einsum("td,ed->te", grad_mixer, full_out, preferred_element_type=jnp.float32).astype(
-            jnp.bfloat16
-        )
-    )
-    delta_rows = jnp.sum(grad_heads.astype(jnp.float32) * mixed_full, axis=-1)
-    row_delta = jnp.transpose(delta_rows)[:, :, None]
-
-    def block_grads(key_block, source):
-        probability = jnp.exp(block_scores(key_block, source) - log_sum)
-        key_heads = split_heads(key_block[0])
-        value_heads = split_heads(key_block[1])
-        grad_prob = jnp.einsum(
-            "qhd,khd->hqk", grad_heads, value_heads, preferred_element_type=jnp.float32
-        )
-        grad_score = (probability * (grad_prob - row_delta)).astype(jnp.bfloat16)
-        part_query = (
-            jnp.einsum("hqk,khd->qhd", grad_score, key_heads, preferred_element_type=jnp.float32)
-            * score_scale
-        )
-        part_key = (
-            jnp.einsum("hqk,qhd->khd", grad_score, query_rot, preferred_element_type=jnp.float32)
-            * score_scale
-        )
-        part_value = jnp.einsum(
-            "hqk,qhd->khd",
-            probability.astype(jnp.bfloat16),
-            grad_heads,
-            preferred_element_type=jnp.float32,
-        )
-        return (part_query, part_key.reshape(tokens, -1), part_value.reshape(tokens, -1))
-
-    own_query, own_key, own_value = block_grads(own_block, my_index)
-
-    def take_block(previous):
-        return jax.tree.map(
-            lambda part, own: part.astype(own.dtype),
-            passed_along(as_sent(previous), "seq", 1),
-            previous,
-        )
-
-    def back_step(carried_in, scan_item):
-        step_back, kept_item = scan_item
-        passing, grad_now, previous = carried_in
-        key_block = take_block(previous)
-        part_query, part_key, part_value = block_grads(key_block, my_index - step_back)
-        grad_now = grad_now + part_query
-        passing = jax.tree.map(
-            lambda part, own: part.astype(own.dtype),
-            passed_along_2(as_sent(passing), "seq", 1),
-            passing,
-        )
-        return (((passing[0] + part_key, passing[1] + part_value), grad_now, key_block), None)
-
-    (passing, grad_query_rot, unused_block), sent_parts = lax.scan(
-        back_step, ((own_key, own_value), own_query, own_block), (steps_back, kept_blocks)
-    )
-    carried = (
-        passed_along_2(passing[0].astype(jnp.bfloat16), "seq", -reach_count).astype(jnp.float32),
-        passed_along_2(passing[1].astype(jnp.bfloat16), "seq", -reach_count).astype(jnp.float32),
-    )
-    grad_query_low = rotary(grad_query_rot, places, -1.0).reshape(tokens, -1).astype(jnp.bfloat16)
-    grad_key_low = (
-        rotary(split_heads(carried[0]), places, -1.0).reshape(tokens, -1).astype(jnp.bfloat16)
-    )
-    grad_value_low = carried[1].astype(jnp.bfloat16)
+    grad_out = from_padded_rows(
+        jnp.einsum("te,td->ed", heads_low, grad_mixer, preferred_element_type=jnp.float32)
+    )
+    grad_heads = jnp.einsum(
+        "td,ed->te", grad_mixer, out_rows, preferred_element_type=jnp.float32
+    ).astype(jnp.bfloat16)
+    parts, grad_query_turned, grad_key_groups, grad_value_groups = attention_backward(
+        mixer_in,
+        blocks,
+        slots,
+        valid,
+        (query_groups, key_groups, key_turned, value_grouped),
+        tables,
+        turned,
+        features,
+        grad_heads,
+        mixed_full,
+        log_sum,
+    )
+    grad_key = from_rotary_groups(grad_key_groups)
+    grad_value = from_value_groups(grad_value_groups)
+    grad_mixer_in = halo_reduce(parts, seq_count // 4) + jnp.einsum(
+        "et,de->td", grad_query_turned, full_query, preferred_element_type=jnp.float32
+    )
     grad_query = jnp.einsum(
-        "td,te->de", mixer_in, grad_query_low, preferred_element_type=jnp.float32
-    )
-    grad_key = jnp.einsum("td,te->de", mixer_in, grad_key_low, preferred_element_type=jnp.float32)
-    grad_value = jnp.einsum(
-        "td,te->de", mixer_in, grad_value_low, preferred_element_type=jnp.float32
-    )
-    grad_mixer_in = jnp.einsum(
-        "te,de->td", grad_query_low, full_query, preferred_element_type=jnp.float32
-    )
-    grad_mixer_in = grad_mixer_in + jnp.einsum(
-        "te,de->td", grad_key_low, full_key, preferred_element_type=jnp.float32
-    )
-    grad_mixer_in = grad_mixer_in + jnp.einsum(
-        "te,de->td", grad_value_low, full_value, preferred_element_type=jnp.float32
+        "td,et->de", mixer_in, grad_query_turned, preferred_element_type=jnp.float32
     )
     back_one, grad_mixer_gain = norm_back(grad_mixer_in, unit_one, inverse_one, gain_mixer)
     grad_residual = grad_middle + back_one

time: 1680 us -> 1180 us (0.70)
  starting transfers between devices: 346 us -> 24.2 us
  Pallas kernels: 0 us -> 317 us
  matrix products: 362 us -> 57.7 us
  local copies, waits for them, and re-layouts: 210 us -> 117 us
  other arithmetic: 103 us -> 38.2 us
  waiting for transfers between devices: 149 us -> 126 us
  loops' own time: 19.6 us -> 0 us
    ppermute x66 -> x0, starting transfers between devices: 330 us -> none  [the longest x48 296 us: passed_along(): return lax.ppermute(block, axis, route)]
    pallas_call x0 -> x4, Pallas kernels: none -> 317 us  [the longest x1 244 us: halo_reduce(): pl.pallas_call(functools.partial(reduce_kernel, group_count), out_shape=j...]
    dot_general x90 -> x4, matrix products: 313 us -> 13.2 us  [the longest x1 4.06 us: shards(): jnp.einsum('et,de->td', grad_query_turned, full_query, preferred_element_...]
    while x152 -> x0, local copies, waits for them, and re-layouts: 68.8 us -> none
    ppermute x66 -> x0, waiting for transfers between devices: 59.7 us -> none  [the longest x18 59.5 us: passed_along_2(): return lax.ppermute(block, axis, route)]
    reduce_scatter x1, waiting for transfers between devices: 0.01 us -> 46.1 us  [shards(): lax.psum_scatter(grad_gate.astype(jnp.bfloat16), 'shard', scatter_dimensi...]
    reduce_scatter x1, waiting for transfers between devices: 46.1 us -> 0.02 us  [shards(): lax.psum_scatter(grad_down.astype(jnp.bfloat16), 'shard', scatter_dimensi...]
    add x68 -> x1, other arithmetic: 38 us -> 1.22 us  [shards(): sin_block * cos_turn + cos_block * sin_turn]
  transfers between devices with their start and end apart: 85 -> 20, of which waited for: 5 -> 5; matrix products, arithmetic and copies ran while one was open for 34% -> 15% of each run, Pallas kernels for 0% -> 3%
where the time goes in v1:
time: 1180 us; the launch traced here: 1170 us
  blocking collectives  465 us (39%)
  Pallas kernels  317 us (27%)
  waiting for transfers between devices  126 us (11%)
  local copies, waits for them, and re-layouts  117 us (10%)
  matrix products  57.7 us (5%)
  other arithmetic  38.2 us (3%)
  starting transfers between devices  24.2 us (2%)
  between operations  21.2 us (2%)
    psum x1, blocking collectives, shards(): lax.psum((shares[0], shares[1], shares[2], shares[3], shares[4], shares[5...  309 us
    pallas_call x1, Pallas kernels, halo_reduce(): pl.pallas_call(functools.partial(reduce_kernel, group_count), out_shape=j...  244 us
    unnamed x86, local copies, waits for them, and re-layouts  65 us
    psum x1, blocking collectives, shards(): lax.psum((jnp.sum(stream * stream), jnp.sum(mixer_out * mixer_out), jnp.s...  58.3 us
    reduce_scatter x1, waiting for transfers between devices, shards(): lax.psum_scatter(grad_gate.astype(jnp.bfloat16), 'shard', scatter_dimensi...  46.1 us
    all_to_all x1, blocking collectives, shards(): lax.all_to_all(outgoing.reshape(seq_count, shard_count, capacity, -1), 's...  43.7 us
    pallas_call x1, Pallas kernels, attention_backward(): pl.pallas_call(backward_kernel, out_shape=(jax.ShapeDtypeStruct((SLOTS +...  32.7 us
    reduce_scatter x1, waiting for transfers between devices, shards(): lax.psum_scatter(grad_up.astype(jnp.bfloat16), 'shard', scatter_dimension...  28.3 us
  transfers between devices with their start and end apart: 20, of which 5 were waited for; matrix products, arithmetic and copies ran while one was open for 15% of the time, Pallas kernels for 3%

profile of v1, /device:TPU:0, one launch (start us, length us, event | category | flops | bytes accessed | tf_op | source)
XLA Modules:
  0.0 1166.3 jit_solution(14312452150493331475)
XLA Ops:
  20.4 7.4 all-to-all-start
  42.4 12.6 %all_gather.36 = bf16[384,768]{1,0:T(8,128)(2,1)S(1)} all-gather(bf16[192,768]{1,0:T(8,128)(2,1)S(1)} %copy-done.13), channel_id=1, replica_groups=mesh['seq'=16,'shard'=2] {'shard'}, dimensions={0}, use_global_device_ids=true | all-gather | bytes 884736 | tf_op jit(solution)/shard_map/all_gather | solution.py:825
  60.8 22.0 %all-gather.2 = s32[16,1,512]{2,1,0:T(1,128)S(1)} all-gather(s32[1,1,512]{2,1,0:T(1,128)S(1)} %bitcast.136), channel_id=1, replica_groups=mesh['seq'=16,'shard'=2] {'seq'}, dimensions={0}, use_global_device_ids=true | all-gather | bytes 34816 | tf_op jit(solution)/shard_map/all_gather | solution.py:911
  82.9 14.8 %copy.147 = bf16[25000,192]{1,0:T(8,128)(2,1)} copy(bf16[25000,192]{0,1:T(8,128)(2,1)} %param.21) | data formatting | bytes 19200000 | tf_op args[4]
  99.2 12.9 %gather_fusion = bf16[2048,192]{1,0:T(8,128)(2,1)S(1)} fusion(bf16[25000,192]{1,0:T(8,128)(2,1)} %copy.147, s32[2048]{0:T(1024)S(1)} %broadcast_clamp_fusion), kind=kCustom, calls=%fused_computation | custom fusion | bytes 1581056 | tf_op jit(solution)/shard_map/jit(_take)/gather | solution.py:880
  123.0 17.1 %all-to-all-done.2 = bf16[16,2,64,192]{3,2,1,0:T(8,128)(2,1)S(1)} async-done(((bf16[16,2,64,192]{3,2,1,0:T(8,128)(2,1)}), bf16[16,2,64,192]{3,2,1,0:T(8,128)(2,1)S(1)}, u32[]{:S(2)}, u32[]{:S(2)}) %all-to-all-start.2) | async-done | bytes 786464 | tf_op jit(solution)/shard_map/all_to_all | solution.py:883
  161.7 8.6 all-to-all-done.3
  179.6 20.1 %halo_gather.1.x_ref = bf16[13,512,768]{2,1,0:T(8,128)(2,1)} custom-call(bf16[512,768]{1,0:T(8,128)(2,1)} %multiply_convert_fusion.4.own_ref), custom_call_target="tpu_custom_call" | custom-call | tf_op jit(solution)/shard_map/halo_gather/pallas_call | solution.py:219
  199.7 20.7 %attention_forward.1 = (f32[512,1024]{1,0:T(8,128)}, f32[512,128]{1,0:T(8,128)}) custom-call(s32[9]{0:T(128)} %compare_select_fusion.6.slot_ref, s32[9]{0:T(128)} %compare_convert_fusion.valid_ref, bf16[512,768]{1,0:T(8,128)(2,1)} %multiply_convert_fusion.4.own_ref, bf16[13,512,768]{2,1,0:T(8,128)(2,1)} %halo_gather.1.x_ref, ...), custom_call_target="tpu_custom_call" | custom-call | tf_op jit(solution)/shard_map/attention_forward/pallas_call | solution.py:519
  226.6 6.3 fusion.29
  232.9 5.9 fusion.28
  238.9 22.8 %all-gather.24.cloned.1.call-done = bf16[2048,768]{1,0:T(8,128)(2,1)} async-done(((bf16[1024,768]{1,0:T(8,128)(2,1)}), bf16[2048,768]{1,0:T(8,128)(2,1)}) %all-gather.24.cloned.1.call-update) | async-done | bytes 3145744 | tf_op jit(solution)/shard_map/all_gather | solution.py:834
  261.7 7.9 multiply_convert_fusion
  281.7 32.7 %attention_backward.1 = (bf16[13,512,768]{2,1,0:T(8,128)(2,1)}, bf16[768,512]{1,0:T(8,128)(2,1)}, bf16[4,768,256]{2,1,0:T(8,128)(2,1)}, bf16[4,768,256]{2,1,0:T(8,128)(2,1)}) custom-call(s32[9]{0:T(128)} %compare_select_fusion.6.slot_ref, s32[9]{0:T(128)} %compare_convert_fusion.valid_ref, bf16[512,768]{1,0:T(8,128)(2,1)} %multiply_convert_fusion.4.own_ref, ...), custom_call_target="tpu_custom_call" | custom-call | tf_op jit(solution)/shard_map/attention_backward/pallas_call | solution.py:702
  314.4 243.8 %halo_reduce.1 = f32[512,768]{1,0:T(8,128)} custom-call(bf16[13,512,768]{2,1,0:T(8,128)(2,1)} %get-tuple-element.25.part_ref), custom_call_target="tpu_custom_call" | custom-call | tf_op jit(solution)/shard_map/halo_reduce/pallas_call | solution.py:378
  599.3 5.3 scatter_custom_fusion.1
  604.6 43.7 %all_to_all.30 = bf16[16,2,64,192]{3,2,1,0:T(8,128)(2,1)S(1)} all-to-all(bf16[16,2,64,192]{3,2,1,0:T(8,128)(2,1)S(1)} %bitcast.124), channel_id=1, replica_groups=mesh['seq'=16,'shard'=2] {'seq'}, dimensions={0} | all-to-all | bytes 1572864 | tf_op jit(solution)/shard_map/all_to_all | solution.py:1025
  654.3 58.3 %all-reduce.9 = (f32[]{:T(128)}, f32[]{:T(128)}, f32[]{:T(128)}) all-reduce(f32[]{:T(128)} %get-tuple-element.120, f32[]{:T(128)} %get-tuple-element.147, f32[]{:T(128)} %get-tuple-element.144), channel_id=1, replica_groups=mesh['seq'=16,'shard'=2] {'seq','shard'}, use_global_device_ids=true, to_apply=%region_9.10 | all-reduce | flops 3 | bytes 24 | tf_op jit(solution)/shard_map/psum | solution.py:957
  714.6 5.7 all-reduce.11
  721.1 22.3 %scatter_custom_fusion.2 = f32[25000,192]{1,0:T(8,128)} fusion(s32[2048]{0:T(1024)S(1)} %bitcast.132, f32[]{:T(128)} %constant.120.clone.1, bf16[2048,192]{1,0:T(8,128)(2,1)S(1)} %bitcast.123), kind=kCustom, calls=%fused_computation.6 | custom fusion | flops 786432 | bytes 20248580 | tf_op jit(solution)/shard_map/scatter-add | solution.py:1043
  743.4 23.5 %copy.164 = f32[25000,192]{0,1:T(8,128)} copy(f32[25000,192]{1,0:T(8,128)} %scatter_custom_fusion.2) | data formatting | bytes 38400000
  769.7 28.3 %reduce-scatter.21.cloned.1.call-done = bf16[384,2048]{1,0:T(8,128)(2,1)} async-done(((bf16[768,2048]{1,0:T(8,128)(2,1)}), bf16[384,2048]{1,0:T(8,128)(2,1)}) %reduce-scatter.21.cloned.1.call-update) | async-done | bytes 1572880 | tf_op jit(solution)/shard_map/reduce_scatter | solution.py:1070
  798.1 46.1 %reduce-scatter.19.cloned.1.call-done = bf16[384,2048]{1,0:T(8,128)(2,1)} async-done(((bf16[768,2048]{1,0:T(8,128)(2,1)}), bf16[384,2048]{1,0:T(8,128)(2,1)}) %reduce-scatter.19.cloned.1.call-update) | async-done | bytes 1572880 | tf_op jit(solution)/shard_map/reduce_scatter | solution.py:1067
  844.2 309.3 %all-reduce.13 = (f32[192,768]{1,0:T(8,128)}, f32[384]{0:T(512)}, f32[384,768]{1,0:T(8,128)}, f32[384,768]{0,1:T(8,128)S(1)}, f32[384,768]{0,1:T(8,128)S(1)}, /*...) all-reduce(bf16[192,768]{1,0:T(8,128)(2,1)} %reduce-scatter.13.clon, ...), channel_id=1, replica_groups=mesh['seq'=16,'shard'=2] {'seq'}, use_global_device_ids=true, to_apply=%region_17.18 | all-reduce | flops 3687552 | bytes 22127616 | tf_op jit(solution)/shard_map/psum | solution.py:1080
  (243 shorter events, 147.1 us)
Async XLA Ops:
  7.2 141.1 %all-gather.14.cloned.1.call-start = ((), (), s32[]{:S(2)}) async-start(), calls=%async_computation.15 | async-start | bytes 1769472 | tf_op jit(solution)/shard_map/all_gather | solution.py:828
  9.4 140.2 %all-gather.18.cloned.1.call-start = ((), (), s32[]{:S(2)}) async-start(), calls=%async_computation.17 | async-start | bytes 1769472 | tf_op jit(solution)/shard_map/all_gather | solution.py:830
  10.2 143.7 %all-gather.12.cloned.1.call-start = ((), (), s32[]{:S(2)}) async-start(), calls=%async_computation.14 | async-start | bytes 1769472 | tf_op jit(solution)/shard_map/all_gather | solution.py:827
  11.3 145.7 %all-gather.16.cloned.1.call-start = ((), (), s32[]{:S(2)}) async-start(), calls=%async_computation.16 | async-start | bytes 1769472 | tf_op jit(solution)/shard_map/all_gather | solution.py:829
  12.5 214.2 %all-gather.22.cloned.1.call-start = ((), (), s32[]{:S(2)}) async-start(), calls=%async_computation.19 | async-start | bytes 4718592 | tf_op jit(solution)/shard_map/all_gather | solution.py:833
  13.1 219.8 %all-gather.20.cloned.1.call-start = ((), (), s32[]{:S(2)}) async-start(), calls=%async_computation.18 | async-start | bytes 4718592 | tf_op jit(solution)/shard_map/all_gather | solution.py:832
  14.7 18.7 %copy-start.18 = (bf16[384]{0:T(512)(128)(2,1)S(1)}, bf16[384]{0:T(512)(128)(2,1)}, u32[]{:S(2)}) copy-start(bf16[384]{0:T(512)(128)(2,1)} %param.28) | copy-start | bytes 2308
  14.7 23.1 %copy-start.19 = (bf16[384]{0:T(512)(128)(2,1)S(1)}, bf16[384]{0:T(512)(128)(2,1)}, u32[]{:S(2)}) copy-start(bf16[384]{0:T(512)(128)(2,1)} %param.32) | copy-start | bytes 2308
  14.7 27.6 %copy-start.13 = (bf16[192,768]{1,0:T(8,128)(2,1)S(1)}, bf16[192,768]{1,0:T(8,128)(2,1)}, u32[]{:S(2)}) copy-start(bf16[192,768]{1,0:T(8,128)(2,1)} %param.22) | copy-start | bytes 884740
  20.4 34.7 %all-to-all-start = ((s32[16,1,128]{2,1,0:T(1,128)}), s32[16,1,128]{2,1,0:T(1,128)S(1)}, u32[]{:S(2)}, u32[]{:S(2)}) async-start(s32[16,1,128]{2,1,0:T(1,128)} %reshape.530), calls=%async_computation | async-start | bytes 16384 | tf_op jit(solution)/shard_map/all_to_all | solution.py:867
  27.8 33.0 %copy-start.15 = (s32[1,512]{1,0:T(1,128)S(1)}, s32[1,512]{1,0:T(1,128)}, u32[]{:S(2)}) copy-start(s32[1,512]{1,0:T(1,128)} %param.18) | copy-start | bytes 6148
  27.8 233.9 %all-gather.24.cloned.1.call-start = ((), (), s32[]{:S(2)}) async-start(), calls=%async_computation.20 | async-start | bytes 4718592 | tf_op jit(solution)/shard_map/all_gather | solution.py:834
  57.1 41.2 %all-to-all-start.1 = ((s32[2,1,1024]{2,1,0:T(1,128)}), s32[2,1,1024]{2,1,0:T(1,128)S(1)}, u32[]{:S(2)}, u32[]{:S(2)}) async-start(s32[2,1,1024]{2,1,0:T(1,128)} %reshape.532), calls=%async_computation.1 | async-start | bytes 16384 | tf_op jit(solution)/shard_map/all_to_all | solution.py:866
  113.6 26.5 %all-to-all-start.2 = ((bf16[16,2,64,192]{3,2,1,0:T(8,128)(2,1)}), bf16[16,2,64,192]{3,2,1,0:T(8,128)(2,1)S(1)}, u32[]{:S(2)}, u32[]{:S(2)}) async-start(bf16[16,2,64,192]{3,2,1,0:T(8,128)(2,1)} %select_select_fusion), calls=%async_computation.2 | async-start | bytes 2097152 | tf_op jit(solution)/shard_map/all_to_all | solution.py:883
  141.2 29.1 %all-to-all-start.3 = ((bf16[16,2,64,192]{3,2,0,1:T(8,128)(2,1)}), bf16[16,2,64,192]{3,2,0,1:T(8,128)(2,1)}, u32[]{:S(2)}, u32[]{:S(2)}) async-start(bf16[16,2,64,192]{3,2,0,1:T(8,128)(2,1)} %copy.148), calls=%async_computation.3 | async-start | bytes 2097152 | tf_op jit(solution)/shard_map/all_to_all | solution.py:882
  145.6 575.0 %reduce-scatter.13.cloned.1.call-start = ((), (), s32[]{:S(2)}) async-start(), calls=%async_computation.21 | async-start | bytes 884736 | tf_op jit(solution)/shard_map/reduce_scatter | solution.py:1046
  566.1 200.8 %reduce-scatter.25.cloned.1.call-start = ((), (), s32[]{:S(2)}) async-start(), calls=%async_computation.27 | async-start | bytes 1769472
  569.6 198.7 %reduce-scatter.27.cloned.1.call-start = ((), (), s32[]{:S(2)}) async-start(), calls=%async_computation.28 | async-start | bytes 1769472
  575.1 194.6 %reduce-scatter.15.cloned.1.call-start = ((), (), s32[]{:S(2)}) async-start(), calls=%async_computation.22 | async-start | bytes 1769472 | tf_op jit(solution)/shard_map/reduce_scatter | solution.py:1052
  578.3 191.4 %reduce-scatter.17.cloned.1.call-start = ((), (), s32[]{:S(2)}) async-start(), calls=%async_computation.23 | async-start | bytes 1769472 | tf_op jit(solution)/shard_map/reduce_scatter | solution.py:1061
  581.9 187.8 %reduce-scatter.23.cloned.1.call-start = ((), (), s32[]{:S(2)}) async-start(), calls=%async_computation.26 | async-start | bytes 4718592 | tf_op jit(solution)/shard_map/reduce_scatter | solution.py:1073
  586.6 211.5 %reduce-scatter.21.cloned.1.call-start = ((), (), s32[]{:S(2)}) async-start(), calls=%async_computation.25 | async-start | bytes 4718592 | tf_op jit(solution)/shard_map/reduce_scatter | solution.py:1070
  591.9 252.3 %reduce-scatter.19.cloned.1.call-start = ((), (), s32[]{:S(2)}) async-start(), calls=%async_computation.24 | async-start | bytes 4718592 | tf_op jit(solution)/shard_map/reduce_scatter | solution.py:1067
  649.3 71.3 %all-to-all-start.5 = ((bf16[16,2,64,192]{3,2,0,1:T(8,128)(2,1)}), bf16[16,2,64,192]{3,2,0,1:T(8,128)(2,1)S(1)}, u32[]{:S(2)}, u32[]{:S(2)}) async-start(bf16[16,2,64,192]{3,2,0,1:T(8,128)(2,1)} %copy.159), calls=%async_computation.5 | async-start | bytes 2097152 | tf_op jit(solution)/shard_map/all_to_all | solution.py:1024
  (28 other events, 85.1 us)
Sparse Core Ops, SparseCore 0:
  10.1 25.5 all-gather.13
  37.2 25.4 all-gather.17
  64.8 23.2 all-gather.11
  90.1 22.7 all-gather.15
  114.3 54.7 all-gather.21
  170.5 44.6 all-gather.19
  216.7 44.8 all-gather.23
  566.2 28.9 reduce-scatter.12
  598.1 21.8 reduce-scatter.24
  622.6 21.8 reduce-scatter.26
  647.3 33.2 reduce-scatter.14
  683.3 22.0 reduce-scatter.16
  708.3 43.5 reduce-scatter.22
  754.6 43.4 reduce-scatter.20
  800.7 43.4 reduce-scatter.18

commit v2 on v1

--- a/solution.py
+++ b/solution.py
@@ -57,6 +57,82 @@
         scaled - unit_rows * jnp.mean(scaled * unit_rows, axis=-1, keepdims=True)
     )
     return (back_rows, jnp.sum(gradient * unit_rows, axis=0))
+
+
+def exchange_kernel(seq_count, shard_count, shared, *refs):
+    count = len(shared)
+    srcs, dsts = refs[:count], refs[count : 2 * count]
+    send_sem, recv_sem, local_sem = refs[2 * count :]
+    total = seq_count * shard_count
+    me = lax.axis_index("seq") * shard_count + lax.axis_index("shard")
+    barrier = pltpu.get_barrier_semaphore()
+
+    def place(target):
+        return {"seq": target // shard_count, "shard": target % shard_count}
+
+    def greet(step, carry):
+        pl.semaphore_signal(
+            barrier,
+            inc=1,
+            device_id=place(lax.rem(me + step, total)),
+            device_id_type=pl.DeviceIdType.MESH,
+        )
+        return carry
+
+    lax.fori_loop(1, total, greet, 0)
+    local = []
+    for p in range(count):
+        own = srcs[p] if shared[p] else srcs[p].at[me]
+        local.append(pltpu.make_async_copy(own, dsts[p].at[me], local_sem.at[p]))
+        local[p].start()
+    pl.semaphore_wait(barrier, total - 1)
+
+    def send(step, carry):
+        target = lax.rem(me + step, total)
+        for p in range(count):
+            pltpu.make_async_remote_copy(
+                src_ref=srcs[p] if shared[p] else srcs[p].at[target],
+                dst_ref=dsts[p].at[me],
+                send_sem=send_sem.at[p],
+                recv_sem=recv_sem.at[p],
+                device_id=place(target),
+                device_id_type=pl.DeviceIdType.MESH,
+            ).start()
+        return carry
+
+    lax.fori_loop(1, total, send, 0)
+    for p in range(count):
+        local[p].wait()
+        others = dsts[p].at[pl.ds(0, total - 1)]
+        every = pltpu.make_async_remote_copy(
+            src_ref=others,
+            dst_ref=others,
+            send_sem=send_sem.at[p],
+            recv_sem=recv_sem.at[p],
+            device_id=place(lax.rem(me + 1, total)),
+            device_id_type=pl.DeviceIdType.MESH,
+        )
+        every.wait_recv()
+        every.wait_send()
+
+
+def exchange(payloads, shared, collective_id, name):
+    seq_count = lax.axis_size("seq")
+    shard_count = lax.axis_size("shard")
+    total = seq_count * shard_count
+    shapes = [
+        jax.ShapeDtypeStruct((total,) + (p.shape if whole_one else p.shape[1:]), p.dtype)
+        for p, whole_one in zip(payloads, shared)
+    ]
+    return pl.pallas_call(
+        functools.partial(exchange_kernel, seq_count, shard_count, shared),
+        out_shape=shapes,
+        in_specs=[pl.BlockSpec(memory_space=pltpu.VMEM)] * len(payloads),
+        out_specs=[pl.BlockSpec(memory_space=pltpu.VMEM)] * len(payloads),
+        scratch_shapes=[pltpu.SemaphoreType.DMA((len(payloads),))] * 3,
+        compiler_params=pltpu.CompilerParams(collective_id=collective_id, has_side_effects=True),
+        name=name,
+    )(*payloads)
 
 
 CHUNKS = 2
@@ -549,6 +625,9 @@
         ),
         compiler_params=pltpu.CompilerParams(
             dimension_semantics=("arbitrary",), vmem_limit_bytes=VMEM_BIG
+        ),
+        cost_estimate=pl.CostEstimate(
+            flops=70_000_000_000, bytes_accessed=10_000_000, transcendentals=0
         ),
         name="attention_forward",
     )(slots, valid, own, blocks, wq, wk, wv, *tables, key_features, query_features)
@@ -752,6 +831,9 @@
         compiler_params=pltpu.CompilerParams(
             dimension_semantics=("arbitrary",), vmem_limit_bytes=VMEM_BIG
         ),
+        cost_estimate=pl.CostEstimate(
+            flops=120_000_000_000, bytes_accessed=20_000_000, transcendentals=0
+        ),
         name="attention_backward",
     )(
         slots, valid, own, blocks, wq, wk, wkt, wv, *tables, ct, st, key_features,
@@ -794,6 +876,42 @@
 def from_padded_rows(grouped):
     split = grouped.reshape(GROUPS, 256, grouped.shape[1])[:, : GROUP * HEAD_DIM]
     return split.reshape(HEADS * HEAD_DIM, grouped.shape[1])
+
+
+def rows_each(rows, seq_count):
+    return -(-rows // seq_count)
+
+
+def lay_rows(grads, seq_count, shard_count):
+    laid = []
+    for grad in grads:
+        width = grad.shape[1]
+        own = grad.shape[0] // shard_count
+        each = rows_each(own, seq_count)
+        block = grad.reshape(shard_count, own, width)
+        block = jnp.pad(block, ((0, 0), (0, seq_count * each - own), (0, 0)))
+        laid.append(block.reshape(shard_count, seq_count, each, width).transpose(1, 0, 2, 3))
+    return laid[0] if len(laid) == 1 else jnp.concatenate(laid, axis=2)
+
+
+def sum_share(block):
+    seq_count, shard_count, rows, width = block.shape
+    part = block.reshape(seq_count * shard_count * rows, width)
+    part = lax.psum_scatter(part, "seq", scatter_dimension=0, tiled=True)
+    part = lax.psum_scatter(part, "shard", scatter_dimension=0, tiled=True)
+    whole_part = lax.all_gather(part, "seq", axis=0, tiled=True)
+    return whole_part.reshape(seq_count, rows, width)
+
+
+def take_rows(share, sizes):
+    seq_count, _, width = share.shape
+    start, taken = 0, []
+    for own in sizes:
+        each = rows_each(own, seq_count)
+        rows = share[:, start : start + each].reshape(seq_count * each, width)[:own]
+        taken.append(rows.astype(F32))
+        start += each
+    return taken
 
 
 def shards(
@@ -863,35 +981,22 @@
     rank_index = jnp.sum(before * one_hot, axis=1).astype(jnp.int32)
     slot_index = flat_owner * capacity + rank_index
     request = jnp.full((owner_count * capacity,), -1, jnp.int32).at[slot_index].set(flat_row)
-    asked_rows = lax.all_to_all(
-        lax.all_to_all(
-            request.reshape(seq_count, shard_count, capacity),
-            "seq",
-            split_axis=0,
-            concat_axis=0,
-            tiled=True,
-        ),
-        "shard",
-        split_axis=1,
-        concat_axis=1,
-        tiled=True,
-    )
+    doc_rows = -(-tokens // 128)
+    slab = jnp.concatenate(
+        [
+            jnp.pad(request.reshape(owner_count, 1, capacity), ((0, 0), (0, 0), (0, 128 - capacity))),
+            jnp.broadcast_to(doc_ids.reshape(1, doc_rows, 128), (owner_count, doc_rows, 128)),
+        ],
+        axis=1,
+    )
+    (slabs,) = exchange((slab,), (False,), 3, "ask")
+    asked_rows = slabs[:, 0, :capacity]
+    docs_of = slabs[:, 1:].reshape(seq_count, shard_count, tokens)
+    all_docs = lax.dynamic_index_in_dim(docs_of, lax.axis_index("shard"), 1, keepdims=False)
     present = asked_rows >= 0
     found_rows = jnp.take(table, jnp.maximum(asked_rows, 0).reshape(-1), axis=0)
     found_rows = jnp.where(present.reshape(-1)[:, None], found_rows, jnp.zeros_like(found_rows))
-    answer = lax.all_to_all(
-        lax.all_to_all(
-            found_rows.reshape(seq_count, shard_count, capacity, -1),
-            "seq",
-            split_axis=0,
-            concat_axis=0,
-            tiled=True,
-        ),
-        "shard",
-        split_axis=1,
-        concat_axis=1,
-        tiled=True,
-    )
+    (answer,) = exchange((found_rows.reshape(owner_count, capacity, -1),), (False,), 4, "answer")
     picked = jnp.take(answer.reshape(owner_count * capacity, -1), slot_index, axis=0).reshape(
         tokens, -1
     )
@@ -908,7 +1013,6 @@
     valid = (sources >= 0).astype(jnp.int32)
     levels = my_index // 4 - sources // 4
     slots = jnp.where(sources >= 0, levels * 4 + sources % 4, SLOTS)
-    all_docs = lax.all_gather(doc_ids[0], "seq", axis=0)
     step_docs = jnp.take(all_docs, jnp.maximum(sources, 0), axis=0)
     lane = jnp.arange(128, dtype=jnp.int32)
     doc_lane = (lane >= DOC_LANE) & (lane < DOC_LANE + DOC_FEATURES)
@@ -954,14 +1058,10 @@
     feed_out = jnp.dot(hidden, full_down, preferred_element_type=jnp.float32)
     result = middle + feed_out
     mixed = result.astype(jnp.bfloat16)[None]
-    energies = lax.psum(
-        (jnp.sum(stream * stream), jnp.sum(mixer_out * mixer_out), jnp.sum(feed_out * feed_out)),
-        ("seq", "shard"),
-    )
-    entry_count = owner_count * tokens * stream.shape[1]
-    stream_rms = jnp.sqrt(energies[0] / entry_count)
-    mixer_rms = jnp.sqrt(energies[1] / entry_count)
-    feed_rms = jnp.sqrt(energies[2] / entry_count)
+    energy = jnp.stack(
+        [jnp.sum(stream * stream), jnp.sum(mixer_out * mixer_out), jnp.sum(feed_out * feed_out)]
+    )
+    energy = jnp.broadcast_to(jnp.pad(energy, (0, 5))[:, None], (8, 128))
     grad_result = cotangent[0].astype(jnp.float32)
     grad_feed = cotangent[0]
     grad_down = jnp.einsum("tf,td->fd", hidden, grad_feed, preferred_element_type=jnp.float32)
@@ -984,6 +1084,11 @@
     grad_heads = jnp.einsum(
         "td,ed->te", grad_mixer, out_rows, preferred_element_type=jnp.float32
     ).astype(jnp.bfloat16)
+    early = lay_rows(
+        (jnp.concatenate([grad_gate, grad_up], axis=1).astype(BF16),), seq_count, shard_count
+    ), lay_rows((grad_down.astype(BF16), grad_out.astype(BF16)), seq_count, shard_count)
+    grad_heads, early = lax.optimization_barrier((grad_heads, early))
+    early_shares = [sum_share(block) for block in early]
     parts, grad_query_turned, grad_key_groups, grad_value_groups = attention_backward(
         mixer_in,
         blocks,
@@ -1021,19 +1126,14 @@
         .at[slot_index]
         .set(grad_picked)
     )
-    incoming = lax.all_to_all(
-        lax.all_to_all(
-            outgoing.reshape(seq_count, shard_count, capacity, -1),
-            "seq",
-            split_axis=0,
-            concat_axis=0,
-            tiled=True,
-        ),
-        "shard",
-        split_axis=1,
-        concat_axis=1,
-        tiled=True,
-    )
+    incoming, energy_parts = exchange(
+        (outgoing.reshape(owner_count, capacity, -1), energy), (False, True), 5, "give_back"
+    )
+    energies = jnp.sum(energy_parts[:, :, 0], axis=0)
+    entry_count = owner_count * tokens * stream.shape[1]
+    stream_rms = jnp.sqrt(energies[0] / entry_count)
+    mixer_rms = jnp.sqrt(energies[1] / entry_count)
+    feed_rms = jnp.sqrt(energies[2] / entry_count)
     incoming = (
         jnp.where(present[..., None], incoming, jnp.zeros_like(incoming))
         .reshape(owner_count * capacity, -1)
@@ -1042,57 +1142,38 @@
     grad_table = (
         jnp.zeros(table.shape, jnp.float32).at[jnp.maximum(asked_rows, 0).reshape(-1)].add(incoming)
     )
-    shares = (
-        lax.psum_scatter(
-            grad_ngram.astype(jnp.bfloat16), "shard", scatter_dimension=0, tiled=True
-        ).astype(jnp.float32),
-        lax.psum_scatter(
-            grad_stream_gain.astype(jnp.bfloat16), "shard", scatter_dimension=0, tiled=True
-        ).astype(jnp.float32),
-        lax.psum_scatter(
-            grad_query.astype(jnp.bfloat16), "shard", scatter_dimension=0, tiled=True
-        ).astype(jnp.float32),
-        lax.psum_scatter(
-            grad_key.astype(jnp.bfloat16), "shard", scatter_dimension=0, tiled=True
-        ).astype(jnp.float32),
-        lax.psum_scatter(
-            grad_value.astype(jnp.bfloat16), "shard", scatter_dimension=0, tiled=True
-        ).astype(jnp.float32),
-        lax.psum_scatter(
-            grad_out.astype(jnp.bfloat16), "shard", scatter_dimension=0, tiled=True
-        ).astype(jnp.float32),
-        lax.psum_scatter(
-            grad_mixer_gain.astype(jnp.bfloat16), "shard", scatter_dimension=0, tiled=True
-        ).astype(jnp.float32),
-        lax.psum_scatter(
-            grad_gate.astype(jnp.bfloat16), "shard", scatter_dimension=0, tiled=True
-        ).astype(jnp.float32),
-        lax.psum_scatter(
-            grad_up.astype(jnp.bfloat16), "shard", scatter_dimension=0, tiled=True
-        ).astype(jnp.float32),
-        lax.psum_scatter(
-            grad_down.astype(jnp.bfloat16), "shard", scatter_dimension=0, tiled=True
-        ).astype(jnp.float32),
-        lax.psum_scatter(
-            grad_feed_gain.astype(jnp.bfloat16), "shard", scatter_dimension=0, tiled=True
-        ).astype(jnp.float32),
-    )
-    totals = lax.psum(
-        (
-            shares[0],
-            shares[1],
-            shares[2],
-            shares[3],
-            shares[4],
-            shares[5],
-            shares[6],
-            shares[7],
-            shares[8],
-            shares[9],
-            shares[10],
-        ),
-        "seq",
-    )
+    share_width = stream_gain.shape[0]
+    gains = jnp.stack([grad_stream_gain, grad_mixer_gain, grad_feed_gain])
+    gains = gains.reshape(3, shard_count, 1, share_width)
+    gains = jnp.pad(
+        gains, ((0, seq_count - 3), (0, 0), (0, 0), (0, stream.shape[1] - share_width))
+    ).astype(BF16)
+    late = jnp.concatenate(
+        [
+            lay_rows(
+                (
+                    grad_query.astype(BF16),
+                    grad_key.astype(BF16),
+                    grad_value.astype(BF16),
+                    grad_ngram.astype(BF16),
+                ),
+                seq_count,
+                shard_count,
+            ),
+            gains,
+        ],
+        axis=2,
+    )
+    gain_row = late.shape[2] - 1
+    late = jnp.pad(late, ((0, 0), (0, 0), (0, -late.shape[2] % 16), (0, 0)))
+    late_share = sum_share(late)
+    wide = stream.shape[1] // shard_count
+    total_gate_up = take_rows(early_shares[0], (wide,))[0]
+    total_down, total_out = take_rows(early_shares[1], (down_weight.shape[0], wide))
+    total_query, total_key, total_value, total_ngram = take_rows(
+        late_share, (wide, wide, wide, ngram_weight.shape[0])
+    )
+    total_gains = late_share[:3, gain_row, :share_width].astype(F32)
     return (
         mixed,
         grad_input,
@@ -1100,17 +1181,17 @@
         mixer_rms,
         feed_rms,
         grad_table,
-        totals[0],
-        totals[1],
-        totals[2],
-        totals[3],
-        totals[4],
-        totals[5],
-        totals[6],
-        totals[7],
-        totals[8],
-        totals[9],
-        totals[10],
+        total_ngram,
+        total_gains[0],
+        total_query,
+        total_key,
+        total_value,
+        total_out,
+        total_gains[1],
+        total_gate_up[:, : gate_weight.shape[1]],
+        total_gate_up[:, gate_weight.shape[1] :],
+        total_down,
+        total_gains[2],
     )
 
 

time: 1180 us -> 1020 us (0.86)
  blocking collectives: 465 us -> 26.9 us
  waiting for transfers between devices: 126 us -> 315 us
  local copies, waits for them, and re-layouts: 117 us -> 171 us
  Pallas kernels: 317 us -> 358 us
  other arithmetic: 38.2 us -> 63.1 us
  starting transfers between devices: 24.2 us -> 0.88 us
    psum x2 -> x0, blocking collectives: 368 us -> none  [the longest x1 309 us: shards(): lax.psum((shares[0], shares[1], shares[2], shares[3], shares[4], shares[5...]
    reduce_scatter x6, waiting for transfers between devices: 74.5 us -> 215 us  [the longest x3 173 us: sum_share(): part = lax.psum_scatter(part, 'seq', scatter_dimension=0, tiled=True)]
    pallas_call x0 -> x3, Pallas kernels: none -> 63.1 us  [exchange(): pl.pallas_call(functools.partial(exchange_kernel, seq_count, shard_count,...]
    all_gather x0 -> x3, waiting for transfers between devices: none -> 46.9 us  [sum_share(): whole_part = lax.all_gather(part, 'seq', axis=0, tiled=True)]
    all_to_all x1 -> x0, blocking collectives: 43.7 us -> none  [shards(): lax.all_to_all(outgoing.reshape(seq_count, shard_count, capacity, -1), 's...]
    pallas_call x1, Pallas kernels: 244 us -> 218 us  [halo_reduce(): pl.pallas_call(functools.partial(reduce_kernel, group_count), out_shape=j...]
    all_to_all x5 -> x0, waiting for transfers between devices: 25.7 us -> none  [the longest x1 17.1 us: shards(): lax.all_to_all(found_rows.reshape(seq_count, shard_count, capacity, -1),...]
    all_to_all x5 -> x0, starting transfers between devices: 22.9 us -> none  [the longest x1 7.38 us: shards(): lax.all_to_all(request.reshape(seq_count, shard_count, capacity), 'seq',...]
  transfers between devices with their start and end apart: 20 -> 16, of which waited for: 5 -> 9; matrix products, arithmetic and copies ran while one was open for 15% -> 23% of each run, Pallas kernels for 3% -> 36%
where the time goes in v2:
time: 1020 us; the launch traced here: 1010 us
  Pallas kernels  358 us (35%)
  waiting for transfers between devices  315 us (31%)
  local copies, waits for them, and re-layouts  171 us (17%)
  other arithmetic  63.1 us (6%)
  matrix products  49.8 us (5%)
  blocking collectives  26.9 us (3%)
  between operations  20.9 us (2%)
    pallas_call x1, Pallas kernels, halo_reduce(): pl.pallas_call(functools.partial(reduce_kernel, group_count), out_shape=j...  218 us
    reduce_scatter x3, waiting for transfers between devices, sum_share(): part = lax.psum_scatter(part, 'seq', scatter_dimension=0, tiled=True)  173 us
    pallas_call x3, Pallas kernels, exchange(): pl.pallas_call(functools.partial(exchange_kernel, seq_count, shard_count,...  63.1 us
    unnamed x107, local copies, waits for them, and re-layouts  51.8 us
    all_gather x3, waiting for transfers between devices, sum_share(): whole_part = lax.all_gather(part, 'seq', axis=0, tiled=True)  46.9 us
    reduce_scatter x3, waiting for transfers between devices, sum_share(): part = lax.psum_scatter(part, 'shard', scatter_dimension=0, tiled=True)  42.5 us
    all_gather x1, waiting for transfers between devices, shards(): lax.all_gather(down_weight, 'shard', axis=0, tiled=True)  40.8 us
    pallas_call x1, Pallas kernels, attention_backward(): pl.pallas_call(backward_kernel, out_shape=(jax.ShapeDtypeStruct((SLOTS +...  32.7 us
  transfers between devices with their start and end apart: 16, of which 9 were waited for; matrix products, arithmetic and copies ran while one was open for 23% of the time, Pallas kernels for 36%

profile of v2, /device:TPU:0, one launch (start us, length us, event | category | flops | bytes accessed | tf_op | source)
XLA Modules:
  0.0 1005.8 jit_solution(3503866551583229075)
XLA Ops:
  21.7 11.2 %ask.1 = s32[32,5,128]{2,1,0:T(8,128)} custom-call(s32[32,5,128]{2,1,0:T(8,128)} %pad_add_fusion.refs_0_), custom_call_target="tpu_custom_call" | custom-call | tf_op jit(solution)/shard_map/ask/pallas_call | solution.py:127
  53.9 13.7 %all_gather.42 = bf16[384,768]{1,0:T(8,128)(2,1)S(1)} all-gather(bf16[192,768]{1,0:T(8,128)(2,1)S(1)} %copy-done.22), channel_id=1, replica_groups=mesh['seq'=16,'shard'=2] {'shard'}, dimensions={0}, use_global_device_ids=true | all-gather | bytes 884736 | tf_op jit(solution)/shard_map/all_gather | solution.py:943
  67.5 15.1 %copy.121 = bf16[25000,192]{1,0:T(8,128)(2,1)} copy(bf16[25000,192]{0,1:T(8,128)(2,1)} %param.21) | data formatting | bytes 19200000 | tf_op args[4]
  82.6 12.9 %gather_fusion = bf16[2048,192]{1,0:T(8,128)(2,1)S(1)} fusion(bf16[25000,192]{1,0:T(8,128)(2,1)} %copy.121, s32[2048]{0:T(1024)S(1)} %broadcast_clamp_fusion), kind=kCustom, calls=%fused_computation | custom fusion | bytes 1581056 | tf_op jit(solution)/shard_map/jit(_take)/gather | solution.py:997
  97.1 23.9 %answer.1 = bf16[32,64,192]{2,1,0:T(8,128)(2,1)} custom-call(bf16[32,64,192]{2,1,0:T(8,128)(2,1)} %select_select_fusion.refs_0_), custom_call_target="tpu_custom_call" | custom-call | tf_op jit(solution)/shard_map/answer/pallas_call | solution.py:127
  129.3 24.3 %halo_gather.1.x_ref = bf16[13,512,768]{2,1,0:T(8,128)(2,1)} custom-call(bf16[512,768]{1,0:T(8,128)(2,1)} %multiply_convert_fusion.4.own_ref), custom_call_target="tpu_custom_call" | custom-call | tf_op jit(solution)/shard_map/halo_gather/pallas_call | solution.py:295
  171.4 20.2 %attention_forward.1 = (f32[512,1024]{1,0:T(8,128)}, f32[512,128]{1,0:T(8,128)}) custom-call(s32[9]{0:T(128)} %compare_select_fusion.6.slot_ref, s32[9]{0:T(128)} %compare_convert_fusion.valid_ref, bf16[512,768]{1,0:T(8,128)(2,1)} %multiply_convert_fusion.4.own_ref, bf16[13,512,768]{2,1,0:T(8,128)(2,1)} %halo_gather.1.x_ref, ...), custom_call_target="tpu_custom_call" | custom-call | flops 70000001024 | bytes 10000000 | tf_op jit(solution)/shard_map/attention_forward/pallas_call | solution.py:595
  209.2 9.4 all-gather.22.cloned.1.call-done
  224.2 40.8 %all-gather.26.cloned.1.call-done = bf16[2048,768]{1,0:T(8,128)(2,1)} async-done(((bf16[1024,768]{1,0:T(8,128)(2,1)}), bf16[2048,768]{1,0:T(8,128)(2,1)}) %all-gather.26.cloned.1.call-update) | async-done | bytes 3145744 | tf_op jit(solution)/shard_map/all_gather | solution.py:952
  301.3 32.7 %attention_backward.1 = (bf16[13,512,768]{2,1,0:T(8,128)(2,1)}, bf16[768,512]{1,0:T(8,128)(2,1)}, bf16[4,768,256]{2,1,0:T(8,128)(2,1)}, bf16[4,768,256]{2,1,0:T(8,128)(2,1)}) custom-call(s32[9]{0:T(128)} %compare_select_fusion.6.slot_ref, s32[9]{0:T(128)} %compare_convert_fusion.valid_ref, bf16[512,768]{1,0:T(8,128)(2,1)} %multiply_convert_fusion.4.own_ref, ...), custom_call_target="tpu_custom_call" | custom-call | flops 120000004096 | bytes 20000000 | tf_op jit(solution)/shard_map/attention_backward/pallas_call | solution.py:781
  334.1 218.0 %halo_reduce.1 = f32[512,768]{1,0:T(8,128)} custom-call(bf16[13,512,768]{2,1,0:T(8,128)(2,1)} %get-tuple-element.31.part_ref), custom_call_target="tpu_custom_call" | custom-call | tf_op jit(solution)/shard_map/halo_reduce/pallas_call | solution.py:454
  570.7 11.4 %copy.134 = bf16[768,4,3,2,32]{4,3,2,1,0:T(2,128)(2,1)} copy(bf16[768,4,3,2,32]{0,4,2,3,1:T(8,128)(2,1)} %bitcast.156) | data formatting | bytes 2359296 | tf_op jit(solution)/shard_map/transpose | solution.py:855
  582.2 12.2 %reshape.544 = bf16[2,16,24,768]{3,2,1,0:T(8,128)(2,1)S(1)} reshape(bf16[768,4,3,2,32]{4,3,2,1,0:T(2,128)(2,1)} %copy.134) | data formatting | bytes 2359296 | tf_op jit(solution)/shard_map/reshape | solution.py:893
  597.6 17.3 %concatenate.29 = bf16[16,2,85,768]{3,2,0,1:T(8,128)(2,1)} concatenate(bf16[16,2,24,768]{3,2,0,1:T(8,128)(2,1)} %bitcast.172, bf16[16,2,24,768]{3,2,0,1:T(8,128)(2,1)S(1)} %bitcast.151, bf16[16,2,24,768]{3,2,0,1:T(8,128)(2,1)S(1)} %bitcast.150, bf16[16,2,12,768]{3,2,0,1:T(8,128)(2,1)S(1)} %bitcast.162, bf16[16,2,1,768]{3,2,0,1:T(2,128)(2,1)S(1)} %select_maximum_fusion), dimensions={2} | concatenate | bytes 8355840 | tf_op jit(solution)/shard_map/concatenate | solution.py:1151
  627.3 83.9 %reduce-scatter.7.cloned.1.call-done = bf16[192,768]{1,0:T(8,128)(2,1)} async-done(((bf16[3072,768]{1,0:T(8,128)(2,1)}), bf16[192,768]{1,0:T(8,128)(2,1)}) %reduce-scatter.7.cloned.1.call-update) | async-done | bytes 294928 | tf_op jit(solution)/shard_map/reduce_scatter | solution.py:900
  711.3 88.6 %reduce-scatter.15.cloned.1.call-done = bf16[48,4096]{1,0:T(8,128)(2,1)} async-done(((bf16[768,4096]{1,0:T(8,128)(2,1)}), bf16[48,4096]{1,0:T(8,128)(2,1)}) %reduce-scatter.15.cloned.1.call-update) | async-done | bytes 393232 | tf_op jit(solution)/shard_map/reduce_scatter | solution.py:900
  799.9 13.1 %reduce-scatter.13.cloned.1.call-done = bf16[88,768]{1,0:T(8,128)(2,1)} async-done(((bf16[176,768]{1,0:T(8,128)(2,1)}), bf16[88,768]{1,0:T(8,128)(2,1)}) %reduce-scatter.13.cloned.1.call-update) | async-done | bytes 135184 | tf_op jit(solution)/shard_map/reduce_scatter | solution.py:901
  813.1 14.2 %reduce-scatter.9.cloned.1.call-done = bf16[96,768]{1,0:T(8,128)(2,1)} async-done(((bf16[192,768]{1,0:T(8,128)(2,1)}), bf16[96,768]{1,0:T(8,128)(2,1)}) %reduce-scatter.9.cloned.1.call-update) | async-done | bytes 147472 | tf_op jit(solution)/shard_map/reduce_scatter | solution.py:901
  827.6 15.2 %reduce-scatter.17.cloned.1.call-done = bf16[24,4096]{1,0:T(8,128)(2,1)} async-done(((bf16[48,4096]{1,0:T(8,128)(2,1)}), bf16[24,4096]{1,0:T(8,128)(2,1)}) %reduce-scatter.17.cloned.1.call-update) | async-done | bytes 196624 | tf_op jit(solution)/shard_map/reduce_scatter | solution.py:901
  852.6 28.0 %give_back.1 = (bf16[32,64,192]{2,1,0:T(8,128)(2,1)}, f32[32,8,128]{2,1,0:T(8,128)}) custom-call(bf16[32,64,192]{2,1,0:T(8,128)(2,1)} %bitcast.159, f32[8,128]{1,0:T(8,128)} %broadcast_in_dim.139.refs_1_), custom_call_target="tpu_custom_call" | custom-call | tf_op jit(solution)/shard_map/give_back/pallas_call | solution.py:127
  885.8 21.8 %scatter_custom_fusion.2 = f32[25000,192]{1,0:T(8,128)} fusion(s32[2048]{0:T(1024)} %copy-done.34, f32[]{:T(128)} %constant.131.clone.1, bf16[2048,192]{1,0:T(8,128)(2,1)S(1)} %bitcast.158), kind=kCustom, calls=%fused_computation.6 | custom fusion | flops 786432 | bytes 19986944 | tf_op jit(solution)/shard_map/scatter-add | solution.py:1143
  907.7 23.4 %copy.141 = f32[25000,192]{0,1:T(8,128)} copy(f32[25000,192]{1,0:T(8,128)} %scatter_custom_fusion.2) | data formatting | bytes 38400000
  936.8 6.8 all-gather.28.cloned.1.call-done
  949.9 40.1 %all-gather.32.cloned.1.call-done = bf16[384,4096]{1,0:T(8,128)(2,1)} async-done(((bf16[24,4096]{1,0:T(8,128)(2,1)}), bf16[384,4096]{1,0:T(8,128)(2,1)}) %all-gather.32.cloned.1.call-update) | async-done | bytes 3145744 | tf_op jit(solution)/shard_map/all_gather | solution.py:902
  (276 shorter events, 186.9 us)
Async XLA Ops:
  7.2 151.3 %all-gather.16.cloned.1.call-start = ((), (), s32[]{:S(2)}) async-start(), calls=%async_computation.7 | async-start | bytes 1769472 | tf_op jit(solution)/shard_map/all_gather | solution.py:946
  9.5 154.2 %all-gather.14.cloned.1.call-start = ((), (), s32[]{:S(2)}) async-start(), calls=%async_computation.6 | async-start | bytes 1769472 | tf_op jit(solution)/shard_map/all_gather | solution.py:945
  10.6 158.3 %all-gather.18.cloned.1.call-start = ((), (), s32[]{:S(2)}) async-start(), calls=%async_computation.8 | async-start | bytes 1769472 | tf_op jit(solution)/shard_map/all_gather | solution.py:947
  11.8 179.8 %all-gather.20.cloned.1.call-start = ((), (), s32[]{:S(2)}) async-start(), calls=%async_computation.9 | async-start | bytes 1769472 | tf_op jit(solution)/shard_map/all_gather | solution.py:948
  12.3 191.1 %all-gather.24.cloned.1.call-start = ((), (), s32[]{:S(2)}) async-start(), calls=%async_computation.11 | async-start | bytes 4718592 | tf_op jit(solution)/shard_map/all_gather | solution.py:951
  12.9 205.6 %all-gather.22.cloned.1.call-start = ((), (), s32[]{:S(2)}) async-start(), calls=%async_computation.10 | async-start | bytes 4718592 | tf_op jit(solution)/shard_map/all_gather | solution.py:950
  13.5 251.5 %all-gather.26.cloned.1.call-start = ((), (), s32[]{:S(2)}) async-start(), calls=%async_computation.12 | async-start | bytes 4718592 | tf_op jit(solution)/shard_map/all_gather | solution.py:952
  14.3 612.3 %reduce-scatter.11.cloned.1.call-start = ((), (), s32[]{:S(2)}) async-start(), calls=%async_computation.16 | async-start | bytes 4595712 | tf_op jit(solution)/shard_map/reduce_scatter | solution.py:900
  301.3 409.9 %reduce-scatter.7.cloned.1.call-start = ((), (), s32[]{:S(2)}) async-start(), calls=%async_computation.13 | async-start | bytes 5013504 | tf_op jit(solution)/shard_map/reduce_scatter | solution.py:900
  334.1 218.1 %copy-start.1 = (f32[512,768]{1,0:T(8,128)S(1)}, f32[512,768]{1,0:T(8,128)}, u32[]{:S(2)}) copy-start(f32[512,768]{1,0:T(8,128)} %copy-done) | copy-start | bytes 4718596
  334.1 218.1 %copy-start.18 = (bf16[768,768]{0,1:T(8,128)(2,1)S(1)}, bf16[768,768]{0,1:T(8,128)(2,1)}, u32[]{:S(2)}) copy-start(bf16[768,768]{0,1:T(8,128)(2,1)} %all-gather.14.cloned.1.call-done) | copy-start | bytes 3538948
  334.1 218.1 %copy-start.26 = (f32[768]{0:T(1024)S(1)}, f32[768]{0:T(1024)}, u32[]{:S(2)}) copy-start(f32[768]{0:T(1024)} %copy-done.25) | copy-start | bytes 9220
  334.1 218.1 %copy-start.28 = (f32[512]{0:T(512)S(1)}, f32[512]{0:T(512)}, u32[]{:S(2)}) copy-start(f32[512]{0:T(512)} %copy-done.27) | copy-start | bytes 6148
  334.1 218.1 %copy-start.32 = (f32[768]{0:T(1024)S(1)}, f32[768]{0:T(1024)}, u32[]{:S(2)}) copy-start(f32[768]{0:T(1024)} %copy-done.31) | copy-start | bytes 9220
  334.1 218.1 %copy-start.36 = (f32[512]{0:T(512)S(1)}, f32[512]{0:T(512)}, u32[]{:S(2)}) copy-start(f32[512]{0:T(512)} %copy-done.35) | copy-start | bytes 6148
  620.1 179.7 %reduce-scatter.15.cloned.1.call-start = ((), (), s32[]{:S(2)}) async-start(), calls=%async_computation.19 | async-start | bytes 6684672 | tf_op jit(solution)/shard_map/reduce_scatter | solution.py:900
  626.5 216.4 %copy-start.3 = (f32[512,768]{1,0:T(8,128)S(1)}, f32[512,768]{1,0:T(8,128)}, u32[]{:S(2)}) copy-start(f32[512,768]{1,0:T(8,128)} %copy-done.2) | copy-start | bytes 4718596
  626.5 216.3 %copy-start.11 = (bf16[384,768]{1,0:T(8,128)(2,1)S(1)}, bf16[384,768]{1,0:T(8,128)(2,1)}, u32[]{:S(2)}) copy-start(bf16[384,768]{1,0:T(8,128)(2,1)} %copy-done.10) | copy-start | bytes 1769476
  626.5 186.6 %reduce-scatter.13.cloned.1.call-start = ((), (), s32[]{:S(2)}) async-start(), calls=%async_computation.17 | async-start | bytes 405504 | tf_op jit(solution)/shard_map/reduce_scatter | solution.py:901
  627.3 200.1 %reduce-scatter.9.cloned.1.call-start = ((), (), s32[]{:S(2)}) async-start(), calls=%async_computation.14 | async-start | bytes 442368 | tf_op jit(solution)/shard_map/reduce_scatter | solution.py:901
  711.2 131.6 %reduce-scatter.17.cloned.1.call-start = ((), (), s32[]{:S(2)}) async-start(), calls=%async_computation.20 | async-start | bytes 589824 | tf_op jit(solution)/shard_map/reduce_scatter | solution.py:901
  799.9 131.1 %all-gather.30.cloned.1.call-start = ((), (), s32[]{:S(2)}) async-start(), calls=%async_computation.18 | async-start | bytes 2297856 | tf_op jit(solution)/shard_map/all_gather | solution.py:902
  813.1 130.6 %all-gather.28.cloned.1.call-start = ((), (), s32[]{:S(2)}) async-start(), calls=%async_computation.15 | async-start | bytes 2506752 | tf_op jit(solution)/shard_map/all_gather | solution.py:902
  827.3 162.7 %all-gather.32.cloned.1.call-start = ((), (), s32[]{:S(2)}) async-start(), calls=%async_computation.21 | async-start | bytes 3342336 | tf_op jit(solution)/shard_map/all_gather | solution.py:902
  (39 other events, 798.1 us)
Sparse Core Ops, SparseCore 0:
  10.1 26.3 all-gather.15
  38.6 28.3 all-gather.13
  69.1 22.7 all-gather.17
  93.3 33.9 all-gather.19
  128.7 43.3 all-gather.23
  173.6 44.8 all-gather.21
  220.1 44.8 all-gather.25
  301.4 125.9 reduce-scatter.10
  620.3 90.8 reduce-scatter.6
  715.5 84.2 reduce-scatter.14
  802.1 10.9 reduce-scatter.12
  815.2 12.1 reduce-scatter.8
  829.6 13.1 reduce-scatter.16
  844.9 53.9 all-gather.29
  901.1 42.5 all-gather.27
  945.8 44.1 all-gather.31

commit v3 on v2

--- a/solution.py
+++ b/solution.py
@@ -59,15 +59,19 @@
     return (back_rows, jnp.sum(gradient * unit_rows, axis=0))
 
 
-def exchange_kernel(seq_count, shard_count, shared, *refs):
+def exchange_kernel(seq_count, shard_count, shared, along_seq, *refs):
     count = len(shared)
     srcs, dsts = refs[:count], refs[count : 2 * count]
     send_sem, recv_sem, local_sem = refs[2 * count :]
-    total = seq_count * shard_count
-    me = lax.axis_index("seq") * shard_count + lax.axis_index("shard")
+    total = seq_count if along_seq else seq_count * shard_count
+    me = lax.axis_index("seq")
+    if not along_seq:
+        me = me * shard_count + lax.axis_index("shard")
     barrier = pltpu.get_barrier_semaphore()
 
     def place(target):
+        if along_seq:
+            return {"seq": target}
         return {"seq": target // shard_count, "shard": target % shard_count}
 
     def greet(step, carry):
@@ -116,16 +120,16 @@
         every.wait_send()
 
 
-def exchange(payloads, shared, collective_id, name):
+def exchange(payloads, shared, collective_id, name, along_seq=False):
     seq_count = lax.axis_size("seq")
     shard_count = lax.axis_size("shard")
-    total = seq_count * shard_count
+    total = seq_count if along_seq else seq_count * shard_count
     shapes = [
         jax.ShapeDtypeStruct((total,) + (p.shape if whole_one else p.shape[1:]), p.dtype)
         for p, whole_one in zip(payloads, shared)
     ]
     return pl.pallas_call(
-        functools.partial(exchange_kernel, seq_count, shard_count, shared),
+        functools.partial(exchange_kernel, seq_count, shard_count, shared, along_seq),
         out_shape=shapes,
         in_specs=[pl.BlockSpec(memory_space=pltpu.VMEM)] * len(payloads),
         out_specs=[pl.BlockSpec(memory_space=pltpu.VMEM)] * len(payloads),
@@ -135,7 +139,7 @@
     )(*payloads)
 
 
-CHUNKS = 2
+CHUNKS = 4
 
 
 def remote(src, dst, sems, kind, chunk, target):
@@ -878,39 +882,46 @@
     return split.reshape(HEADS * HEAD_DIM, grouped.shape[1])
 
 
-def rows_each(rows, seq_count):
-    return -(-rows // seq_count)
-
-
-def lay_rows(grads, seq_count, shard_count):
-    laid = []
-    for grad in grads:
-        width = grad.shape[1]
-        own = grad.shape[0] // shard_count
+TILE = 256
+
+
+def rows_each(own, seq_count):
+    return -(-own // (8 * seq_count)) * 8
+
+
+def pieces(grouped, seq_count, shard_count):
+    groups, rows, _ = grouped.shape
+    own = rows // shard_count
+    each = rows_each(own, seq_count)
+    block = grouped.astype(BF16).reshape(groups, shard_count, own, TILE)
+    block = jnp.pad(block, ((0, 0), (0, 0), (0, seq_count * each - own), (0, 0)))
+    block = block.reshape(groups, shard_count, seq_count, each, TILE).transpose(2, 1, 0, 3, 4)
+    return block.reshape(seq_count, shard_count, groups * each, TILE)
+
+
+def columns(grad):
+    return grad.reshape(grad.shape[0], -1, TILE).transpose(1, 0, 2)
+
+
+def from_columns(grouped):
+    return grouped.transpose(1, 0, 2).reshape(grouped.shape[1], -1)
+
+
+def sum_pieces(block):
+    seq_count, shard_count, rows, _ = block.shape
+    flat = block.reshape(seq_count * shard_count * rows, TILE)
+    return lax.psum_scatter(flat, ("seq", "shard"), scatter_dimension=0, tiled=True)
+
+
+def take_pieces(share, sizes, seq_count):
+    share = share.reshape(seq_count, -1, TILE)
+    start, taken = 0, []
+    for groups, own in sizes:
         each = rows_each(own, seq_count)
-        block = grad.reshape(shard_count, own, width)
-        block = jnp.pad(block, ((0, 0), (0, seq_count * each - own), (0, 0)))
-        laid.append(block.reshape(shard_count, seq_count, each, width).transpose(1, 0, 2, 3))
-    return laid[0] if len(laid) == 1 else jnp.concatenate(laid, axis=2)
-
-
-def sum_share(block):
-    seq_count, shard_count, rows, width = block.shape
-    part = block.reshape(seq_count * shard_count * rows, width)
-    part = lax.psum_scatter(part, "seq", scatter_dimension=0, tiled=True)
-    part = lax.psum_scatter(part, "shard", scatter_dimension=0, tiled=True)
-    whole_part = lax.all_gather(part, "seq", axis=0, tiled=True)
-    return whole_part.reshape(seq_count, rows, width)
-
-
-def take_rows(share, sizes):
-    seq_count, _, width = share.shape
-    start, taken = 0, []
-    for own in sizes:
-        each = rows_each(own, seq_count)
-        rows = share[:, start : start + each].reshape(seq_count * each, width)[:own]
-        taken.append(rows.astype(F32))
-        start += each
+        part = share[:, start : start + groups * each].reshape(seq_count, groups, each, TILE)
+        part = part.transpose(1, 0, 2, 3).reshape(groups, seq_count * each, TILE)[:, :own]
+        taken.append(part.astype(F32))
+        start += groups * each
     return taken
 
 
@@ -940,34 +951,37 @@
     capacity = max(2, 4 * tokens // owner_count)
     score_scale = HEAD_DIM ** (-0.5)
     gathered = (
-        lax.all_gather(ngram_weight, "shard", axis=0, tiled=True),
-        lax.all_gather(stream_gain, "shard", axis=0, tiled=True),
         lax.all_gather(query_weight, "shard", axis=0, tiled=True),
         lax.all_gather(key_weight, "shard", axis=0, tiled=True),
         lax.all_gather(value_weight, "shard", axis=0, tiled=True),
         lax.all_gather(out_weight, "shard", axis=0, tiled=True),
-        lax.all_gather(mixer_gain, "shard", axis=0, tiled=True),
         lax.all_gather(gate_weight, "shard", axis=0, tiled=True),
         lax.all_gather(up_weight, "shard", axis=0, tiled=True),
         lax.all_gather(down_weight, "shard", axis=0, tiled=True),
-        lax.all_gather(feed_gain, "shard", axis=0, tiled=True),
     )
     (
-        full_ngram,
-        full_stream_gain,
         full_query,
         full_key,
         full_value,
         full_out,
-        full_mixer_gain,
         full_gate,
         full_up,
         full_down,
-        full_feed_gain,
     ) = gathered
-    gain_stream = full_stream_gain.astype(jnp.float32)
-    gain_mixer = full_mixer_gain.astype(jnp.float32)
-    gain_feed = full_feed_gain.astype(jnp.float32)
+    ngram_rows, width = ngram_weight.shape
+    share_width = stream_gain.shape[0]
+    own_gains = jnp.pad(
+        jnp.stack([stream_gain, mixer_gain, feed_gain]),
+        ((0, -(ngram_rows + 3) % 16 + 0), (0, width - share_width)),
+    )
+    small = lax.all_gather(
+        jnp.concatenate([ngram_weight, own_gains], axis=0), "shard", axis=0, tiled=True
+    ).reshape(shard_count, -1, width)
+    full_ngram = small[:, :ngram_rows].reshape(shard_count * ngram_rows, width)
+    full_gains = small[:, ngram_rows : ngram_rows + 3, :share_width].astype(F32)
+    gain_stream, gain_mixer, gain_feed = (
+        full_gains[:, which].reshape(shard_count * share_width) for which in range(3)
+    )
     flat_owner = owners.reshape(-1)
     flat_row = row_ids.reshape(-1)
     request_count = flat_owner.shape[0]
@@ -1084,11 +1098,15 @@
     grad_heads = jnp.einsum(
         "td,ed->te", grad_mixer, out_rows, preferred_element_type=jnp.float32
     ).astype(jnp.bfloat16)
-    early = lay_rows(
-        (jnp.concatenate([grad_gate, grad_up], axis=1).astype(BF16),), seq_count, shard_count
-    ), lay_rows((grad_down.astype(BF16), grad_out.astype(BF16)), seq_count, shard_count)
+    early = jnp.concatenate(
+        [
+            pieces(columns(grad.astype(BF16)), seq_count, shard_count)
+            for grad in (grad_gate, grad_up, grad_down, grad_out)
+        ],
+        axis=2,
+    )
     grad_heads, early = lax.optimization_barrier((grad_heads, early))
-    early_shares = [sum_share(block) for block in early]
+    early_part = sum_pieces(early)
     parts, grad_query_turned, grad_key_groups, grad_value_groups = attention_backward(
         mixer_in,
         blocks,
@@ -1102,13 +1120,22 @@
         mixed_full,
         log_sum,
     )
-    grad_key = from_rotary_groups(grad_key_groups)
-    grad_value = from_value_groups(grad_value_groups)
-    grad_mixer_in = halo_reduce(parts, seq_count // 4) + jnp.einsum(
-        "et,de->td", grad_query_turned, full_query, preferred_element_type=jnp.float32
-    )
     grad_query = jnp.einsum(
         "td,et->de", mixer_in, grad_query_turned, preferred_element_type=jnp.float32
+    )
+    late = jnp.concatenate(
+        [
+            pieces(grouped, seq_count, shard_count)
+            for grouped in (columns(grad_query.astype(BF16)), grad_key_groups, grad_value_groups)
+        ],
+        axis=2,
+    )
+    parts, late, early_part = lax.optimization_barrier((parts, late, early_part))
+    late_part = sum_pieces(late)
+    reduced, early_part = lax.optimization_barrier((halo_reduce(parts, seq_count // 4), early_part))
+    early_share = lax.all_gather(early_part, "seq", axis=0, tiled=True)
+    grad_mixer_in = reduced + jnp.einsum(
+        "et,de->td", grad_query_turned, full_query, preferred_element_type=jnp.float32
     )
     back_one, grad_mixer_gain = norm_back(grad_mixer_in, unit_one, inverse_one, gain_mixer)
     grad_residual = grad_middle + back_one
@@ -1126,9 +1153,34 @@
         .at[slot_index]
         .set(grad_picked)
     )
-    incoming, energy_parts = exchange(
-        (outgoing.reshape(owner_count, capacity, -1), energy), (False, True), 5, "give_back"
-    )
+    each = -(-ngram_rows // seq_count)
+    ngram_pieces = jnp.pad(
+        grad_ngram.reshape(shard_count, ngram_rows, width),
+        ((0, 0), (0, seq_count * each - ngram_rows), (0, 0)),
+    )
+    ngram_pieces = ngram_pieces.reshape(shard_count, seq_count, each, width)
+    gain_rows = jnp.stack([grad_stream_gain, grad_mixer_gain, grad_feed_gain])
+    gain_rows = gain_rows.reshape(3, shard_count, share_width).transpose(1, 0, 2)
+    gain_rows = jnp.pad(gain_rows, ((0, 0), (0, -(each + 3) % 16), (0, width - share_width)))
+    gain_rows = jnp.broadcast_to(
+        gain_rows[:, None], (shard_count, seq_count) + gain_rows.shape[1:]
+    )
+    small_rows = jnp.concatenate([ngram_pieces, gain_rows], axis=2).astype(BF16)
+    small_rows = small_rows.transpose(1, 0, 2, 3).reshape(owner_count, -1, width)
+    incoming, small_parts, energy_parts = exchange(
+        (outgoing.reshape(owner_count, capacity, -1), small_rows, energy),
+        (False, False, True),
+        5,
+        "give_back",
+    )
+    incoming, small_parts, energy_parts, late_part = lax.optimization_barrier(
+        (incoming, small_parts, energy_parts, late_part)
+    )
+    late_share = lax.all_gather(late_part, "seq", axis=0, tiled=True)
+    small_sum = jnp.sum(small_parts.astype(F32), axis=0)
+    total_gains = small_sum[each : each + 3, :share_width]
+    (ngram_share,) = exchange((small_sum.astype(BF16),), (True,), 6, "spread", along_seq=True)
+    total_ngram = ngram_share[:, :each].reshape(seq_count * each, width)[:ngram_rows].astype(F32)
     energies = jnp.sum(energy_parts[:, :, 0], axis=0)
     entry_count = owner_count * tokens * stream.shape[1]
     stream_rms = jnp.sqrt(energies[0] / entry_count)
@@ -1142,38 +1194,23 @@
     grad_table = (
         jnp.zeros(table.shape, jnp.float32).at[jnp.maximum(asked_rows, 0).reshape(-1)].add(incoming)
     )
-    share_width = stream_gain.shape[0]
-    gains = jnp.stack([grad_stream_gain, grad_mixer_gain, grad_feed_gain])
-    gains = gains.reshape(3, shard_count, 1, share_width)
-    gains = jnp.pad(
-        gains, ((0, seq_count - 3), (0, 0), (0, 0), (0, stream.shape[1] - share_width))
-    ).astype(BF16)
-    late = jnp.concatenate(
-        [
-            lay_rows(
-                (
-                    grad_query.astype(BF16),
-                    grad_key.astype(BF16),
-                    grad_value.astype(BF16),
-                    grad_ngram.astype(BF16),
-                ),
-                seq_count,
-                shard_count,
+    wide = share_width
+    total_gate, total_up, total_down, total_out = (
+        from_columns(total)
+        for total in take_pieces(
+            early_share,
+            (
+                (gate_weight.shape[1] // TILE, wide),
+                (up_weight.shape[1] // TILE, wide),
+                (width // TILE, down_weight.shape[0]),
+                (width // TILE, wide),
             ),
-            gains,
-        ],
-        axis=2,
-    )
-    gain_row = late.shape[2] - 1
-    late = jnp.pad(late, ((0, 0), (0, 0), (0, -late.shape[2] % 16), (0, 0)))
-    late_share = sum_share(late)
-    wide = stream.shape[1] // shard_count
-    total_gate_up = take_rows(early_shares[0], (wide,))[0]
-    total_down, total_out = take_rows(early_shares[1], (down_weight.shape[0], wide))
-    total_query, total_key, total_value, total_ngram = take_rows(
-        late_share, (wide, wide, wide, ngram_weight.shape[0])
-    )
-    total_gains = late_share[:3, gain_row, :share_width].astype(F32)
+            seq_count,
+        )
+    )
+    total_query, total_key, total_value = take_pieces(
+        late_share, ((width // TILE, wide), (GROUPS, wide), (GROUPS, wide)), seq_count
+    )
     return (
         mixed,
         grad_input,
@@ -1183,13 +1220,13 @@
         grad_table,
         total_ngram,
         total_gains[0],
-        total_query,
-        total_key,
-        total_value,
+        from_columns(total_query),
+        from_rotary_groups(total_key),
+        from_value_groups(total_value),
         total_out,
         total_gains[1],
-        total_gate_up[:, : gate_weight.shape[1]],
-        total_gate_up[:, gate_weight.shape[1] :],
+        total_gate,
+        total_up,
         total_down,
         total_gains[2],
     )

time: 1020 us -> 814 us (0.80)
  Pallas kernels: 358 us -> 254 us
  waiting for transfers between devices: 315 us -> 252 us
  blocking collectives: 26.9 us -> 9.64 us
  local copies, waits for them, and re-layouts: 171 us -> 156 us
    pallas_call x1, Pallas kernels: 218 us -> 64.1 us  [halo_reduce(): pl.pallas_call(functools.partial(reduce_kernel, group_count), out_shape=j...]
    reduce_scatter x6 -> x2, waiting for transfers between devices: 215 us -> 151 us  [sum_pieces(): lax.psum_scatter(flat, ('seq', 'shard'), scatter_dimension=0, tiled=True)]
    pallas_call x3 -> x4, Pallas kernels: 63.1 us -> 110 us  [exchange(): pl.pallas_call(functools.partial(exchange_kernel, seq_count, shard_count,...]
    all_gather x1, waiting for transfers between devices: 0.02 us -> 31 us  [shards(): lax.all_gather(up_weight, 'shard', axis=0, tiled=True)]
    unnamed x107 -> x129, local copies, waits for them, and re-layouts: 51.8 us -> 72.9 us
    all_gather x3 -> x2, waiting for transfers between devices: 46.9 us -> 27.5 us  [the longest x1 27.5 us: shards(): early_share = lax.all_gather(early_part, 'seq', axis=0, tiled=True)]
    concatenate x1 -> x0, local copies, waits for them, and re-layouts: 17.3 us -> none  [shards(): jnp.concatenate([lay_rows((grad_query.astype(BF16), grad_key.astype(BF16)...]
    all_gather x4 -> x1, blocking collectives: 26.9 us -> 9.64 us  [shards(): lax.all_gather(jnp.concatenate([ngram_weight, own_gains], axis=0), 'shard...]
  transfers between devices with their start and end apart: 16 -> 11, of which waited for: 9 -> 5; matrix products, arithmetic and copies ran while one was open for 23% -> 22% of each run, Pallas kernels for 36% -> 32%
where the time goes in v3:
time: 814 us; the launch traced here: 805 us
  Pallas kernels  254 us (31%)
  waiting for transfers between devices  252 us (31%)
  local copies, waits for them, and re-layouts  156 us (19%)
  other arithmetic  63.5 us (8%)
  matrix products  46.6 us (6%)
  between operations  20.8 us (3%)
  blocking collectives  9.64 us (1%)
    reduce_scatter x2, waiting for transfers between devices, sum_pieces(): lax.psum_scatter(flat, ('seq', 'shard'), scatter_dimension=0, tiled=True)  151 us
    pallas_call x4, Pallas kernels, exchange(): pl.pallas_call(functools.partial(exchange_kernel, seq_count, shard_count,...  110 us
    unnamed x129, local copies, waits for them, and re-layouts  72.9 us
    pallas_call x1, Pallas kernels, halo_reduce(): pl.pallas_call(functools.partial(reduce_kernel, group_count), out_shape=j...  64.1 us
    all_gather x1, waiting for transfers between devices, shards(): lax.all_gather(down_weight, 'shard', axis=0, tiled=True)  40.7 us
    pallas_call x1, Pallas kernels, attention_backward(): pl.pallas_call(backward_kernel, out_shape=(jax.ShapeDtypeStruct((SLOTS +...  32.9 us
    all_gather x1, waiting for transfers between devices, shards(): lax.all_gather(up_weight, 'shard', axis=0, tiled=True)  31 us
    all_gather x1, waiting for transfers between devices, shards(): early_share = lax.all_gather(early_part, 'seq', axis=0, tiled=True)  27.5 us
  transfers between devices with their start and end apart: 11, of which 5 were waited for; matrix products, arithmetic and copies ran while one was open for 22% of the time, Pallas kernels for 32%

profile of v3, /device:TPU:0, one launch (start us, length us, event | category | flops | bytes accessed | tf_op | source)
XLA Modules:
  0.0 804.5 jit_solution(10196703751881050683)
XLA Ops:
  21.1 11.2 %ask.1 = s32[32,5,128]{2,1,0:T(8,128)} custom-call(s32[32,5,128]{2,1,0:T(8,128)} %pad_add_fusion.refs_0_), custom_call_target="tpu_custom_call" | custom-call | tf_op jit(solution)/shard_map/ask/pallas_call | solution.py:131
  36.5 14.8 %copy.178 = bf16[25000,192]{1,0:T(8,128)(2,1)} copy(bf16[25000,192]{0,1:T(8,128)(2,1)} %param.21) | data formatting | bytes 19200000 | tf_op args[4]
  51.4 12.9 %gather_fusion = bf16[2048,192]{1,0:T(8,128)(2,1)S(1)} fusion(bf16[25000,192]{1,0:T(8,128)(2,1)} %copy.178, s32[2048]{0:T(1024)S(1)} %broadcast_clamp_fusion), kind=kCustom, calls=%fused_computation | custom fusion | bytes 1581056 | tf_op jit(solution)/shard_map/jit(_take)/gather | solution.py:1011
  65.8 25.0 %answer.1 = bf16[32,64,192]{2,1,0:T(8,128)(2,1)} custom-call(bf16[32,64,192]{2,1,0:T(8,128)(2,1)} %select_select_fusion.refs_0_), custom_call_target="tpu_custom_call" | custom-call | tf_op jit(solution)/shard_map/answer/pallas_call | solution.py:131
  90.8 4.8 gather_fusion.1
  96.9 9.6 %all_gather.30 = bf16[416,768]{1,0:T(8,128)(2,1)S(1)} all-gather(bf16[208,768]{1,0:T(8,128)(2,1)S(1)} %pad_maximum_fusion.2), channel_id=1, replica_groups=mesh['seq'=16,'shard'=2] {'shard'}, dimensions={0}, use_global_device_ids=true | all-gather | bytes 958464 | tf_op jit(solution)/shard_map/all_gather | solution.py:977
  110.6 26.7 %halo_gather.1.x_ref = bf16[13,512,768]{2,1,0:T(8,128)(2,1)} custom-call(bf16[512,768]{1,0:T(8,128)(2,1)} %multiply_convert_fusion.4.own_ref), custom_call_target="tpu_custom_call" | custom-call | tf_op jit(solution)/shard_map/halo_gather/pallas_call | solution.py:299
  156.5 20.3 %attention_forward.1 = (f32[512,1024]{1,0:T(8,128)}, f32[512,128]{1,0:T(8,128)}) custom-call(s32[9]{0:T(128)} %compare_select_fusion.5.slot_ref, s32[9]{0:T(128)} %compare_convert_fusion.valid_ref, bf16[512,768]{1,0:T(8,128)(2,1)} %multiply_convert_fusion.4.own_ref, bf16[13,512,768]{2,1,0:T(8,128)(2,1)} %halo_gather.1.x_ref, ...), custom_call_target="tpu_custom_call" | custom-call | flops 70000001024 | bytes 10000000 | tf_op jit(solution)/shard_map/attention_forward/pallas_call | solution.py:599
  182.0 5.9 fusion.44
  187.9 31.0 %all-gather.20.cloned.1.call-done = bf16[768,2048]{1,0:T(8,128)(2,1)} async-done(((bf16[384,2048]{1,0:T(8,128)(2,1)}), bf16[768,2048]{1,0:T(8,128)(2,1)}) %all-gather.20.cloned.1.call-update) | async-done | bytes 3145744 | tf_op jit(solution)/shard_map/all_gather | solution.py:959
  218.9 5.8 fusion.45
  224.6 40.7 %all-gather.22.cloned.1.call-done = bf16[2048,768]{1,0:T(8,128)(2,1)} async-done(((bf16[1024,768]{1,0:T(8,128)(2,1)}), bf16[2048,768]{1,0:T(8,128)(2,1)}) %all-gather.22.cloned.1.call-update) | async-done | bytes 3145744 | tf_op jit(solution)/shard_map/all_gather | solution.py:960
  265.4 6.5 multiply_convert_fusion
  307.3 10.8 %pad_maximum_fusion = bf16[16,2,648,256]{3,2,1,0:T(8,128)(2,1)} fusion(bf16[16,2,72,256]{3,2,1,0:T(8,128)(2,1)} %bitcast.253, bf16[16,2,192,256]{3,2,1,0:T(8,128)(2,1)S(1)} %bitcast.226, bf16[16,2,192,256]{3,2,1,0:T(8,128)(2,1)S(1)} %bitcast.225, bf16[16,2,192,256]{3,2,1,0:T(8,128)(2,1)S(1)} %bitcast.224), kind=kLoop, calls=%fused_computation.8 | loop fusion | flops 42467328 | bytes 21233664 | tf_op jit(solution)/shard_map/concatenate | solution.py:1101
  322.1 32.9 %attention_backward.1 = (bf16[13,512,768]{2,1,0:T(8,128)(2,1)}, bf16[768,512]{1,0:T(8,128)(2,1)}, bf16[4,768,256]{2,1,0:T(8,128)(2,1)}, bf16[4,768,256]{2,1,0:T(8,128)(2,1)}) custom-call(s32[9]{0:T(128)} %compare_select_fusion.5.slot_ref, s32[9]{0:T(128)} %compare_convert_fusion.valid_ref, bf16[512,768]{1,0:T(8,128)(2,1)} %multiply_convert_fusion.4.own_ref, ...), custom_call_target="tpu_custom_call" | custom-call | flops 120000004096 | bytes 20000000 | tf_op jit(solution)/shard_map/attention_backward/pallas_call | solution.py:785
  363.1 128.5 %reduce-scatter.3.cloned.1.call-done = bf16[648,256]{1,0:T(8,128)(2,1)} async-done(((bf16[20736,256]{1,0:T(8,128)(2,1)}), bf16[648,256]{1,0:T(8,128)(2,1)}) %reduce-scatter.3.cloned.1.call-update) | async-done | bytes 331792 | tf_op jit(solution)/shard_map/reduce_scatter | solution.py:913
  493.8 64.1 %halo_reduce.1 = f32[512,768]{1,0:T(8,128)} custom-call(bf16[13,512,768]{2,1,0:T(8,128)(2,1)} %get-tuple-element.45.part_ref), custom_call_target="tpu_custom_call" | custom-call | tf_op jit(solution)/shard_map/halo_reduce/pallas_call | solution.py:458
  568.8 6.1 scatter_custom_fusion.1
  577.6 58.8 %give_back.1 = (bf16[32,64,192]{2,1,0:T(8,128)(2,1)}, bf16[32,16,768]{2,1,0:T(8,128)(2,1)}, f32[32,8,128]{2,1,0:T(8,128)}) custom-call(bf16[32,64,192]{2,1,0:T(8,128)(2,1)} %bitcast.255, bf16[32,16,768]{2,1,0:T(8,128)(2,1)} %bitcast.257, f32[8,128]{1,0:T(8,128)} %broadcast_in_dim.143.refs_2_), custom_call_target="tpu_custom_call" | custom-call | tf_op jit(solution)/shard_map/give_back/pallas_call | solution.py:131
  636.4 22.0 %reduce-scatter.5.cloned.1.call-done = bf16[264,256]{1,0:T(8,128)(2,1)} async-done(((bf16[8448,256]{1,0:T(8,128)(2,1)}), bf16[264,256]{1,0:T(8,128)(2,1)}) %reduce-scatter.5.cloned.1.call-update) | async-done | bytes 135184 | tf_op jit(solution)/shard_map/reduce_scatter | solution.py:913
  660.7 23.5 %scatter_custom_fusion.2 = f32[25000,192]{1,0:T(8,128)} fusion(s32[2048]{0:T(1024)} %copy-done.38, f32[]{:T(128)} %constant.130.clone.1, bf16[2048,192]{1,0:T(8,128)(2,1)S(1)} %bitcast.254), kind=kCustom, calls=%fused_computation.6 | custom fusion | flops 786432 | bytes 19986944 | tf_op jit(solution)/shard_map/scatter-add | solution.py:1195
  684.2 23.6 %copy.218 = f32[25000,192]{0,1:T(8,128)} copy(f32[25000,192]{1,0:T(8,128)} %scatter_custom_fusion.2) | data formatting | bytes 38400000
  708.6 15.3 %spread.1 = bf16[16,16,768]{2,1,0:T(8,128)(2,1)} custom-call(bf16[16,768]{1,0:T(8,128)(2,1)} %convert_element_type.243.refs_0_), custom_call_target="tpu_custom_call" | custom-call | tf_op jit(solution)/shard_map/spread/pallas_call | solution.py:131
  738.4 27.5 %all-gather.26.cloned.1.call-done = bf16[10368,256]{1,0:T(8,128)(2,1)} async-done(((bf16[648,256]{1,0:T(8,128)(2,1)}), bf16[10368,256]{1,0:T(8,128)(2,1)}) %all-gather.26.cloned.1.call-update) | async-done | bytes 5308432 | tf_op jit(solution)/shard_map/all_gather | solution.py:1136
  (310 shorter events, 155.2 us)
Async XLA Ops:
  7.2 136.4 %all-gather.10.cloned.1.call-start = ((), (), s32[]{:S(2)}) async-start(), calls=%async_computation.2 | async-start | bytes 1769472 | tf_op jit(solution)/shard_map/all_gather | solution.py:954
  9.5 139.4 %all-gather.12.cloned.1.call-start = ((), (), s32[]{:S(2)}) async-start(), calls=%async_computation.3 | async-start | bytes 1769472 | tf_op jit(solution)/shard_map/all_gather | solution.py:955
  10.6 143.4 %all-gather.14.cloned.1.call-start = ((), (), s32[]{:S(2)}) async-start(), calls=%async_computation.4 | async-start | bytes 1769472 | tf_op jit(solution)/shard_map/all_gather | solution.py:956
  11.8 165.1 %all-gather.16.cloned.1.call-start = ((), (), s32[]{:S(2)}) async-start(), calls=%async_computation.5 | async-start | bytes 1769472 | tf_op jit(solution)/shard_map/all_gather | solution.py:957
  12.3 169.6 %all-gather.18.cloned.1.call-start = ((), (), s32[]{:S(2)}) async-start(), calls=%async_computation.6 | async-start | bytes 4718592 | tf_op jit(solution)/shard_map/all_gather | solution.py:958
  12.9 205.9 %all-gather.20.cloned.1.call-start = ((), (), s32[]{:S(2)}) async-start(), calls=%async_computation.7 | async-start | bytes 4718592 | tf_op jit(solution)/shard_map/all_gather | solution.py:959
  13.5 251.8 %all-gather.22.cloned.1.call-start = ((), (), s32[]{:S(2)}) async-start(), calls=%async_computation.8 | async-start | bytes 4718592 | tf_op jit(solution)/shard_map/all_gather | solution.py:960
  14.3 477.3 %reduce-scatter.3.cloned.1.call-start = ((), (), s32[]{:S(2)}) async-start(), calls=%async_computation.9 | async-start | bytes 10948608 | tf_op jit(solution)/shard_map/reduce_scatter | solution.py:913
  15.9 35.4 %copy-start.43 = (s32[1024,1]{0,1:T(1,128)}, s32[1024,1]{0,1:T(1,128)S(1)}, u32[]{:S(2)}) copy-start(s32[1024,1]{0,1:T(1,128)S(1)} %compare_select_fusion) | copy-start | bytes 12292
  108.9 69.5 %copy-start = (f32[512,768]{1,0:T(8,128)}, f32[512,768]{1,0:T(8,128)S(1)}, u32[]{:S(2)}) copy-start(f32[512,768]{1,0:T(8,128)S(1)} %get-tuple-element.169) | copy-start | bytes 4718596
  108.9 69.4 %copy-start.31 = (f32[512]{0:T(512)}, f32[512]{0:T(512)S(1)}, u32[]{:S(2)}) copy-start(f32[512]{0:T(512)S(1)} %add_rsqrt_fusion.2) | copy-start | bytes 6148
  109.0 69.4 %copy-start.28 = (f32[768]{0:T(1024)}, f32[768]{0:T(1024)S(1)}, u32[]{:S(2)}) copy-start(f32[768]{0:T(1024)S(1)} %mul.352) | copy-start | bytes 9220
  187.8 77.5 %copy-start.54 = (bf16[1,512,768]{2,1,0:T(8,128)(2,1)S(1)}, bf16[1,512,768]{2,1,0:T(8,128)(2,1)}, u32[]{:S(2)}) copy-start(bf16[1,512,768]{2,1,0:T(8,128)(2,1)} %param.33) | copy-start | bytes 2359300
  318.2 340.2 %reduce-scatter.5.cloned.1.call-start = ((), (), s32[]{:S(2)}) async-start(), calls=%async_computation.10 | async-start | bytes 4460544 | tf_op jit(solution)/shard_map/reduce_scatter | solution.py:913
  322.1 33.0 %copy-start.18 = (bf16[512,768]{1,0:T(8,128)(2,1)S(1)}, bf16[512,768]{1,0:T(8,128)(2,1)}, u32[]{:S(2)}) copy-start(bf16[512,768]{1,0:T(8,128)(2,1)} %multiply_convert_fusion.4.own_ref) | copy-start | bytes 2359300
  491.7 237.7 %all-gather.24.cloned.1.call-start = ((), (), s32[]{:S(2)}) async-start(), calls=%async_computation.11 | async-start | bytes 2297856 | tf_op jit(solution)/shard_map/all_gather | solution.py:1179
  493.7 64.1 %copy-start.1 = (f32[512,768]{1,0:T(8,128)S(1)}, f32[512,768]{1,0:T(8,128)}, u32[]{:S(2)}) copy-start(f32[512,768]{1,0:T(8,128)} %copy-done) | copy-start | bytes 4718596
  493.7 64.1 %copy-start.29 = (f32[768]{0:T(1024)S(1)}, f32[768]{0:T(1024)}, u32[]{:S(2)}) copy-start(f32[768]{0:T(1024)} %copy-done.28) | copy-start | bytes 9220
  493.7 64.1 %copy-start.32 = (f32[512]{0:T(512)S(1)}, f32[512]{0:T(512)}, u32[]{:S(2)}) copy-start(f32[512]{0:T(512)} %copy-done.31) | copy-start | bytes 6148
  493.7 64.1 %copy-start.37 = (f32[768]{0:T(1024)S(1)}, f32[768]{0:T(1024)}, u32[]{:S(2)}) copy-start(f32[768]{0:T(1024)} %copy-done.36) | copy-start | bytes 9220
  493.7 64.1 %copy-start.40 = (f32[512]{0:T(512)S(1)}, f32[512]{0:T(512)}, u32[]{:S(2)}) copy-start(f32[512]{0:T(512)} %copy-done.39) | copy-start | bytes 6148
  568.7 90.4 %copy-start.34 = (pred[32,64]{1,0:T(8,128)(4,1)S(1)}, pred[32,64]{1,0:T(8,128)(4,1)}, u32[]{:S(2)}) copy-start(pred[32,64]{1,0:T(8,128)(4,1)} %copy-done.33) | copy-start | bytes 6148
  658.4 107.4 %all-gather.26.cloned.1.call-start = ((), (), s32[]{:S(2)}) async-start(), calls=%async_computation.12 | async-start | bytes 5640192 | tf_op jit(solution)/shard_map/all_gather | solution.py:1136
  684.2 23.7 %copy-start.24 = (bf16[32,16,768]{2,1,0:T(8,128)(2,1)S(1)}, bf16[32,16,768]{2,1,0:T(8,128)(2,1)}, u32[]{:S(2)}) copy-start(bf16[32,16,768]{2,1,0:T(8,128)(2,1)} %get-tuple-element.54) | copy-start | bytes 2359300
  (42 other events, 159.6 us)
Sparse Core Ops, SparseCore 0:
  10.1 26.3 all-gather.9
  38.6 22.7 all-gather.11
  63.6 33.9 all-gather.13
  99.0 20.6 all-gather.15
  121.1 51.4 all-gather.17
  173.9 44.8 all-gather.19
  220.4 44.9 all-gather.21
  318.3 173.2 reduce-scatter.2
  497.1 161.2 reduce-scatter.4
  660.5 41.6 all-gather.23
  704.4 61.4 all-gather.25

commit v4 on v3

--- a/solution.py
+++ b/solution.py
@@ -499,7 +499,7 @@
 
 def forward_kernel(
     slot_ref, valid_ref, own_ref, x_ref, wq_ref, wk_ref, wv_ref, cr_ref, sr_ref, cb_ref, sb_ref,
-    kf_ref, qf_ref, out_ref, lse_ref, qm_ref, kb_ref, vt_ref, acc_ref, top_ref,
+    kf_ref, qf_ref, out_ref, lse_ref, kb_ref, qm_ref, vt_ref, acc_ref, top_ref,
 ):
     step = pl.program_id(0)
     tokens = own_ref.shape[0]
@@ -534,8 +534,8 @@
 
         def keys(g, carry):
             first, second = rotate(nn(x_ref[0], wk_ref[g]), cosine, sine)
-            kb_ref[g, :, :128] = (first + features).astype(BF16)
-            kb_ref[g, :, 128:] = second.astype(BF16)
+            kb_ref[0, g, :, :128] = (first + features).astype(BF16)
+            kb_ref[0, g, :, 128:] = second.astype(BF16)
             values = nt(wv_ref[g], x_ref[0])
             row = lax.broadcasted_iota(jnp.int32, values.shape, 0) % VROWS
             values = jnp.where(row == HEAD_DIM, 1.0, values).astype(BF16)
@@ -549,7 +549,7 @@
             def one_group(g, carry):
                 for hh in range(GROUP):
                     h = g * GROUP + hh
-                    scores = nt(kb_ref[g], qm_ref[h])
+                    scores = nt(kb_ref[0, g], qm_ref[h])
                     if causal:
                         key = lax.broadcasted_iota(jnp.int32, scores.shape, 0)
                         query = lax.broadcasted_iota(jnp.int32, scores.shape, 1)
@@ -601,6 +601,7 @@
         out_shape=(
             jax.ShapeDtypeStruct((tokens, GROUPS * 256), F32),
             jax.ShapeDtypeStruct((tokens, 128), F32),
+            jax.ShapeDtypeStruct((steps, GROUPS, tokens, 256), BF16),
         ),
         grid_spec=pltpu.PrefetchScalarGridSpec(
             num_scalar_prefetch=2,
@@ -618,10 +619,13 @@
                 pl.BlockSpec((1, tokens, 128), lambda t, slot, valid: (t, 0, 0)),
                 whole(tokens, 128),
             ],
-            out_specs=[whole(tokens, GROUPS * 256), whole(tokens, 128)],
+            out_specs=[
+                whole(tokens, GROUPS * 256),
+                whole(tokens, 128),
+                pl.BlockSpec((1, GROUPS, tokens, 256), lambda t, slot, valid: (t, 0, 0, 0)),
+            ],
             scratch_shapes=[
                 pltpu.VMEM((HEADS, tokens, 256), BF16),
-                pltpu.VMEM((GROUPS, tokens, 256), BF16),
                 pltpu.VMEM((HEADS, VROWS, tokens), BF16),
                 pltpu.VMEM((HEADS, VROWS, tokens), F32),
                 pltpu.VMEM((HEADS, 1, tokens), F32),
@@ -644,8 +648,8 @@
 
 def backward_kernel(
     slot_ref, valid_ref, own_ref, x_ref, wq_ref, wk_ref, wkt_ref, wv_ref, cr_ref, sr_ref, cb_ref,
-    sb_ref, ct_ref, st_ref, kf_ref, qf_ref, go_ref, heads_ref, lse_ref, gx_ref, dq_ref, dwk_ref,
-    dwv_ref, qb_ref, gm_ref, kb_ref, kt_ref, vb_ref, dqt_ref, dk_ref, dv_ref, gxa_ref, wka_ref,
+    sb_ref, ct_ref, st_ref, kb_ref, qf_ref, go_ref, heads_ref, lse_ref, gx_ref, dq_ref, dwk_ref,
+    dwv_ref, qb_ref, gm_ref, kt_ref, vb_ref, dqt_ref, dk_ref, dv_ref, gxa_ref, wka_ref,
     wva_ref,
 ):
     step = pl.program_id(0)
@@ -693,12 +697,8 @@
     @pl.when(valid_ref[step] > 0)
     def _():
         cosine, sine = block_angles(step, cr_ref, sr_ref, cb_ref, sb_ref)
-        features = kf_ref[0].astype(F32)
 
         def keys(g, carry):
-            first, second = rotate(nn(x_ref[0], wk_ref[g]), cosine, sine)
-            kb_ref[g, :, :128] = (first + features).astype(BF16)
-            kb_ref[g, :, 128:] = second.astype(BF16)
             values = nn(x_ref[0], wv_ref[g])
             wide = lax.broadcasted_iota(jnp.int32, values.shape, 1)
             ones = (wide == DELTA_LANE) | (wide == DELTA_LANE + 1)
@@ -718,7 +718,7 @@
             def one_group(g, carry):
                 for hh in range(GROUP):
                     h = g * GROUP + hh
-                    prob = jnp.exp2(nt(kb_ref[g], qb_ref[h]))
+                    prob = jnp.exp2(nt(kb_ref[0, g], qb_ref[h]))
                     if causal:
                         key = lax.broadcasted_iota(jnp.int32, prob.shape, 0)
                         query = lax.broadcasted_iota(jnp.int32, prob.shape, 1)
@@ -775,11 +775,10 @@
 
 
 def attention_backward(
-    own, blocks, slots, valid, weights, tables, turned, features, grad_heads, heads, lse
+    own, blocks, slots, valid, weights, tables, turned, keys, query_features, grad_heads, heads, lse
 ):
     tokens, width = own.shape
     steps = slots.shape[0]
-    key_features, query_features = features
     wq, wk, wkt, wv = weights
     ct, st = turned
     return pl.pallas_call(
@@ -806,7 +805,7 @@
                 whole(*tables[3].shape),
                 whole(*ct.shape),
                 whole(*st.shape),
-                pl.BlockSpec((1, tokens, 128), lambda t, slot, valid: (t, 0, 0)),
+                pl.BlockSpec((1, GROUPS, tokens, 256), lambda t, slot, valid: (t, 0, 0, 0)),
                 whole(tokens, 128),
                 whole(tokens, GROUPS * 256),
                 whole(tokens, GROUPS * 256),
@@ -821,7 +820,6 @@
             scratch_shapes=[
                 pltpu.VMEM((HEADS, tokens, 256), BF16),
                 pltpu.VMEM((HEADS, tokens, 256), BF16),
-                pltpu.VMEM((GROUPS, tokens, 256), BF16),
                 pltpu.VMEM((HEADS, HEAD_DIM, tokens), BF16),
                 pltpu.VMEM((GROUPS, tokens, 256), BF16),
                 pltpu.VMEM((HEADS, HEAD_DIM, tokens), F32),
@@ -840,7 +838,7 @@
         ),
         name="attention_backward",
     )(
-        slots, valid, own, blocks, wq, wk, wkt, wv, *tables, ct, st, key_features,
+        slots, valid, own, blocks, wq, wk, wkt, wv, *tables, ct, st, keys,
         query_features, grad_heads, heads, lse,
     )
 
@@ -1057,7 +1055,7 @@
     value_grouped = value_groups(full_value)
     out_rows = padded_rows(full_out)
     blocks = halo_gather(mixer_in, seq_count // 4)
-    mixed_full, log_sum = attention_forward(
+    mixed_full, log_sum, keys = attention_forward(
         mixer_in, blocks, slots, valid, (query_groups, key_groups, value_turned), tables, features
     )
     heads_low = mixed_full.astype(BF16)
@@ -1115,7 +1113,8 @@
         (query_groups, key_groups, key_turned, value_grouped),
         tables,
         turned,
-        features,
+        keys,
+        query_features,
         grad_heads,
         mixed_full,
         log_sum,
@@ -1131,9 +1130,8 @@
         axis=2,
     )
     parts, late, early_part = lax.optimization_barrier((parts, late, early_part))
-    late_part = sum_pieces(late)
-    reduced, early_part = lax.optimization_barrier((halo_reduce(parts, seq_count // 4), early_part))
     early_share = lax.all_gather(early_part, "seq", axis=0, tiled=True)
+    reduced = halo_reduce(parts, seq_count // 4)
     grad_mixer_in = reduced + jnp.einsum(
         "et,de->td", grad_query_turned, full_query, preferred_element_type=jnp.float32
     )
@@ -1167,20 +1165,17 @@
     )
     small_rows = jnp.concatenate([ngram_pieces, gain_rows], axis=2).astype(BF16)
     small_rows = small_rows.transpose(1, 0, 2, 3).reshape(owner_count, -1, width)
+    outgoing, late, early_share = lax.optimization_barrier((outgoing, late, early_share))
+    late_part = sum_pieces(late)
     incoming, small_parts, energy_parts = exchange(
         (outgoing.reshape(owner_count, capacity, -1), small_rows, energy),
         (False, False, True),
         5,
         "give_back",
     )
-    incoming, small_parts, energy_parts, late_part = lax.optimization_barrier(
-        (incoming, small_parts, energy_parts, late_part)
-    )
-    late_share = lax.all_gather(late_part, "seq", axis=0, tiled=True)
     small_sum = jnp.sum(small_parts.astype(F32), axis=0)
     total_gains = small_sum[each : each + 3, :share_width]
     (ngram_share,) = exchange((small_sum.astype(BF16),), (True,), 6, "spread", along_seq=True)
-    total_ngram = ngram_share[:, :each].reshape(seq_count * each, width)[:ngram_rows].astype(F32)
     energies = jnp.sum(energy_parts[:, :, 0], axis=0)
     entry_count = owner_count * tokens * stream.shape[1]
     stream_rms = jnp.sqrt(energies[0] / entry_count)
@@ -1194,6 +1189,11 @@
     grad_table = (
         jnp.zeros(table.shape, jnp.float32).at[jnp.maximum(asked_rows, 0).reshape(-1)].add(incoming)
     )
+    grad_table, ngram_share, late_part = lax.optimization_barrier(
+        (grad_table, ngram_share, late_part)
+    )
+    late_share = lax.all_gather(late_part, "seq", axis=0, tiled=True)
+    total_ngram = ngram_share[:, :each].reshape(seq_count * each, width)[:ngram_rows].astype(F32)
     wide = share_width
     total_gate, total_up, total_down, total_out = (
         from_columns(total)

time: 814 us -> 816 us (level)
  waiting for transfers between devices: 252 us -> 220 us
  Pallas kernels: 254 us -> 275 us
  local copies, waits for them, and re-layouts: 156 us -> 165 us
    all_gather x1, waiting for transfers between devices: 31 us -> 0.02 us  [shards(): lax.all_gather(up_weight, 'shard', axis=0, tiled=True)]
    all_gather x1, waiting for transfers between devices: 0.02 us -> 18.1 us  [shards(): lax.all_gather(gate_weight, 'shard', axis=0, tiled=True)]
    pallas_call x4, Pallas kernels: 110 us -> 124 us  [exchange(): pl.pallas_call(functools.partial(exchange_kernel, seq_count, shard_count,...]
    all_gather x1, waiting for transfers between devices: 27.5 us -> 16.1 us  [shards(): early_share = lax.all_gather(early_part, 'seq', axis=0, tiled=True)]
    reduce_scatter x2, waiting for transfers between devices: 151 us -> 142 us  [sum_pieces(): lax.psum_scatter(flat, ('seq', 'shard'), scatter_dimension=0, tiled=True)]
    unnamed x129 -> x145, local copies, waits for them, and re-layouts: 72.9 us -> 71.9 us
  transfers between devices with their start and end apart: 11 -> 11, of which waited for: 5 -> 5; matrix products, arithmetic and copies ran while one was open for 22% -> 24% of each run, Pallas kernels for 32% -> 34%
where the time goes in v4:
time: 816 us; the launch traced here: 806 us
  Pallas kernels  275 us (34%)
  waiting for transfers between devices  220 us (27%)
  local copies, waits for them, and re-layouts  165 us (20%)
  other arithmetic  60.3 us (7%)
  matrix products  51.9 us (6%)
  between operations  20.9 us (3%)
  blocking collectives  13.2 us (2%)
    reduce_scatter x2, waiting for transfers between devices, sum_pieces(): lax.psum_scatter(flat, ('seq', 'shard'), scatter_dimension=0, tiled=True)  142 us
    pallas_call x4, Pallas kernels, exchange(): pl.pallas_call(functools.partial(exchange_kernel, seq_count, shard_count,...  124 us
    unnamed x145, local copies, waits for them, and re-layouts  71.9 us
    pallas_call x1, Pallas kernels, halo_reduce(): pl.pallas_call(functools.partial(reduce_kernel, group_count), out_shape=j...  70.7 us
    all_gather x1, waiting for transfers between devices, shards(): lax.all_gather(down_weight, 'shard', axis=0, tiled=True)  40.8 us
    pallas_call x1, Pallas kernels, attention_backward(): pl.pallas_call(backward_kernel, out_shape=(jax.ShapeDtypeStruct((SLOTS +...  33.7 us
    pallas_call x1, Pallas kernels, halo_gather(): pl.pallas_call(functools.partial(gather_kernel, group_count), out_shape=j...  24.6 us
    scatter-add x1, other arithmetic, shards(): jnp.zeros(table.shape, jnp.float32)  23 us
  transfers between devices with their start and end apart: 11, of which 5 were waited for; matrix products, arithmetic and copies ran while one was open for 24% of the time, Pallas kernels for 34%

profile of v4, /device:TPU:0, one launch (start us, length us, event | category | flops | bytes accessed | tf_op | source)
XLA Modules:
  0.0 806.3 jit_solution(12072419418920869861)
XLA Ops:
  21.7 11.2 %ask.1 = s32[32,5,128]{2,1,0:T(8,128)} custom-call(s32[32,5,128]{2,1,0:T(8,128)} %pad_add_fusion.refs_0_), custom_call_target="tpu_custom_call" | custom-call | tf_op jit(solution)/shard_map/ask/pallas_call | solution.py:131
  40.3 13.2 %all_gather.30 = bf16[416,768]{1,0:T(8,128)(2,1)S(1)} all-gather(bf16[208,768]{1,0:T(8,128)(2,1)S(1)} %pad_maximum_fusion.2), channel_id=1, replica_groups=mesh['seq'=16,'shard'=2] {'shard'}, dimensions={0}, use_global_device_ids=true | all-gather | bytes 958464 | tf_op jit(solution)/shard_map/all_gather | solution.py:975
  53.6 14.9 %copy.178 = bf16[25000,192]{1,0:T(8,128)(2,1)} copy(bf16[25000,192]{0,1:T(8,128)(2,1)} %param.21) | data formatting | bytes 19200000 | tf_op args[4]
  68.5 13.1 %gather_fusion = bf16[2048,192]{1,0:T(8,128)(2,1)S(1)} fusion(bf16[25000,192]{1,0:T(8,128)(2,1)} %copy.178, s32[2048]{0:T(1024)S(1)} %broadcast_clamp_fusion), kind=kCustom, calls=%fused_computation | custom fusion | bytes 1581056 | tf_op jit(solution)/shard_map/jit(_take)/gather | solution.py:1009
  83.1 26.0 %answer.1 = bf16[32,64,192]{2,1,0:T(8,128)(2,1)} custom-call(bf16[32,64,192]{2,1,0:T(8,128)(2,1)} %select_select_fusion.refs_0_), custom_call_target="tpu_custom_call" | custom-call | tf_op jit(solution)/shard_map/answer/pallas_call | solution.py:131
  109.1 4.8 gather_fusion.1
  119.9 24.6 %halo_gather.1.x_ref = bf16[13,512,768]{2,1,0:T(8,128)(2,1)} custom-call(bf16[512,768]{1,0:T(8,128)(2,1)} %multiply_convert_fusion.4.own_ref), custom_call_target="tpu_custom_call" | custom-call | tf_op jit(solution)/shard_map/halo_gather/pallas_call | solution.py:299
  160.9 21.9 %attention_forward.1 = (f32[512,1024]{1,0:T(8,128)}, f32[512,128]{1,0:T(8,128)}, bf16[9,4,512,256]{3,2,1,0:T(8,128)(2,1)}) custom-call(s32[9]{0:T(128)} %compare_select_fusion.5.slot_ref, s32[9]{0:T(128)} %compare_convert_fusion.valid_ref, bf16[512,768]{1,0:T(8,128)(2,1)} %multiply_convert_fusion.4.own_ref, bf16[13,512,768]{2,1,0:T(8,128)(2,1)} %halo_gather.1.x_ref, ...), custom_call_target="tpu_custom_call" | custom-call | flops 70000001024 | bytes 10000000 | tf_op jit(solution)/shard_map/attention_forward/pallas_call | solution.py:599
  188.0 5.8 fusion.45
  193.7 18.1 %all-gather.18.cloned.1.call-done = bf16[768,2048]{1,0:T(8,128)(2,1)} async-done(((bf16[384,2048]{1,0:T(8,128)(2,1)}), bf16[768,2048]{1,0:T(8,128)(2,1)}) %all-gather.18.cloned.1.call-update) | async-done | bytes 3145744 | tf_op jit(solution)/shard_map/all_gather | solution.py:956
  211.8 5.7 fusion.44
  217.5 40.8 %all-gather.22.cloned.1.call-done = bf16[2048,768]{1,0:T(8,128)(2,1)} async-done(((bf16[1024,768]{1,0:T(8,128)(2,1)}), bf16[2048,768]{1,0:T(8,128)(2,1)}) %all-gather.22.cloned.1.call-update) | async-done | bytes 3145744 | tf_op jit(solution)/shard_map/all_gather | solution.py:958
  258.3 6.6 multiply_convert_fusion
  309.2 11.7 %pad_maximum_fusion = bf16[16,2,648,256]{3,2,1,0:T(8,128)(2,1)} fusion(bf16[16,2,72,256]{3,2,1,0:T(8,128)(2,1)S(1)} %bitcast.255, bf16[16,2,192,256]{3,2,1,0:T(8,128)(2,1)S(1)} %bitcast.226, bf16[16,2,192,256]{3,2,1,0:T(8,128)(2,1)} %bitcast.227, bf16[16,2,192,256]{3,2,1,0:T(8,128)(2,1)} %bitcast.228), kind=kLoop, calls=%fused_computation.8 | loop fusion | flops 42467328 | bytes 21233664 | tf_op jit(solution)/shard_map/concatenate | solution.py:1099
  325.4 33.7 %attention_backward.1 = (bf16[13,512,768]{2,1,0:T(8,128)(2,1)}, bf16[768,512]{1,0:T(8,128)(2,1)}, bf16[4,768,256]{2,1,0:T(8,128)(2,1)}, bf16[4,768,256]{2,1,0:T(8,128)(2,1)}) custom-call(s32[9]{0:T(128)} %compare_select_fusion.5.slot_ref, s32[9]{0:T(128)} %compare_convert_fusion.valid_ref, bf16[512,768]{1,0:T(8,128)(2,1)} %multiply_convert_fusion.4.own_ref, ...), custom_call_target="tpu_custom_call" | custom-call | flops 120000004096 | bytes 20000000 | tf_op jit(solution)/shard_map/attention_backward/pallas_call | solution.py:784
  368.2 132.7 %reduce-scatter.3.cloned.1.call-done = bf16[648,256]{1,0:T(8,128)(2,1)} async-done(((bf16[20736,256]{1,0:T(8,128)(2,1)}), bf16[648,256]{1,0:T(8,128)(2,1)}) %reduce-scatter.3.cloned.1.call-update) | async-done | bytes 331792 | tf_op jit(solution)/shard_map/reduce_scatter | solution.py:911
  501.0 70.7 %halo_reduce.1 = f32[512,768]{1,0:T(8,128)} custom-call(bf16[13,512,768]{2,1,0:T(8,128)(2,1)} %get-tuple-element.47.part_ref), custom_call_target="tpu_custom_call" | custom-call | tf_op jit(solution)/shard_map/halo_reduce/pallas_call | solution.py:458
  579.3 6.1 scatter_custom_fusion.1
  585.4 16.1 %all-gather.24.cloned.1.call-done = bf16[10368,256]{1,0:T(8,128)(2,1)} async-done(((bf16[648,256]{1,0:T(8,128)(2,1)}), bf16[10368,256]{1,0:T(8,128)(2,1)}) %all-gather.24.cloned.1.call-update) | async-done | bytes 5308432 | tf_op jit(solution)/shard_map/all_gather | solution.py:1133
  607.9 55.7 %give_back.1 = (bf16[32,64,192]{2,1,0:T(8,128)(2,1)}, bf16[32,16,768]{2,1,0:T(8,128)(2,1)}, f32[32,8,128]{2,1,0:T(8,128)}) custom-call(bf16[32,64,192]{2,1,0:T(8,128)(2,1)} %bitcast.257, bf16[32,16,768]{2,1,0:T(8,128)(2,1)} %bitcast.259, f32[8,128]{1,0:T(8,128)} %broadcast_in_dim.143.refs_2_), custom_call_target="tpu_custom_call" | custom-call | tf_op jit(solution)/shard_map/give_back/pallas_call | solution.py:131
  665.5 31.1 %spread.1 = bf16[16,16,768]{2,1,0:T(8,128)(2,1)} custom-call(bf16[16,768]{1,0:T(8,128)(2,1)} %convert_element_type.243.refs_0_), custom_call_target="tpu_custom_call" | custom-call | tf_op jit(solution)/shard_map/spread/pallas_call | solution.py:131
  697.1 23.0 %scatter_custom_fusion.2 = f32[25000,192]{1,0:T(8,128)} fusion(s32[2048]{0:T(1024)} %copy-done.42, f32[]{:T(128)} %constant.130.clone.1, bf16[2048,192]{1,0:T(8,128)(2,1)S(1)} %bitcast.256), kind=kCustom, calls=%fused_computation.6 | custom fusion | flops 786432 | bytes 19986944 | tf_op jit(solution)/shard_map/scatter-add | solution.py:1190
  720.1 9.7 %reduce-scatter.5.cloned.1.call-done = bf16[264,256]{1,0:T(8,128)(2,1)} async-done(((bf16[8448,256]{1,0:T(8,128)(2,1)}), bf16[264,256]{1,0:T(8,128)(2,1)}) %reduce-scatter.5.cloned.1.call-update) | async-done | bytes 135184 | tf_op jit(solution)/shard_map/reduce_scatter | solution.py:911
  760.9 23.3 %copy.218 = f32[25000,192]{0,1:T(8,128)} copy(f32[25000,192]{1,0:T(8,128)} %scatter_custom_fusion.2) | data formatting | bytes 38400000
  (327 shorter events, 165.1 us)
Async XLA Ops:
  7.2 140.7 %all-gather.12.cloned.1.call-start = ((), (), s32[]{:S(2)}) async-start(), calls=%async_computation.3 | async-start | bytes 1769472 | tf_op jit(solution)/shard_map/all_gather | solution.py:953
  9.5 143.7 %all-gather.10.cloned.1.call-start = ((), (), s32[]{:S(2)}) async-start(), calls=%async_computation.2 | async-start | bytes 1769472 | tf_op jit(solution)/shard_map/all_gather | solution.py:952
  10.6 147.8 %all-gather.14.cloned.1.call-start = ((), (), s32[]{:S(2)}) async-start(), calls=%async_computation.4 | async-start | bytes 1769472 | tf_op jit(solution)/shard_map/all_gather | solution.py:954
  11.8 171.1 %all-gather.16.cloned.1.call-start = ((), (), s32[]{:S(2)}) async-start(), calls=%async_computation.5 | async-start | bytes 1769472 | tf_op jit(solution)/shard_map/all_gather | solution.py:955
  12.3 175.6 %all-gather.20.cloned.1.call-start = ((), (), s32[]{:S(2)}) async-start(), calls=%async_computation.7 | async-start | bytes 4718592 | tf_op jit(solution)/shard_map/all_gather | solution.py:957
  12.9 198.8 %all-gather.18.cloned.1.call-start = ((), (), s32[]{:S(2)}) async-start(), calls=%async_computation.6 | async-start | bytes 4718592 | tf_op jit(solution)/shard_map/all_gather | solution.py:956
  13.5 244.7 %all-gather.22.cloned.1.call-start = ((), (), s32[]{:S(2)}) async-start(), calls=%async_computation.8 | async-start | bytes 4718592 | tf_op jit(solution)/shard_map/all_gather | solution.py:958
  14.3 486.6 %reduce-scatter.3.cloned.1.call-start = ((), (), s32[]{:S(2)}) async-start(), calls=%async_computation.9 | async-start | bytes 10948608 | tf_op jit(solution)/shard_map/reduce_scatter | solution.py:911
  53.5 62.9 %copy-start.22 = (bf16[416,768]{1,0:T(8,128)(2,1)}, bf16[416,768]{1,0:T(8,128)(2,1)S(1)}, u32[]{:S(2)}) copy-start(bf16[416,768]{1,0:T(8,128)(2,1)S(1)} %all_gather.30) | copy-start | bytes 1916932
  53.6 130.8 %copy-start.32 = (f32[768]{0:T(1024)}, f32[768]{0:T(1024)S(1)}, u32[]{:S(2)}) copy-start(f32[768]{0:T(1024)S(1)} %mul.352) | copy-start | bytes 9220
  53.6 65.1 %copy-start.40 = (f32[768]{0:T(1024)}, f32[768]{0:T(1024)S(1)}, u32[]{:S(2)}) copy-start(f32[768]{0:T(1024)S(1)} %mul.359) | copy-start | bytes 9220
  118.3 66.1 %copy-start = (f32[512,768]{1,0:T(8,128)}, f32[512,768]{1,0:T(8,128)S(1)}, u32[]{:S(2)}) copy-start(f32[512,768]{1,0:T(8,128)S(1)} %get-tuple-element.171) | copy-start | bytes 4718596
  118.3 66.1 %copy-start.35 = (f32[512]{0:T(512)}, f32[512]{0:T(512)S(1)}, u32[]{:S(2)}) copy-start(f32[512]{0:T(512)S(1)} %add_rsqrt_fusion.2) | copy-start | bytes 6148
  193.7 64.5 %copy-start.61 = (bf16[1,512,768]{2,1,0:T(8,128)(2,1)S(1)}, bf16[1,512,768]{2,1,0:T(8,128)(2,1)}, u32[]{:S(2)}) copy-start(bf16[1,512,768]{2,1,0:T(8,128)(2,1)} %param.33) | copy-start | bytes 2359300
  320.9 280.6 %all-gather.24.cloned.1.call-start = ((), (), s32[]{:S(2)}) async-start(), calls=%async_computation.10 | async-start | bytes 5640192 | tf_op jit(solution)/shard_map/all_gather | solution.py:1133
  365.9 135.0 %copy-start.23 = (bf16[416,768]{1,0:T(8,128)(2,1)S(1)}, bf16[416,768]{1,0:T(8,128)(2,1)}, u32[]{:S(2)}) copy-start(bf16[416,768]{1,0:T(8,128)(2,1)} %copy-done.22) | copy-start | bytes 1916932
  500.9 228.9 %reduce-scatter.5.cloned.1.call-start = ((), (), s32[]{:S(2)}) async-start(), calls=%async_computation.11 | async-start | bytes 4460544 | tf_op jit(solution)/shard_map/reduce_scatter | solution.py:911
  501.0 70.7 %copy-start.1 = (f32[512,768]{1,0:T(8,128)S(1)}, f32[512,768]{1,0:T(8,128)}, u32[]{:S(2)}) copy-start(f32[512,768]{1,0:T(8,128)} %copy-done) | copy-start | bytes 4718596
  501.0 70.7 %copy-start.33 = (f32[768]{0:T(1024)S(1)}, f32[768]{0:T(1024)}, u32[]{:S(2)}) copy-start(f32[768]{0:T(1024)} %copy-done.32) | copy-start | bytes 9220
  501.0 70.7 %copy-start.36 = (f32[512]{0:T(512)S(1)}, f32[512]{0:T(512)}, u32[]{:S(2)}) copy-start(f32[512]{0:T(512)} %copy-done.35) | copy-start | bytes 6148
  501.0 70.7 %copy-start.41 = (f32[768]{0:T(1024)S(1)}, f32[768]{0:T(1024)}, u32[]{:S(2)}) copy-start(f32[768]{0:T(1024)} %copy-done.40) | copy-start | bytes 9220
  501.0 70.7 %copy-start.44 = (f32[512]{0:T(512)S(1)}, f32[512]{0:T(512)}, u32[]{:S(2)}) copy-start(f32[512]{0:T(512)} %copy-done.43) | copy-start | bytes 6148
  601.6 183.6 %all-gather.26.cloned.1.call-start = ((), (), s32[]{:S(2)}) async-start(), calls=%async_computation.12 | async-start | bytes 2297856 | tf_op jit(solution)/shard_map/all_gather | solution.py:1195
  607.9 88.7 %copy-start.38 = (pred[32,64]{1,0:T(8,128)(4,1)S(1)}, pred[32,64]{1,0:T(8,128)(4,1)}, u32[]{:S(2)}) copy-start(pred[32,64]{1,0:T(8,128)(4,1)} %copy-done.37) | copy-start | bytes 6148
  (50 other events, 397.1 us)
Sparse Core Ops, SparseCore 0:
  10.1 26.3 all-gather.11
  38.6 24.8 all-gather.9
  65.7 23.5 all-gather.13
  90.7 25.5 all-gather.15
  117.7 47.6 all-gather.19
  166.8 44.8 all-gather.17
  213.3 44.8 all-gather.21
  321.0 179.7 reduce-scatter.2
  503.0 98.4 all-gather.23
  606.9 122.8 reduce-scatter.4
  732.0 40.7 all-gather.25
